TPU v7x, 32 devices: a whole 2x2x4 slice. The times are simulated.
32 devices in a mesh: row: 8 (over z, y), col: 4 (over x, core).
Axes of the slice: x: 2, y: 2, z: 4, core: 2. Of those that a mesh axis runs over, the one named last changes fastest.
Arguments:
- residual: float32 [512, 512, 256], P('row', 'col'), may hold values from -6 to 6
- adjoint: float32 [512, 512, 256], P('row', 'col'), may hold values from -6 to 6
- coefficient: bfloat16 [512, 512, 256], P('row', 'col'), may hold values from 0.25 to 4
- basis_x: float32 [512, 512], replicated, may hold values from -0.25 to 0.25
- basis_y: float32 [512, 512], replicated, may hold values from -0.25 to 0.25
- basis_z: float32 [256, 256], replicated, may hold values from -0.375 to 0.375
- eigen_x: float32 [512], replicated, may hold values from 0.02 to 2
- eigen_y: float32 [512], replicated, may hold values from 0.02 to 2
- eigen_z: float32 [256], replicated, may hold values from 0.02 to 2
Outputs:
- adjoint_next: float32 [512, 512, 256], P('row', 'col')
- residual_next: float32 [512, 512, 256], P('row', 'col')
All inputs are finite; a program needn't handle non-finite values.
Results may differ from a plain program's by a relative error of at most 0.0003.
Values sent between devices are 32-bit elements; how exact they have to be, the bound alone decides.
No kernel may reach another device: no remote copies, remote signals or barrier semaphores. Data moves between devices by JAX's collectives and lax.ppermute only.
A program may use at most 192 MiB of HBM per device.

v0:
```python
import jax
import jax.numpy as jnp
from jax import lax
from jax.sharding import PartitionSpec as P

MASS_TAPS = (
    1.0 / 5040,
    120.0 / 5040,
    1191.0 / 5040,
    2416.0 / 5040,
    1191.0 / 5040,
    120.0 / 5040,
    1.0 / 5040,
)
STIFF_TAPS = (-1.0 / 120, -0.2, -0.125, 2.0 / 3.0, -0.125, -0.2, -1.0 / 120)
HIGHEST = lax.Precision.HIGHEST


def with_halo(shard, sides, width):
    for axis, dim in sides:
        peers, length = (lax.axis_size(axis), shard.shape[dim])
        up = [(i, (i + 1) % peers) for i in range(peers - 1)]
        down = [(j, i) for i, j in up]
        last = lax.slice_in_dim(shard, length - width, length, axis=dim)
        leading = lax.slice_in_dim(shard, 0, width, axis=dim)
        before = lax.ppermute(last, axis, up)
        after = lax.ppermute(leading, axis, down)
        shard = jnp.concatenate([before, shard, after], axis=dim)
    return shard


def taps_along(padded, coeffs, axis_dim, length):
    running = coeffs[0] * lax.slice_in_dim(padded, 0, length, axis=axis_dim)
    for offset in range(1, 7):
        running = running + coeffs[offset] * lax.slice_in_dim(
            padded, offset, offset + length, axis=axis_dim
        )
    return running


def stiffness(padded, length_x, length_y, length_z):
    mass_x = taps_along(padded, MASS_TAPS, 0, length_x)
    stiff_x = taps_along(padded, STIFF_TAPS, 0, length_x)
    mass_xy = taps_along(mass_x, MASS_TAPS, 1, length_y)
    stiff_y = taps_along(mass_x, STIFF_TAPS, 1, length_y)
    stiff_xm = taps_along(stiff_x, MASS_TAPS, 1, length_y)
    return taps_along(stiff_y + stiff_xm, MASS_TAPS, 2, length_z) + taps_along(
        mass_xy, STIFF_TAPS, 2, length_z
    )


def shards(residual, adjoint, coefficient, basis_x, basis_y, basis_z, eigen_x, eigen_y, eigen_z):
    rows_local, cols_local, depth = residual.shape
    row_count = lax.axis_size("row")
    col_count = lax.axis_size("col")
    width_x = rows_local * row_count
    width_y = cols_local * col_count
    row_index = lax.axis_index("row")
    col_index = lax.axis_index("col")
    depth_part = depth // row_count
    xpart_col = width_x // col_count
    basis_zr = basis_z.reshape(depth, row_count, depth_part)
    basis_x4 = basis_x.reshape(row_count, rows_local, col_count, xpart_col)
    basis_y3 = basis_y.reshape(col_count, cols_local, width_y)
    outgoing = jnp.einsum("xyz,zjc->jcxy", residual, basis_zr, precision=HIGHEST)
    middle = jnp.einsum(
        "icxy,ixnq->ncqy",
        lax.all_to_all(outgoing, "row", split_axis=0, concat_axis=0, tiled=True),
        basis_x4,
        precision=HIGHEST,
    )
    spectrum = jnp.einsum(
        "jcqy,jyk->cqk",
        lax.all_to_all(middle, "col", split_axis=0, concat_axis=0, tiled=True),
        basis_y3,
        precision=HIGHEST,
    )
    zslice = lax.dynamic_slice_in_dim(eigen_z, row_index * depth_part, depth_part)
    xslice = lax.dynamic_slice_in_dim(eigen_x, col_index * xpart_col, xpart_col)
    denominator = zslice[:, None, None] + xslice[None, :, None] + eigen_y[None, None, :]
    scaled = spectrum / denominator
    returning = jnp.einsum("cqk,jyk->jcqy", scaled, basis_y3, precision=HIGHEST)
    middle_back = jnp.einsum(
        "ncqy,ixnq->icxy",
        lax.all_to_all(returning, "col", split_axis=0, concat_axis=0, tiled=True),
        basis_x4,
        precision=HIGHEST,
    )
    correction = jnp.einsum(
        "jcxy,zjc->xyz",
        lax.all_to_all(middle_back, "row", split_axis=0, concat_axis=0, tiled=True),
        basis_zr,
        precision=HIGHEST,
    )
    weighted = coefficient.astype(jnp.float32) * correction
    extended = with_halo(weighted, (("row", 0), ("col", 1)), 3)
    extended = jnp.pad(extended, ((0, 0), (0, 0), (3, 3)))
    image = stiffness(extended, rows_local, cols_local, depth)
    return (adjoint + correction, residual - image)


def solution(mesh):
    return jax.shard_map(
        shards,
        mesh=mesh,
        in_specs=(
            P("row", "col", None),
            P("row", "col", None),
            P("row", "col", None),
            P(),
            P(),
            P(),
            P(),
            P(),
            P(),
        ),
        out_specs=(P("row", "col", None), P("row", "col", None)),
        check_vma=False,
    )
```

profile of v0, /device:TPU:9, one launch (start us, length us, event | category | flops | bytes accessed | tf_op | source)
XLA Modules:
  0.0 972.2 jit_solution(8155281669922954859)
XLA Ops:
  1.8 11.5 %fusion.28 = f32[8,32,64,128]{3,1,2,0:T(8,128)} fusion(f32[256,8,32,1]{0,2,3,1:T(8,128)S(1)} %bitcast.61, f32[64,128,256]{2,1,0:T(8,128)} %param.9), kind=kOutput, calls=%fused_computation.61 | convolution fusion | flops 6442450944 | bytes 17039360 | tf_op jit(solution)/shard_map/xyz,zjc->jcxy/dot_general | solution.py:65
  13.3 5.7 all-to-all-start
  20.6 179.8 %all-to-all-done = f32[8,32,64,128]{3,1,2,0:T(8,128)} async-done(((f32[8,32,64,128]{3,1,2,0:T(8,128)}), f32[8,32,64,128]{3,1,2,0:T(8,128)}, u32[]{:S(2)}, u32[]{:S(2)}) %all-to-all-start) | async-done | bytes 8388640 | tf_op jit(solution)/shard_map/all_to_all | solution.py:68
  200.4 17.3 %fusion.33 = f32[4,32,128,128]{2,3,0,1:T(8,128)S(1)} fusion(f32[8,32,64,128,1]{3,1,2,0,4:T(8,128)} %bitcast.4, f32[8,64,4,128]{3,2,1,0:T(4,128)S(1)} %reshape.47), kind=kOutput, calls=%fused_computation.66 | convolution fusion | flops 12884901888 | bytes 17825792 | tf_op jit(solution)/shard_map/icxy,ixnq->ncqy/dot_general | solution.py:66
  217.7 4.0 copy.16
  221.7 6.4 all-to-all-start.1
  229.1 91.2 %all-to-all-done.1 = f32[4,32,128,128]{2,3,1,0:T(8,128)} async-done(((f32[4,32,128,128]{2,3,1,0:T(8,128)}), f32[4,32,128,128]{2,3,1,0:T(8,128)}, u32[]{:S(2)}, u32[]{:S(2)}) %all-to-all-start.1) | async-done | bytes 8388640 | tf_op jit(solution)/shard_map/all_to_all | solution.py:74
  320.3 15.5 %fusion.47 = f32[32,128,512,1]{2,1,0,3:T(8,128)S(1)} fusion(f32[4,32,128,128]{2,3,1,0:T(8,128)} %all-to-all-done.1, f32[4,128,512,1]{2,1,3,0:T(8,128)S(1)} %bitcast.60), kind=kOutput, calls=%fused_computation.78 | convolution fusion | flops 12884901888 | bytes 17825792 | tf_op jit(solution)/shard_map/jcqy,jyk->cqk/dot_general | solution.py:72
  335.8 14.6 %fusion.39 = f32[4,32,128,128]{3,2,0,1:T(8,128)S(1)} fusion(f32[4,128,512,1]{2,1,0,3:T(8,128)S(1)} %bitcast.59, f32[32,128,512,1]{2,1,0,3:T(8,128)S(1)} %fusion.47, f32[512]{0:T(512)S(1)} %copy-done.3, f32[32,128]{1,0:T(8,128)S(1)} %broadcast_add_fusion), kind=kOutput, calls=%fused_computation.68 | convolution fusion | flops 12889096192 | bytes 17844224 | tf_op jit(solution)/shard_map/cqk,jyk->jcqy/dot_general | solution.py:82
  351.6 95.8 %all_to_all.20 = f32[4,32,128,128]{3,2,1,0:T(8,128)S(1)} all-to-all(f32[4,32,128,128]{3,2,1,0:T(8,128)S(1)} %copy.18), channel_id=1, replica_groups=mesh['row'=8,'col'=4] {'col'}, dimensions={0} | all-to-all | bytes 16777216 | tf_op jit(solution)/shard_map/all_to_all | solution.py:85
  447.3 16.1 %fusion.36 = f32[8,32,64,128]{3,2,0,1:T(8,128)S(1)} fusion(f32[8,64,4,128]{3,2,1,0:T(4,128)S(1)} %reshape.47, f32[4,32,128,128]{3,2,1,0:T(8,128)S(1)} %all_to_all.20), kind=kOutput, calls=%fused_computation.67 | convolution fusion | flops 12884901888 | bytes 17825792 | tf_op jit(solution)/shard_map/ncqy,ixnq->icxy/dot_general | solution.py:83
  463.4 4.8 copy.21
  468.2 187.1 %all_to_all.21 = f32[8,32,64,128]{3,1,2,0:T(8,128)} all-to-all(f32[8,32,64,128]{3,1,2,0:T(8,128)S(1)} %copy.21), channel_id=1, replica_groups=mesh['row'=8,'col'=4] {'row'}, dimensions={0} | all-to-all | bytes 16777216 | tf_op jit(solution)/shard_map/all_to_all | solution.py:91
  655.2 19.0 %bitcast_multiply_fusion = (f32[64,128,256]{2,1,0:T(8,128)S(1)}, f32[64,128,256]{2,1,0:T(8,128)}) fusion(bf16[64,128,256]{2,1,0:T(8,128)(2,1)S(1)} %copy-done.2, f32[64,128,256]{2,1,0:T(8,128)} %param.10, f32[8,32,64,128]{3,1,2,0:T(8,128)} %all_to_all.21, f32[256,8,32,1]{0,2,3,1:T(8,128)S(1)} %bitcast.62), kind=kOutput, calls=%fused_computation.54 | convolution fusion | flops 6448742400 | bytes 38010880 | tf_op jit(solution)/shard_map/jcxy,zjc->xyz/dot_general | solution.py:89
  676.2 4.3 collective-permute-start.1
  680.5 10.2 %collective-permute-done = f32[3,128,256]{2,1,0:T(8,128)S(1)} collective-permute-done((f32[3,128,256]{2,1,0:T(8,128)S(1)}, f32[3,128,256]{2,1,0:T(8,128)S(1)}, u32[]{:S(2)}, u32[]{:S(2)}) %collective-permute-start) | collective-permute-done | bytes 393248 | tf_op jit(solution)/shard_map/ppermute | solution.py:26
  690.8 5.8 collective-permute-done.1
  696.7 3.0 collective-permute-start.2
  703.3 4.4 collective-permute-done.3
  707.7 15.0 %select_maximum_fusion = f32[70,134,262]{2,1,0:T(8,128)} fusion(f32[70,3,256]{2,1,0:T(4,128)S(1)} %collective-permute-done.3, f32[70,3,256]{2,1,0:T(4,128)S(1)} %collective-permute-done.2, f32[3,128,256]{2,1,0:T(8,128)S(1)} %collective-permute-done.1, f32[64,128,256]{2,1,0:T(8,128)S(1)} %get-tuple-element.8, f32[3,128,256]{2,1,0:T(8,128)S(1)} %collective-permute-done), kind=kLoop, calls=%fused_computation.2 | loop fusion | flops 29490720 | bytes 19435360 | tf_op jit(solution)/shard_map/concatenate | solution.py:28
  722.7 40.7 %multiply_add_fusion = (f32[64,134,262]{2,1,0:T(8,128)}, f32[64,134,262]{2,1,0:T(8,128)}) fusion(f32[70,134,262]{2,1,0:T(8,128)} %select_maximum_fusion), kind=kLoop, calls=%fused_computation.7 | loop fusion | flops 58419712 | bytes 80888832 | tf_op jit(solution)/shard_map/add | solution.py:35
  763.4 40.1 %multiply_add_fusion.2 = f32[64,128,262]{2,1,0:T(8,128)} fusion(f32[64,134,262]{2,1,0:T(8,128)} %get-tuple-element.3), kind=kLoop, calls=%fused_computation.23 | loop fusion | flops 27901952 | bytes 68681728 | tf_op jit(solution)/shard_map/add | solution.py:35
  803.5 84.3 %fusion.2 = f32[64,128,262]{2,1,0:T(8,128)} fusion(f32[64,134,262]{2,1,0:T(8,128)} %get-tuple-element.2, f32[64,134,262]{2,1,0:T(8,128)} %get-tuple-element.3), kind=kLoop, calls=%fused_computation.11 | loop fusion | flops 57950208 | bytes 128778240 | tf_op jit(solution)/shard_map/add | solution.py:47
  887.8 83.9 %fusion.10 = f32[64,128,256]{2,1,0:T(8,128)} fusion(f32[64,128,256]{2,1,0:T(8,128)} %param.9, f32[64,128,262]{2,1,0:T(8,128)} %multiply_add_fusion.2, f32[64,128,262]{2,1,0:T(8,128)} %fusion.2), kind=kLoop, calls=%fused_computation.27 | loop fusion | flops 58720256 | bytes 134217728 | tf_op jit(solution)/shard_map/sub | solution.py:99
  (21 shorter events, 10.4 us)
Async XLA Ops:
  0.6 319.7 %copy-start = (f32[512,512]{1,0:T(8,128)S(1)}, f32[512,512]{1,0:T(8,128)}, u32[]{:S(2)}) copy-start(f32[512,512]{1,0:T(8,128)} %param.13) | copy-start | bytes 3145732
  13.3 187.1 %all-to-all-start = ((f32[8,32,64,128]{3,1,2,0:T(8,128)}), f32[8,32,64,128]{3,1,2,0:T(8,128)}, u32[]{:S(2)}, u32[]{:S(2)}) async-start(f32[8,32,64,128]{3,1,2,0:T(8,128)} %fusion.28), calls=%async_computation | async-start | bytes 16777216 | tf_op jit(solution)/shard_map/all_to_all | solution.py:68
  221.7 6.5 copy-start.4
  221.7 98.6 %all-to-all-start.1 = ((f32[4,32,128,128]{2,3,1,0:T(8,128)}), f32[4,32,128,128]{2,3,1,0:T(8,128)}, u32[]{:S(2)}, u32[]{:S(2)}) async-start(f32[4,32,128,128]{2,3,1,0:T(8,128)} %copy.16), calls=%async_computation.1 | async-start | bytes 16777216 | tf_op jit(solution)/shard_map/all_to_all | solution.py:74
  228.1 107.7 %copy-start.3 = (f32[512]{0:T(512)S(1)}, f32[512]{0:T(512)}, u32[]{:S(2)}) copy-start(f32[512]{0:T(512)} %param.16) | copy-start | bytes 6148
  468.2 187.1 %copy-start.2 = (bf16[64,128,256]{2,1,0:T(8,128)(2,1)S(1)}, bf16[64,128,256]{2,1,0:T(8,128)(2,1)}, u32[]{:S(2)}) copy-start(bf16[64,128,256]{2,1,0:T(8,128)(2,1)} %param.11) | copy-start | bytes 12582916
  674.3 16.4 %collective-permute-start = (f32[3,128,256]{2,1,0:T(8,128)S(1)}, f32[3,128,256]{2,1,0:T(8,128)S(1)}, u32[]{:S(2)}, u32[]{:S(2)}) collective-permute-start(f32[3,128,256]{2,1,0:T(8,128)S(1)} %get-tuple-element.6), channel_id=1, source_target_pairs={{0,4},{4,8},{8,12},{12,16},{16,20},{20,24},{24,28},{1,5},{5,9},{9,... | collective-permute-start | bytes 1179656 | tf_op jit(solution)/shard_map/ppermute | solution.py:26
  676.2 20.3 %collective-permute-start.1 = (f32[3,128,256]{2,1,0:T(8,128)S(1)}, f32[3,128,256]{2,1,0:T(8,128)S(1)}, u32[]{:S(2)}, u32[]{:S(2)}) collective-permute-start(f32[3,128,256]{2,1,0:T(8,128)S(1)} %get-tuple-element.7), channel_id=1, source_target_pairs={{4,0},{8,4},{12,8},{16,12},{20,16},{24,20},{28,24},{5,1},{9,5},{13... | collective-permute-start | bytes 1179656 | tf_op jit(solution)/shard_map/ppermute | solution.py:27
  696.7 6.6 collective-permute-start.2
  699.7 8.0 collective-permute-start.3
  887.8 83.9 %copy-start.1 = (f32[512,512]{1,0:T(8,128)S(1)}, f32[512,512]{1,0:T(8,128)}, u32[]{:S(2)}) copy-start(f32[512,512]{1,0:T(8,128)} %param.13) | copy-start | bytes 3145732
where the time goes:
time: 979 us; the launch traced here: 972 us
  waiting for transfers between devices  293 us (30%)
  blocking collectives  283 us (29%)
  other arithmetic  264 us (27%)
  matrix products  94 us (10%)
  starting transfers between devices  23.3 us (2%)
  local copies, waits for them, and re-layouts  13.5 us (1%)
    all_to_all x1, blocking collectives, shards(): lax.all_to_all(middle_back, 'row', split_axis=0, concat_axis=0, tiled=True)  187 us
    all_to_all x1, waiting for transfers between devices, shards(): lax.all_to_all(outgoing, 'row', split_axis=0, concat_axis=0, tiled=True)  180 us
    all_to_all x1, blocking collectives, shards(): lax.all_to_all(returning, 'col', split_axis=0, concat_axis=0, tiled=True)  95.8 us
    all_to_all x1, waiting for transfers between devices, shards(): lax.all_to_all(middle, 'col', split_axis=0, concat_axis=0, tiled=True)  91.2 us
    add x1, other arithmetic, stiffness(): stiff_y + stiff_xm  84.3 us
    sub x1, other arithmetic, shards(): return (adjoint + correction, residual - image)  83.9 us
    add x2, other arithmetic, taps_along(): running + coeffs[offset] * lax.slice_in_dim(padded, offset, offset + leng...  80.8 us
  transfers between devices with their start and end apart: 6, of which 6 were waited for; matrix products, arithmetic and copies ran while one was open for 0% of the time, Pallas kernels for 0%

commit v1 on v0

v1 whole, which is shorter than its diff:
```python
import jax
import jax.numpy as jnp
import numpy as np
from jax import lax
from jax.experimental import pallas as pl
from jax.experimental.pallas import tpu as pltpu
from jax.sharding import PartitionSpec as P


MASS = tuple(t / 5040 for t in (1.0, 120.0, 1191.0, 2416.0, 1191.0, 120.0, 1.0))
STIFF = (-1.0 / 120, -0.2, -0.125, 2.0 / 3.0, -0.125, -0.2, -1.0 / 120)
F32, BF16 = jnp.float32, jnp.bfloat16
NN = (((1,), (0,)), ((), ()))
NT = (((1,), (1,)), ((), ()))
TN = (((0,), (0,)), ((), ()))


def params(n, limit=56 << 20):
    return pltpu.CompilerParams(
        dimension_semantics=("arbitrary",) * n, vmem_limit_bytes=limit
    )


def cost(flops, nbytes):
    return pl.CostEstimate(flops=flops, bytes_accessed=nbytes, transcendentals=0)


def split(v):
    high = v.astype(BF16)
    return high, (v - high.astype(F32)).astype(BF16)


def split_outside(v):
    high = lax.reduce_precision(v, 8, 7)
    return high.astype(BF16), (v - high).astype(BF16)


def dot3(a, b, dims):
    def dot(p, q):
        return lax.dot_general(p, q, dims, preferred_element_type=F32)

    return dot(a[0], b[0]) + (dot(a[0], b[1]) + dot(a[1], b[0]))


def join(parts, axis):
    return parts[0] if len(parts) == 1 else jnp.concatenate(parts, axis=axis)


def sum_dots(parts, mat, dims_width):
    if dims_width % 128 == 0:
        a = (join([p[0] for p in parts], 1), join([p[1] for p in parts], 1))
        return dot3(a, (mat[0][...], mat[1][...]), NN)
    total = None
    for e, p in enumerate(parts):
        rows = pl.ds(e * dims_width, dims_width)
        term = dot3(p, (mat[0][rows, :], mat[1][rows, :]), NN)
        total = term if total is None else total + term
    return total


def whole(shape):
    return pl.BlockSpec(shape, lambda *_: (0,) * len(shape))


def forward_z(residual, basis_zt, where, chunks, peers, part):
    nx, ny, nz = residual.shape
    xb = 8
    group = peers * part

    def kernel(where_ref, r_ref, b_ref, *outs):
        me = where_ref[0]
        rows = [
            b_ref[pl.ds(pl.multiple_of(k * group + (me ^ d) * part, part), part), :]
            for k in chunks
            for d in range(peers)
        ]
        basis = split(join(rows, 0))
        for x in range(xb):
            t = dot3(basis, split(r_ref[x]), NT)
            for n, out in enumerate(outs):
                out[x] = t[n * part : (n + 1) * part, :]

    count = len(chunks) * peers
    outs = pl.pallas_call(
        kernel,
        grid_spec=pltpu.PrefetchScalarGridSpec(
            num_scalar_prefetch=1,
            grid=(nx // xb,),
            in_specs=[
                pl.BlockSpec((xb, ny, nz), lambda i, w: (i, 0, 0)),
                pl.BlockSpec(basis_zt.shape, lambda i, w: (0, 0)),
            ],
            out_specs=[pl.BlockSpec((xb, part, ny), lambda i, w: (i, 0, 0))] * count,
        ),
        out_shape=[jax.ShapeDtypeStruct((nx, part, ny), F32)] * count,
        compiler_params=params(1),
        cost_estimate=cost(6 * nx * ny * nz * len(chunks) * group, nx * ny * nz * 4),
        name="forward_z",
    )(where, residual, basis_zt)
    return [outs[n * peers : (n + 1) * peers] for n in range(len(chunks))]


def forward_x(pieces, bxt, peers, after):
    nx, part, ny = pieces[0].shape
    full = nx * len(pieces)
    wide = full // peers

    def kernel(_, bh, bl, *refs):
        ins, outs = refs[: len(pieces)], refs[len(pieces) :]

        def step(c):
            v = split(join([r[:, c, :] for r in ins], 0))
            t = dot3((bh[...], bl[...]), v, NN)
            for e, out in enumerate(outs):
                out[c] = t[e * wide : (e + 1) * wide, :]
            return 0

        for c in range(part):
            step(c)

    return pl.pallas_call(
        kernel,
        out_shape=[jax.ShapeDtypeStruct((part, wide, ny), F32)] * peers,
        in_specs=[pl.BlockSpec(memory_space=pl.ANY)]
        + [pl.BlockSpec(memory_space=pltpu.VMEM)] * (2 + len(pieces)),
        out_specs=[pl.BlockSpec(memory_space=pltpu.VMEM)] * peers,
        compiler_params=params(0),
        cost_estimate=cost(6 * full * full * part * ny, 8 * full * part * ny),
        name="forward_x",
    )(after, *bxt, *pieces)


def middle_y(pieces, by, byt, shift, eigen_y, after):
    part, wide, ny = pieces[0].shape
    peers = len(pieces)
    full = peers * ny
    cb = 2 if part % 2 == 0 and wide % 8 == 0 else 1

    def kernel(_, bh, bl, th, tl, shift_ref, ey_ref, *refs):
        ins, outs = refs[:peers], refs[peers:]
        parts = [split(r[...].reshape(cb * wide, ny)) for r in ins]
        spectrum = sum_dots(parts, (bh, bl), ny)
        ey = ey_ref[...]
        scaled = [
            spectrum[n * wide : (n + 1) * wide, :] / (shift_ref[n] + ey)
            for n in range(cb)
        ]
        back = dot3(split(join(scaled, 0)), (th[...], tl[...]), NN)
        for e, out in enumerate(outs):
            out[...] = back[:, e * ny : (e + 1) * ny].reshape(cb, wide, ny)

    spec = pl.BlockSpec((cb, wide, ny), lambda i: (i, 0, 0))
    return pl.pallas_call(
        kernel,
        grid=(part // cb,),
        out_shape=[jax.ShapeDtypeStruct((part, wide, ny), F32)] * peers,
        in_specs=[pl.BlockSpec(memory_space=pl.ANY)]
        + [whole((full, full))] * 4
        + [pl.BlockSpec((cb, wide, 1), lambda i: (i, 0, 0)), whole((1, full))]
        + [spec] * peers,
        out_specs=[spec] * peers,
        compiler_params=params(1),
        cost_estimate=cost(12 * full * full * part * wide, 8 * full * part * wide),
        name="middle_y",
    )(after, *by, *byt, shift, eigen_y, *pieces)


def backward_x(pieces, bx, peers, after):
    part, wide, ny = pieces[0].shape
    full = wide * len(pieces)
    nx = full // peers

    def kernel(_, bh, bl, *refs):
        ins, outs = refs[: len(pieces)], refs[len(pieces) :]
        for c in range(part):
            v = split(join([r[c] for r in ins], 0))
            t = dot3((bh[...], bl[...]), v, NN)
            for d, out in enumerate(outs):
                out[:, c, :] = t[d * nx : (d + 1) * nx, :]

    return pl.pallas_call(
        kernel,
        out_shape=[jax.ShapeDtypeStruct((nx, part, ny), F32)] * peers,
        in_specs=[pl.BlockSpec(memory_space=pl.ANY)]
        + [pl.BlockSpec(memory_space=pltpu.VMEM)] * (2 + len(pieces)),
        out_specs=[pl.BlockSpec(memory_space=pltpu.VMEM)] * peers,
        compiler_params=params(0),
        cost_estimate=cost(6 * full * full * part * ny, 8 * full * part * ny),
        name="backward_x",
    )(after, *bx, *pieces)


def backward_z(pieces, basis_zt, where, adjoint, coefficient):
    nx, ny, nz = adjoint.shape
    peers, part = len(pieces[0]), pieces[0][0].shape[1]
    group = peers * part
    chunks = len(pieces)
    xb = 8
    flat = [p for chunk in pieces for p in chunk]

    def kernel(where_ref, b_ref, adj_ref, coef_ref, *refs):
        ins, (next_ref, weighted_ref) = refs[:-2], refs[-2:]
        me = where_ref[0]
        rows = [
            b_ref[pl.ds(pl.multiple_of(k * group + (me ^ d) * part, part), part), :]
            for k in range(chunks)
            for d in range(peers)
        ]
        basis = split(join(rows, 0))
        for x in range(xb):
            v = split(join([r[x] for r in ins], 0))
            correction = dot3(v, basis, TN)
            next_ref[x] = adj_ref[x] + correction
            weighted_ref[x] = coef_ref[x].astype(F32) * correction

    field = pl.BlockSpec((xb, ny, nz), lambda i, w: (i, 0, 0))
    return pl.pallas_call(
        kernel,
        grid_spec=pltpu.PrefetchScalarGridSpec(
            num_scalar_prefetch=1,
            grid=(nx // xb,),
            in_specs=[pl.BlockSpec(basis_zt.shape, lambda i, w: (0, 0)), field, field]
            + [pl.BlockSpec((xb, part, ny), lambda i, w: (i, 0, 0))] * len(flat),
            out_specs=[field, field],
        ),
        out_shape=[jax.ShapeDtypeStruct((nx, ny, nz), F32)] * 2,
        compiler_params=params(1),
        cost_estimate=cost(6 * nx * ny * nz * nz, 22 * nx * ny * nz),
        name="backward_z",
    )(where, basis_zt, adjoint, coefficient, *flat)


def band(n):
    out = np.zeros((2 * n, n), np.float32)
    for j in range(-3, 4):
        out[:n] += MASS[j + 3] * np.eye(n, k=j, dtype=np.float32)
        out[n:] += STIFF[j + 3] * np.eye(n, k=j, dtype=np.float32)
    return out


def taps(load, mass=True, stiff=True):
    mid = load(0)
    pair = [load(j) + load(-j) for j in (1, 2, 3)]
    out = []
    for use, co in ((mass, MASS), (stiff, STIFF)):
        if use:
            out.append(co[3] * mid + co[4] * pair[0] + co[5] * pair[1] + co[6] * pair[2])
    return out


def stencil(weighted, residual, x_low, x_high, y_low, y_high, bands):
    nx, ny, nz = weighted.shape
    xb = 8
    steps = nx // xb
    halves = nz // 128

    def kernel(bh, bl, xl, xh, yl, yh, prev, cur, nxt, r_ref, out, ps, qs, ph, qh):
        i = pl.program_id(0)

        @pl.when(i == 0)
        def _():
            for side, ref in ((0, yl), (1, yh)):
                for j in range(3):
                    p, q = taps(lambda o: ref[j, 3 + o : 3 + o + nx, :])
                    ph[side, :, j, :] = p
                    qh[side, :, j, :] = q

        first, last = i == 0, i == steps - 1
        before = [
            jnp.where(first, xl[j], prev[xb - 3 + j]) for j in range(3)
        ]
        after = [jnp.where(last, xh[j], nxt[j]) for j in range(3)]

        for x in range(xb):

            def plane(o):
                n = x + o
                if n < 0:
                    return before[n + 3]
                return cur[n] if n < xb else after[n - xb]

            p, q = taps(plane)
            for h in range(halves):
                cols = slice(h * 128, (h + 1) * 128)
                ps[h, 8 : 8 + ny, :] = p[:, cols]
                qs[h, 8 : 8 + ny, :] = q[:, cols]
                for side, base in ((0, 5), (1, 8 + ny)):
                    ps[h, base : base + 3, :] = ph[side, i * xb + x, :3, cols]
                    qs[h, base : base + 3, :] = qh[side, i * xb + x, :3, cols]
            first_terms, second_terms = [], []
            for h in range(halves):
                mp, kp = taps(lambda o: ps[h, 8 + o : 8 + o + ny, :])
                (mq,) = taps(lambda o: qs[h, 8 + o : 8 + o + ny, :], stiff=False)
                first_terms.append(kp + mq)
                second_terms.append(mp)
            both = split(join(first_terms + second_terms, 1))
            out[x] = r_ref[x] - dot3(both, (bh[...], bl[...]), NN)

    field = pl.BlockSpec((xb, ny, nz), lambda i: (i, 0, 0))
    return pl.pallas_call(
        kernel,
        grid=(steps,),
        in_specs=[whole(b.shape) for b in bands]
        + [whole(x_low.shape)] * 2
        + [whole(y_low.shape)] * 2
        + [
            pl.BlockSpec((xb, ny, nz), lambda i: (jnp.maximum(i - 1, 0), 0, 0)),
            field,
            pl.BlockSpec((xb, ny, nz), lambda i: (jnp.minimum(i + 1, steps - 1), 0, 0)),
            field,
        ],
        out_specs=field,
        out_shape=jax.ShapeDtypeStruct((nx, ny, nz), F32),
        scratch_shapes=[pltpu.VMEM((halves, ny + 16, 128), F32)] * 2
        + [pltpu.VMEM((2, nx, 8, nz), F32)] * 2,
        compiler_params=params(1),
        cost_estimate=cost(12 * nx * ny * nz * nz, 12 * nx * ny * nz),
        name="stencil",
    )(*bands, x_low, x_high, y_low, y_high, weighted, weighted, weighted, residual)


def exchange(pieces, axis):
    n = len(pieces)
    out = [pieces[0]] + [None] * (n - 1)
    for d in range(n - 1, 0, -1):
        out[d] = lax.ppermute(pieces[d], axis, [(i, i ^ d) for i in range(n)])
    return out


def neighbours(low, high, axis):
    n = lax.axis_size(axis)
    up = [(i, i + 1) for i in range(n - 1)]
    down = [(i + 1, i) for i in range(n - 1)]
    return lax.ppermute(high, axis, up), lax.ppermute(low, axis, down)


def schedule(chunks):
    order = [("z", 0), ("z", 1)][:chunks]
    if chunks == 4:
        order += [("x", 0), ("y", 0), ("b", 0), ("x", 1), ("x", 2), ("y", 1)]
        order += [("x", 3), ("y", 2), ("b", 1), ("y", 3), ("b", 2), ("b", 3)]
    else:
        order += [(s, k) for k in range(chunks) for s in ("x", "y", "b")]
    return order


def chunk_count(nz, rows):
    return max(1, min(4, nz // (rows * 8)))


def shards(residual, adjoint, coefficient, basis_x, basis_y, basis_z, eigen_x, eigen_y, eigen_z):
    nx, ny, nz = residual.shape
    rows, cols = lax.axis_size("row"), lax.axis_size("col")
    ri, ci = lax.axis_index("row"), lax.axis_index("col")
    width_x = nx * rows
    wide = width_x // cols
    chunks = chunk_count(nz, rows)
    part = nz // (rows * chunks)
    where = jnp.stack([ri, ci]).astype(jnp.int32)

    basis_zt = basis_z.T
    bx = jnp.concatenate(
        [lax.dynamic_slice_in_dim(basis_x, (ri ^ d) * nx, nx, 0) for d in range(rows)], 0
    )
    bx = jnp.concatenate(
        [lax.dynamic_slice_in_dim(bx, (ci ^ e) * wide, wide, 1) for e in range(cols)], 1
    )
    by = jnp.concatenate(
        [lax.dynamic_slice_in_dim(basis_y, (ci ^ e) * ny, ny, 0) for e in range(cols)], 0
    )
    bx2, by2 = split_outside(bx), split_outside(by)
    bxt2, byt2 = tuple(b.T for b in bx2), tuple(b.T for b in by2)
    ex = lax.dynamic_slice_in_dim(eigen_x, ci * wide, wide)
    ez = lax.dynamic_slice_in_dim(eigen_z.reshape(chunks, rows, part), ri, 1, 1)[:, 0]
    shift = (ez[:, :, None] + ex[None, None, :])[..., None]
    ey = eigen_y[None, :]
    bands = split_outside(jnp.asarray(band(nz)))

    fw, mid, ret, back = ([None] * chunks for _ in range(4))
    last = where
    for stage, k in schedule(chunks):
        if stage == "z":
            these = (k,) if k == 0 else tuple(range(k, chunks))
            outs = forward_z(residual, basis_zt, where, these, rows, part)
            for n, out in zip(these, outs):
                fw[n] = (out, "row")
            last = outs[-1][0]
        elif stage == "x":
            out = forward_x(fw[k], bxt2, cols, last)
        elif stage == "y":
            out = middle_y(mid[k], by2, byt2, shift[k], ey, last)
        else:
            out = backward_x(ret[k], bx2, rows, last)
        if stage == "z":
            for n in these:
                fw[n] = exchange(*fw[n])
        elif stage == "x":
            mid[k] = exchange(out, "col")
        elif stage == "y":
            ret[k] = exchange(out, "col")
        else:
            back[k] = exchange(out, "row")
        if stage != "z":
            last = out[0]
    adjoint_next, weighted = backward_z(back, basis_zt, where, adjoint, coefficient)
    x_low, x_high = neighbours(weighted[:3], weighted[-3:], "row")
    edge_low = jnp.concatenate([x_low[:, :3], weighted[:, :3], x_high[:, :3]], 0)
    edge_high = jnp.concatenate([x_low[:, -3:], weighted[:, -3:], x_high[:, -3:]], 0)
    y_low, y_high = neighbours(
        edge_low.transpose(1, 0, 2), edge_high.transpose(1, 0, 2), "col"
    )
    residual_next = stencil(weighted, residual, x_low, x_high, y_low, y_high, bands)
    return adjoint_next, residual_next


def solution(mesh):
    field = P("row", "col", None)
    return jax.shard_map(
        shards,
        mesh=mesh,
        in_specs=(field,) * 3 + (P(),) * 6,
        out_specs=(field, field),
        check_vma=False,
    )
```

time: 979 us -> 561 us (0.57)
  blocking collectives: 283 us -> 0 us
  other arithmetic: 264 us -> 1.02 us
  Pallas kernels: 0 us -> 153 us
  starting transfers between devices: 23.3 us -> 137 us
  matrix products: 94 us -> 0 us
  waiting for transfers between devices: 293 us -> 236 us
  local copies, waits for them, and re-layouts: 13.5 us -> 24.9 us
    all_to_all x2 -> x0, blocking collectives: 283 us -> none  [the longest x1 187 us: shards(): lax.all_to_all(middle_back, 'row', split_axis=0, concat_axis=0, tiled=True)]
    all_to_all x2 -> x0, waiting for transfers between devices: 271 us -> none  [the longest x1 180 us: shards(): lax.all_to_all(outgoing, 'row', split_axis=0, concat_axis=0, tiled=True)]
    ppermute x4 -> x84, waiting for transfers between devices: 22.1 us -> 236 us  [the longest x80 212 us: exchange(): out[d] = lax.ppermute(pieces[d], axis, [(i, i ^ d) for i in range(n)])]
    add x4 -> x1, other arithmetic: 165 us -> 0.07 us  [shards(): shift = (ez[:, :, None] + ex[None, None, :])[..., None]]
    pallas_call x0 -> x16, Pallas kernels: none -> 153 us  [the longest x4 30.5 us: middle_y(): pl.pallas_call(kernel, grid=(part // cb,), out_shape=[jax.ShapeDtypeStruc...]
    ppermute x4 -> x84, starting transfers between devices: 11.1 us -> 137 us  [the longest x80 127 us: exchange(): out[d] = lax.ppermute(pieces[d], axis, [(i, i ^ d) for i in range(n)])]
    dot_general x6 -> x0, matrix products: 94 us -> none  [the longest x1 19 us: shards(): jnp.einsum('jcxy,zjc->xyz', lax.all_to_all(middle_back, 'row', split_axis...]
    sub x1 -> x0, other arithmetic: 83.9 us -> none  [shards(): return (adjoint + correction, residual - image)]
  transfers between devices with their start and end apart: 6 -> 84, of which waited for: 6 -> 38; matrix products, arithmetic and copies ran while one was open for 0% -> 2% of each run, Pallas kernels for 0% -> 18%
where the time goes in v1:
time: 561 us; the launch traced here: 553 us
  waiting for transfers between devices  236 us (42%)
  Pallas kernels  153 us (27%)
  starting transfers between devices  137 us (24%)
  local copies, waits for them, and re-layouts  24.9 us (4%)
    ppermute x80, waiting for transfers between devices, exchange(): out[d] = lax.ppermute(pieces[d], axis, [(i, i ^ d) for i in range(n)])  212 us
    ppermute x80, starting transfers between devices, exchange(): out[d] = lax.ppermute(pieces[d], axis, [(i, i ^ d) for i in range(n)])  127 us
    pallas_call x4, Pallas kernels, middle_y(): pl.pallas_call(kernel, grid=(part // cb,), out_shape=[jax.ShapeDtypeStruc...  30.5 us
    pallas_call x4, Pallas kernels, backward_x(): pl.pallas_call(kernel, out_shape=[jax.ShapeDtypeStruct((nx, part, ny), F3...  28.7 us
    pallas_call x1, Pallas kernels, stencil(): pl.pallas_call(kernel, grid=(steps,), in_specs=[whole(b.shape) for b in b...  28.6 us
    pallas_call x4, Pallas kernels, forward_x(): pl.pallas_call(kernel, out_shape=[jax.ShapeDtypeStruct((part, wide, ny),...  26.9 us
    ppermute x4, waiting for transfers between devices, neighbours(): return (lax.ppermute(high, axis, up), lax.ppermute(low, axis, down))  23.7 us
    pallas_call x2, Pallas kernels, forward_z(): pl.pallas_call(kernel, grid_spec=pltpu.PrefetchScalarGridSpec(num_scalar_...  21.5 us
  transfers between devices with their start and end apart: 84, of which 38 were waited for; matrix products, arithmetic and copies ran while one was open for 2% of the time, Pallas kernels for 18%

profile of v1, /device:TPU:9, one launch (start us, length us, event | category | flops | bytes accessed | tf_op | source)
XLA Modules:
  0.0 553.3 jit_solution(11763593566063960018)
XLA Ops:
  3.2 10.1 %forward_z.3 = (f32[64,8,128]{2,1,0:T(8,128)}, f32[64,8,128]{2,1,0:T(8,128)}, f32[64,8,128]{2,1,0:T(8,128)}, f32[64,8,128]{2,1,0:T(8,128)}, f32[64,8,128]{2,1,0:...) custom-call(s32[2]{0:T(128)} %pad_add_fusion.where_ref, f32[64,128,256]{2,1,0:T(8,128)} %r_ref.5, ...), custom_call_target="tpu_custom_call" | custom-call | flops 805306368 | bytes 8388608 | tf_op jit(solution)/shard_map/forward_z/pallas_call | solution.py:84
  22.1 7.7 %collective-permute-done.1.refs_2_ = f32[64,8,128]{2,1,0:T(8,128)S(1)} collective-permute-done((f32[64,8,128]{2,1,0:T(8,128)}, f32[64,8,128]{2,1,0:T(8,128)S(1)}, u32[]{:S(2)}, u32[]{:S(2)}) %collective-permute-start.1) | collective-permute-done | bytes 262176 | tf_op jit(solution)/shard_map/ppermute | solution.py:326
  32.8 11.4 %forward_z.2 = (f32[64,8,128]{2,1,0:T(8,128)}, f32[64,8,128]{2,1,0:T(8,128)}, f32[64,8,128]{2,1,0:T(8,128)}, f32[64,8,128]{2,1,0:T(8,128)}, f32[64,8,128]{2,1,0:...) custom-call(s32[2]{0:T(128)} %pad_add_fusion.where_ref, ...), custom_call_target="tpu_custom_call" | custom-call | flops 2415919104 | bytes 8388608 | tf_op jit(solution)/shard_map/forward_z/pallas_call | solution.py:84
  56.6 8.3 %collective-permute-done.6.refs_7_ = f32[64,8,128]{2,1,0:T(8,128)} collective-permute-done((f32[64,8,128]{2,1,0:T(8,128)}, f32[64,8,128]{2,1,0:T(8,128)}, u32[]{:S(2)}, u32[]{:S(2)}) %collective-permute-start.6) | collective-permute-done | bytes 262176 | tf_op jit(solution)/shard_map/ppermute | solution.py:326
  75.1 10.2 %collective-permute-start.7 = (f32[8,128,128]{2,1,0:T(8,128)}, f32[8,128,128]{2,1,0:T(8,128)S(1)}, u32[]{:S(2)}, u32[]{:S(2)}) collective-permute-start(f32[8,128,128]{2,1,0:T(8,128)} %get-tuple-element.110), channel_id=1, source_target_pairs={{0,1},{1,0},{2,3},{3,2},{4,5},{5,4},{6,7},{7,6},{8,9},{9,8},{10,11... | collective-permute-start | bytes 1572872 | tf_op jit(solution)/shard_map/ppermute | solution.py:326
  86.5 9.4 %collective-permute-done.24.refs_5_ = f32[64,8,128]{2,1,0:T(8,128)S(1)} collective-permute-done((f32[64,8,128]{2,1,0:T(8,128)}, f32[64,8,128]{2,1,0:T(8,128)S(1)}, u32[]{:S(2)}, u32[]{:S(2)}) %collective-permute-start.24) | collective-permute-done | bytes 262176 | tf_op jit(solution)/shard_map/ppermute | solution.py:326
  120.5 7.6 %middle_y.4 = (f32[8,128,128]{2,1,0:T(8,128)}, f32[8,128,128]{2,1,0:T(8,128)}, f32[8,128,128]{2,1,0:T(8,128)}, f32[8,128,128]{2,1,0:T(8,128)}) custom-call(f32[8,128,128]{2,1,0:T(8,128)} %get-tuple-element.109._.refs_0_, bf16[512,512]{1,0:T(8,128)(2,1)} %copy.139.bh, bf16[512,512]{1,0:T(8,128)(2,1)} %copy.140.bl, bf16[512,512]{1,0:T(8,128)(2,1)} %bitcast.30, ...), custom_call_target="tpu_custom_call" | custom-call | flops 3221225472 | bytes 4194304 | tf_op jit(solution)/shard_map/middle_y/pallas_call | solution.py:153
  131.9 14.1 %collective-permute-start.11 = (f32[8,128,128]{2,1,0:T(8,128)}, f32[8,128,128]{2,1,0:T(8,128)S(1)}, u32[]{:S(2)}, u32[]{:S(2)}) collective-permute-start(f32[8,128,128]{2,1,0:T(8,128)} %get-tuple-element.115), channel_id=1, source_target_pairs={{0,2},{1,3},{2,0},{3,1},{4,6},{5,7},{6,4},{7,5},{8,10},{9,11},{10,... | collective-permute-start | bytes 1572872 | tf_op jit(solution)/shard_map/ppermute | solution.py:326
  191.7 11.1 %collective-permute-done.41.refs_5_ = f32[64,8,128]{2,1,0:T(8,128)S(1)} collective-permute-done((f32[64,8,128]{2,1,0:T(8,128)}, f32[64,8,128]{2,1,0:T(8,128)S(1)}, u32[]{:S(2)}, u32[]{:S(2)}) %collective-permute-start.41) | collective-permute-done | bytes 262176 | tf_op jit(solution)/shard_map/ppermute | solution.py:326
  202.7 9.0 %collective-permute-start.34 = (f32[8,128,128]{2,1,0:T(8,128)}, f32[8,128,128]{2,1,0:T(8,128)S(1)}, u32[]{:S(2)}, u32[]{:S(2)}) collective-permute-start(f32[8,128,128]{2,1,0:T(8,128)} %get-tuple-element.143), channel_id=1, source_target_pairs={{0,1},{1,0},{2,3},{3,2},{4,5},{5,4},{6,7},{7,6},{8,9},{9,8},{10,11... | collective-permute-start | bytes 1572872 | tf_op jit(solution)/shard_map/ppermute | solution.py:326
  240.8 7.6 %middle_y.5 = (f32[8,128,128]{2,1,0:T(8,128)}, f32[8,128,128]{2,1,0:T(8,128)}, f32[8,128,128]{2,1,0:T(8,128)}, f32[8,128,128]{2,1,0:T(8,128)}) custom-call(f32[8,128,128]{2,1,0:T(8,128)} %get-tuple-element.142._.refs_0_, bf16[512,512]{1,0:T(8,128)(2,1)} %copy.139.bh, bf16[512,512]{1,0:T(8,128)(2,1)} %copy.140.bl, bf16[512,512]{1,0:T(8,128)(2,1)} %bitcast.31, ...), custom_call_target="tpu_custom_call" | custom-call | flops 3221225472 | bytes 4194304 | tf_op jit(solution)/shard_map/middle_y/pallas_call | solution.py:153
  297.4 12.1 %collective-permute-done.59.refs_3_ = f32[8,128,128]{2,1,0:T(8,128)} collective-permute-done((f32[8,128,128]{2,1,0:T(8,128)}, f32[8,128,128]{2,1,0:T(8,128)}, u32[]{:S(2)}, u32[]{:S(2)}) %collective-permute-start.59) | collective-permute-done | bytes 524320 | tf_op jit(solution)/shard_map/ppermute | solution.py:326
  310.4 8.9 %collective-permute-done.61.refs_2_ = f32[8,128,128]{2,1,0:T(8,128)S(1)} collective-permute-done((f32[8,128,128]{2,1,0:T(8,128)}, f32[8,128,128]{2,1,0:T(8,128)S(1)}, u32[]{:S(2)}, u32[]{:S(2)}) %collective-permute-start.61) | collective-permute-done | bytes 524320 | tf_op jit(solution)/shard_map/ppermute | solution.py:326
  319.3 8.0 %middle_y.7 = (f32[8,128,128]{2,1,0:T(8,128)}, f32[8,128,128]{2,1,0:T(8,128)}, f32[8,128,128]{2,1,0:T(8,128)}, f32[8,128,128]{2,1,0:T(8,128)}) custom-call(f32[64,8,128]{2,1,0:T(8,128)} %get-tuple-element.162._.refs_8_, bf16[512,512]{1,0:T(8,128)(2,1)} %copy.139.bh, bf16[512,512]{1,0:T(8,128)(2,1)} %copy.140.bl, bf16[512,512]{1,0:T(8,128)(2,1)} %bitcast.33, ...), custom_call_target="tpu_custom_call" | custom-call | flops 3221225472 | bytes 4194304 | tf_op jit(solution)/shard_map/middle_y/pallas_call | solution.py:153
  342.1 8.6 %collective-permute-done.54.refs_13_ = f32[64,8,128]{2,1,0:T(8,128)S(1)} collective-permute-done((f32[64,8,128]{2,1,0:T(8,128)S(1)}, f32[64,8,128]{2,1,0:T(8,128)S(1)}, u32[]{:S(2)}, u32[]{:S(2)}) %collective-permute-start.54) | collective-permute-done | bytes 262176 | tf_op jit(solution)/shard_map/ppermute | solution.py:326
  351.2 12.3 %collective-permute-done.55.refs_14_ = f32[64,8,128]{2,1,0:T(8,128)S(1)} collective-permute-done((f32[64,8,128]{2,1,0:T(8,128)S(1)}, f32[64,8,128]{2,1,0:T(8,128)S(1)}, u32[]{:S(2)}, u32[]{:S(2)}) %collective-permute-start.55) | collective-permute-done | bytes 262176 | tf_op jit(solution)/shard_map/ppermute | solution.py:326
  384.3 18.1 %collective-permute-done.67.refs_21_ = f32[64,8,128]{2,1,0:T(8,128)S(1)} collective-permute-done((f32[64,8,128]{2,1,0:T(8,128)}, f32[64,8,128]{2,1,0:T(8,128)S(1)}, u32[]{:S(2)}, u32[]{:S(2)}) %collective-permute-start.67) | collective-permute-done | bytes 262176 | tf_op jit(solution)/shard_map/ppermute | solution.py:326
  409.8 12.8 %collective-permute-done.69.refs_23_ = f32[64,8,128]{2,1,0:T(8,128)S(1)} collective-permute-done((f32[64,8,128]{2,1,0:T(8,128)}, f32[64,8,128]{2,1,0:T(8,128)S(1)}, u32[]{:S(2)}, u32[]{:S(2)}) %collective-permute-start.69) | collective-permute-done | bytes 262176 | tf_op jit(solution)/shard_map/ppermute | solution.py:326
  423.8 18.2 %collective-permute-done.76.refs_28_ = f32[64,8,128]{2,1,0:T(8,128)S(1)} collective-permute-done((f32[64,8,128]{2,1,0:T(8,128)}, f32[64,8,128]{2,1,0:T(8,128)S(1)}, u32[]{:S(2)}, u32[]{:S(2)}) %collective-permute-start.76) | collective-permute-done | bytes 262176 | tf_op jit(solution)/shard_map/ppermute | solution.py:326
  447.7 7.4 %collective-permute-done.78.refs_30_ = f32[64,8,128]{2,1,0:T(8,128)S(1)} collective-permute-done((f32[64,8,128]{2,1,0:T(8,128)}, f32[64,8,128]{2,1,0:T(8,128)S(1)}, u32[]{:S(2)}, u32[]{:S(2)}) %collective-permute-start.78) | collective-permute-done | bytes 262176 | tf_op jit(solution)/shard_map/ppermute | solution.py:326
  462.6 16.9 %backward_z.1 = (f32[64,128,256]{2,1,0:T(8,128)}, f32[64,128,256]{2,1,0:T(8,128)}) custom-call(s32[2]{0:T(128)} %pad_add_fusion.where_ref, f32[256,256]{1,0:T(8,128)} %bitcast.23, f32[64,128,256]{2,1,0:T(8,128)} %adj_ref.1, bf16[64,128,256]{2,1,0:T(8,128)(2,1)} %coef_ref.1, f32[64,8,128]{2,1,0:T(8,128)} %get-tuple-element.117._.refs_0_, ...), custom_call_target="tpu_custom_call" | custom-call | flops 3221225472 | bytes 46137344 | tf_op jit(solution)/shard_map/backward_z/pallas_call | solution.py:217
  479.5 8.3 %copy.157 = f32[64,128,256]{2,0,1:T(8,128)S(1)} copy(f32[64,128,256]{2,1,0:T(8,128)} %get-tuple-element.197.prev.cur.nxt) | data formatting | bytes 16777216 | tf_op jit(solution)/shard_map/backward_z/pallas_call | solution.py:217
  493.3 19.7 %collective-permute-done.81 = f32[3,128,256]{2,0,1:T(4,128)S(1)} collective-permute-done((f32[3,128,256]{2,0,1:T(4,128)S(1)}, f32[3,128,256]{2,0,1:T(4,128)S(1)}, u32[]{:S(2)}, u32[]{:S(2)}) %collective-permute-start.81) | collective-permute-done | bytes 393248 | tf_op jit(solution)/shard_map/ppermute | solution.py:334
  524.5 28.6 %stencil.1 = f32[64,128,256]{2,1,0:T(8,128)} custom-call(bf16[512,256]{1,0:T(8,128)(2,1)} %constant.37.bh, bf16[512,256]{1,0:T(8,128)(2,1)} %constant.39.bl, f32[3,128,256]{2,1,0:T(8,128)} %copy.161.xl, f32[3,128,256]{2,1,0:T(8,128)} %copy.162.xh, f32[3,70,256]{2,1,0:T(8,128)} %copy-done.34, f32[3,70,256]{2,1,0:T(8,128)} %copy-done.35, ...), custom_call_target="tpu_custom_call" | custom-call | flops 6442450944 | bytes 25165824 | tf_op jit(solution)/shard_map/stencil/pallas_call | solution.py:300
  (364 shorter events, 265.1 us)
Async XLA Ops:
  20.8 35.8 %collective-permute-start.5 = (f32[64,8,128]{2,1,0:T(8,128)}, f32[64,8,128]{2,1,0:T(8,128)}, u32[]{:S(2)}, u32[]{:S(2)}) collective-permute-start(f32[64,8,128]{2,1,0:T(8,128)} %get-tuple-element.107), channel_id=1, source_target_pairs={{0,24},{4,28},{8,16},{12,20},{16,8},{20,12},{24,0},{28,4},{1,25},{... | collective-permute-start | bytes 786440 | tf_op jit(solution)/shard_map/ppermute | solution.py:326
  29.7 35.2 %collective-permute-start.6 = (f32[64,8,128]{2,1,0:T(8,128)}, f32[64,8,128]{2,1,0:T(8,128)}, u32[]{:S(2)}, u32[]{:S(2)}) collective-permute-start(f32[64,8,128]{2,1,0:T(8,128)} %get-tuple-element.108), channel_id=1, source_target_pairs={{0,28},{4,24},{8,20},{12,16},{16,12},{20,8},{24,4},{28,0},{1,29},{... | collective-permute-start | bytes 786440 | tf_op jit(solution)/shard_map/ppermute | solution.py:326
  75.0 32.8 %collective-permute-start.26 = (f32[64,8,128]{2,1,0:T(8,128)}, f32[64,8,128]{2,1,0:T(8,128)S(1)}, u32[]{:S(2)}, u32[]{:S(2)}) collective-permute-start(f32[64,8,128]{2,1,0:T(8,128)} %get-tuple-element.132), channel_id=1, source_target_pairs={{0,28},{4,24},{8,20},{12,16},{16,12},{20,8},{24,4},{28,0},{1,29},{... | collective-permute-start | bytes 786440 | tf_op jit(solution)/shard_map/ppermute | solution.py:326
  75.1 43.0 %collective-permute-start.7 = (f32[8,128,128]{2,1,0:T(8,128)}, f32[8,128,128]{2,1,0:T(8,128)S(1)}, u32[]{:S(2)}, u32[]{:S(2)}) collective-permute-start(f32[8,128,128]{2,1,0:T(8,128)} %get-tuple-element.110), channel_id=1, source_target_pairs={{0,1},{1,0},{2,3},{3,2},{4,5},{5,4},{6,7},{7,6},{8,9},{9,8},{10,11... | collective-permute-start | bytes 1572872 | tf_op jit(solution)/shard_map/ppermute | solution.py:326
  85.3 32.8 %collective-permute-start.8 = (f32[8,128,128]{2,1,0:T(8,128)}, f32[8,128,128]{2,1,0:T(8,128)S(1)}, u32[]{:S(2)}, u32[]{:S(2)}) collective-permute-start(f32[8,128,128]{2,1,0:T(8,128)} %get-tuple-element.111), channel_id=1, source_target_pairs={{0,2},{1,3},{2,0},{3,1},{4,6},{5,7},{6,4},{7,5},{8,10},{9,11},{10,... | collective-permute-start | bytes 1572872 | tf_op jit(solution)/shard_map/ppermute | solution.py:326
  118.1 38.1 %collective-permute-start.32 = (f32[64,8,128]{2,1,0:T(8,128)}, f32[64,8,128]{2,1,0:T(8,128)S(1)}, u32[]{:S(2)}, u32[]{:S(2)}) collective-permute-start(f32[64,8,128]{2,1,0:T(8,128)} %get-tuple-element.140), channel_id=1, source_target_pairs={{0,24},{4,28},{8,16},{12,20},{16,8},{20,12},{24,0},{28,4},{1,25},{... | collective-permute-start | bytes 786440 | tf_op jit(solution)/shard_map/ppermute | solution.py:326
  119.3 43.6 %collective-permute-start.33 = (f32[64,8,128]{2,1,0:T(8,128)}, f32[64,8,128]{2,1,0:T(8,128)S(1)}, u32[]{:S(2)}, u32[]{:S(2)}) collective-permute-start(f32[64,8,128]{2,1,0:T(8,128)} %get-tuple-element.141), channel_id=1, source_target_pairs={{0,28},{4,24},{8,20},{12,16},{16,12},{20,8},{24,4},{28,0},{1,29},{... | collective-permute-start | bytes 786440 | tf_op jit(solution)/shard_map/ppermute | solution.py:326
  128.1 42.7 %collective-permute-start.10 = (f32[8,128,128]{2,1,0:T(8,128)}, f32[8,128,128]{2,1,0:T(8,128)S(1)}, u32[]{:S(2)}, u32[]{:S(2)}) collective-permute-start(f32[8,128,128]{2,1,0:T(8,128)} %get-tuple-element.114), channel_id=1, source_target_pairs={{0,1},{1,0},{2,3},{3,2},{4,5},{5,4},{6,7},{7,6},{8,9},{9,8},{10,11... | collective-permute-start | bytes 1572872 | tf_op jit(solution)/shard_map/ppermute | solution.py:326
  131.9 39.3 %collective-permute-start.11 = (f32[8,128,128]{2,1,0:T(8,128)}, f32[8,128,128]{2,1,0:T(8,128)S(1)}, u32[]{:S(2)}, u32[]{:S(2)}) collective-permute-start(f32[8,128,128]{2,1,0:T(8,128)} %get-tuple-element.115), channel_id=1, source_target_pairs={{0,2},{1,3},{2,0},{3,1},{4,6},{5,7},{6,4},{7,5},{8,10},{9,11},{10,... | collective-permute-start | bytes 1572872 | tf_op jit(solution)/shard_map/ppermute | solution.py:326
  171.2 40.5 %collective-permute-start.42 = (f32[64,8,128]{2,1,0:T(8,128)}, f32[64,8,128]{2,1,0:T(8,128)S(1)}, u32[]{:S(2)}, u32[]{:S(2)}) collective-permute-start(f32[64,8,128]{2,1,0:T(8,128)} %get-tuple-element.152), channel_id=1, source_target_pairs={{0,24},{4,28},{8,16},{12,20},{16,8},{20,12},{24,0},{28,4},{1,25},{... | collective-permute-start | bytes 786440 | tf_op jit(solution)/shard_map/ppermute | solution.py:326
  172.3 42.8 %collective-permute-start.43 = (f32[64,8,128]{2,1,0:T(8,128)S(1)}, f32[64,8,128]{2,1,0:T(8,128)S(1)}, u32[]{:S(2)}, u32[]{:S(2)}) collective-permute-start(f32[64,8,128]{2,1,0:T(8,128)S(1)} %copy-done.53), channel_id=1, source_target_pairs={{0,28},{4,24},{8,20},{12,16},{16,12},{20,8},{24,4},{28,0},{1,29},{... | collective-permute-start | bytes 786440 | tf_op jit(solution)/shard_map/ppermute | solution.py:326
  180.6 38.2 %collective-permute-start.13 = (f32[64,8,128]{2,1,0:T(8,128)}, f32[64,8,128]{2,1,0:T(8,128)S(1)}, u32[]{:S(2)}, u32[]{:S(2)}) collective-permute-start(f32[64,8,128]{2,1,0:T(8,128)} %get-tuple-element.118), channel_id=1, source_target_pairs={{0,4},{4,0},{8,12},{12,8},{16,20},{20,16},{24,28},{28,24},{1,5},{5... | collective-permute-start | bytes 786440 | tf_op jit(solution)/shard_map/ppermute | solution.py:326
  181.4 37.5 %collective-permute-start.14 = (f32[64,8,128]{2,1,0:T(8,128)}, f32[64,8,128]{2,1,0:T(8,128)S(1)}, u32[]{:S(2)}, u32[]{:S(2)}) collective-permute-start(f32[64,8,128]{2,1,0:T(8,128)} %get-tuple-element.119), channel_id=1, source_target_pairs={{0,8},{4,12},{8,0},{12,4},{16,24},{20,28},{24,16},{28,20},{1,9},{5... | collective-permute-start | bytes 786440 | tf_op jit(solution)/shard_map/ppermute | solution.py:326
  202.7 35.7 %collective-permute-start.34 = (f32[8,128,128]{2,1,0:T(8,128)}, f32[8,128,128]{2,1,0:T(8,128)S(1)}, u32[]{:S(2)}, u32[]{:S(2)}) collective-permute-start(f32[8,128,128]{2,1,0:T(8,128)} %get-tuple-element.143), channel_id=1, source_target_pairs={{0,1},{1,0},{2,3},{3,2},{4,5},{5,4},{6,7},{7,6},{8,9},{9,8},{10,11... | collective-permute-start | bytes 1572872 | tf_op jit(solution)/shard_map/ppermute | solution.py:326
  238.6 33.4 %collective-permute-start.46 = (f32[8,128,128]{2,1,0:T(8,128)}, f32[8,128,128]{2,1,0:T(8,128)}, u32[]{:S(2)}, u32[]{:S(2)}) collective-permute-start(f32[8,128,128]{2,1,0:T(8,128)} %get-tuple-element.157), channel_id=1, source_target_pairs={{0,3},{1,2},{2,1},{3,0},{4,7},{5,6},{6,5},{7,4},{8,11},{9,10},{10,... | collective-permute-start | bytes 1572872 | tf_op jit(solution)/shard_map/ppermute | solution.py:326
  286.2 33.0 %collective-permute-start.61 = (f32[8,128,128]{2,1,0:T(8,128)}, f32[8,128,128]{2,1,0:T(8,128)S(1)}, u32[]{:S(2)}, u32[]{:S(2)}) collective-permute-start(f32[8,128,128]{2,1,0:T(8,128)} %get-tuple-element.175), channel_id=1, source_target_pairs={{0,2},{1,3},{2,0},{3,1},{4,6},{5,7},{6,4},{7,5},{8,10},{9,11},{10,... | collective-permute-start | bytes 1572872 | tf_op jit(solution)/shard_map/ppermute | solution.py:326
  286.2 44.8 %collective-permute-start.62 = (f32[8,128,128]{2,1,0:T(8,128)}, f32[8,128,128]{2,1,0:T(8,128)S(1)}, u32[]{:S(2)}, u32[]{:S(2)}) collective-permute-start(f32[8,128,128]{2,1,0:T(8,128)} %get-tuple-element.176), channel_id=1, source_target_pairs={{0,3},{1,2},{2,1},{3,0},{4,7},{5,6},{6,5},{7,4},{8,11},{9,10},{10,... | collective-permute-start | bytes 1572872 | tf_op jit(solution)/shard_map/ppermute | solution.py:326
  296.9 34.1 %collective-permute-start.50 = (f32[64,8,128]{2,1,0:T(8,128)}, f32[64,8,128]{2,1,0:T(8,128)S(1)}, u32[]{:S(2)}, u32[]{:S(2)}) collective-permute-start(f32[64,8,128]{2,1,0:T(8,128)} %get-tuple-element.163), channel_id=1, source_target_pairs={{0,4},{4,0},{8,12},{12,8},{16,20},{20,16},{24,28},{28,24},{1,5},{5... | collective-permute-start | bytes 786440 | tf_op jit(solution)/shard_map/ppermute | solution.py:326
  331.1 32.5 %collective-permute-start.71 = (f32[8,128,128]{2,1,0:T(8,128)}, f32[8,128,128]{2,1,0:T(8,128)S(1)}, u32[]{:S(2)}, u32[]{:S(2)}) collective-permute-start(f32[8,128,128]{2,1,0:T(8,128)} %get-tuple-element.186), channel_id=1, source_target_pairs={{0,2},{1,3},{2,0},{3,1},{4,6},{5,7},{6,4},{7,5},{8,10},{9,11},{10,... | collective-permute-start | bytes 1572872 | tf_op jit(solution)/shard_map/ppermute | solution.py:326
  331.2 35.0 %collective-permute-start.72 = (f32[8,128,128]{2,1,0:T(8,128)}, f32[8,128,128]{2,1,0:T(8,128)S(1)}, u32[]{:S(2)}, u32[]{:S(2)}) collective-permute-start(f32[8,128,128]{2,1,0:T(8,128)} %get-tuple-element.187), channel_id=1, source_target_pairs={{0,3},{1,2},{2,1},{3,0},{4,7},{5,6},{6,5},{7,4},{8,11},{9,10},{10,... | collective-permute-start | bytes 1572872 | tf_op jit(solution)/shard_map/ppermute | solution.py:326
  382.1 40.4 %collective-permute-start.69 = (f32[64,8,128]{2,1,0:T(8,128)}, f32[64,8,128]{2,1,0:T(8,128)S(1)}, u32[]{:S(2)}, u32[]{:S(2)}) collective-permute-start(f32[64,8,128]{2,1,0:T(8,128)} %get-tuple-element.184), channel_id=1, source_target_pairs={{0,28},{4,24},{8,20},{12,16},{16,12},{20,8},{24,4},{28,0},{1,29},{... | collective-permute-start | bytes 786440 | tf_op jit(solution)/shard_map/ppermute | solution.py:326
  383.2 39.3 %collective-permute-start.73 = (f32[64,8,128]{2,1,0:T(8,128)}, f32[64,8,128]{2,1,0:T(8,128)S(1)}, u32[]{:S(2)}, u32[]{:S(2)}) collective-permute-start(f32[64,8,128]{2,1,0:T(8,128)} %get-tuple-element.189), channel_id=1, source_target_pairs={{0,4},{4,0},{8,12},{12,8},{16,20},{20,16},{24,28},{28,24},{1,5},{5... | collective-permute-start | bytes 786440 | tf_op jit(solution)/shard_map/ppermute | solution.py:326
  383.4 39.3 %collective-permute-start.74 = (f32[64,8,128]{2,1,0:T(8,128)}, f32[64,8,128]{2,1,0:T(8,128)S(1)}, u32[]{:S(2)}, u32[]{:S(2)}) collective-permute-start(f32[64,8,128]{2,1,0:T(8,128)} %get-tuple-element.190), channel_id=1, source_target_pairs={{0,8},{4,12},{8,0},{12,4},{16,24},{20,28},{24,16},{28,20},{1,9},{5... | collective-permute-start | bytes 786440 | tf_op jit(solution)/shard_map/ppermute | solution.py:326
  422.7 39.2 %collective-permute-start.79 = (f32[64,8,128]{2,1,0:T(8,128)}, f32[64,8,128]{2,1,0:T(8,128)S(1)}, u32[]{:S(2)}, u32[]{:S(2)}) collective-permute-start(f32[64,8,128]{2,1,0:T(8,128)} %get-tuple-element.195), channel_id=1, source_target_pairs={{0,28},{4,24},{8,20},{12,16},{16,12},{20,8},{24,4},{28,0},{1,29},{... | collective-permute-start | bytes 786440 | tf_op jit(solution)/shard_map/ppermute | solution.py:326
  (142 other events, 4434.0 us)

commit v2 on v1

--- a/solution.py
+++ b/solution.py
@@ -58,6 +58,14 @@
     return total
 
 
+def pairwise(a, v, i):
+    ny = v.shape[2]
+    if ny % 128:
+        return [(c, dot3(a, split(v[c]), NN)) for c in (2 * i, 2 * i + 1)]
+    t = dot3(a, split(join([v[2 * i], v[2 * i + 1]], 1)), NN)
+    return [(2 * i, t[:, :ny]), (2 * i + 1, t[:, ny:])]
+
+
 def whole(shape):
     return pl.BlockSpec(shape, lambda *_: (0,) * len(shape))
 
@@ -75,6 +83,7 @@
             for d in range(peers)
         ]
         basis = split(join(rows, 0))
+
         for x in range(xb):
             t = dot3(basis, split(r_ref[x]), NT)
             for n, out in enumerate(outs):
@@ -106,17 +115,16 @@
     wide = full // peers
 
     def kernel(_, bh, bl, *refs):
-        ins, outs = refs[: len(pieces)], refs[len(pieces) :]
-
-        def step(c):
-            v = split(join([r[:, c, :] for r in ins], 0))
-            t = dot3((bh[...], bl[...]), v, NN)
-            for e, out in enumerate(outs):
-                out[c] = t[e * wide : (e + 1) * wide, :]
-            return 0
-
+        ins, outs, v = refs[: len(pieces)], refs[len(pieces) : -1], refs[-1]
         for c in range(part):
-            step(c)
+            for d, r in enumerate(ins):
+                v[c, d * nx : (d + 1) * nx, :] = r[:, c, :]
+
+        @pl.loop(0, part // 2)
+        def _(i):
+            for c, t in pairwise((bh[...], bl[...]), v, i):
+                for e, out in enumerate(outs):
+                    out[c] = t[e * wide : (e + 1) * wide, :]
 
     return pl.pallas_call(
         kernel,
@@ -126,6 +134,7 @@
         out_specs=[pl.BlockSpec(memory_space=pltpu.VMEM)] * peers,
         compiler_params=params(0),
         cost_estimate=cost(6 * full * full * part * ny, 8 * full * part * ny),
+        scratch_shapes=[pltpu.VMEM((part, full, ny), F32)],
         name="forward_x",
     )(after, *bxt, *pieces)
 
@@ -171,12 +180,18 @@
     nx = full // peers
 
     def kernel(_, bh, bl, *refs):
-        ins, outs = refs[: len(pieces)], refs[len(pieces) :]
+        ins, outs, v, w = refs[: len(pieces)], refs[len(pieces) : -2], refs[-2], refs[-1]
+        for n, r in enumerate(ins):
+            v[:, n * wide : (n + 1) * wide, :] = r[...]
+
+        @pl.loop(0, part // 2)
+        def _(i):
+            for c, t in pairwise((bh[...], bl[...]), v, i):
+                w[c] = t
+
         for c in range(part):
-            v = split(join([r[c] for r in ins], 0))
-            t = dot3((bh[...], bl[...]), v, NN)
             for d, out in enumerate(outs):
-                out[:, c, :] = t[d * nx : (d + 1) * nx, :]
+                out[:, c, :] = w[c, d * nx : (d + 1) * nx, :]
 
     return pl.pallas_call(
         kernel,
@@ -186,6 +201,7 @@
         out_specs=[pl.BlockSpec(memory_space=pltpu.VMEM)] * peers,
         compiler_params=params(0),
         cost_estimate=cost(6 * full * full * part * ny, 8 * full * part * ny),
+        scratch_shapes=[pltpu.VMEM((part, full, ny), F32)] * 2,
         name="backward_x",
     )(after, *bx, *pieces)
 
@@ -196,34 +212,56 @@
     group = peers * part
     chunks = len(pieces)
     xb = 8
+    steps = nx // xb
     flat = [p for chunk in pieces for p in chunk]
 
     def kernel(where_ref, b_ref, adj_ref, coef_ref, *refs):
-        ins, (next_ref, weighted_ref) = refs[:-2], refs[-2:]
-        me = where_ref[0]
+        ins, (next_ref, w_ref, *slabs_edges) = refs[: len(flat)], refs[len(flat) :]
+        slabs, edges = slabs_edges[:2], slabs_edges[2:]
+        me, i = where_ref[0], pl.program_id(0)
         rows = [
             b_ref[pl.ds(pl.multiple_of(k * group + (me ^ d) * part, part), part), :]
             for k in range(chunks)
             for d in range(peers)
         ]
         basis = split(join(rows, 0))
+
         for x in range(xb):
             v = split(join([r[x] for r in ins], 0))
             correction = dot3(v, basis, TN)
             next_ref[x] = adj_ref[x] + correction
-            weighted_ref[x] = coef_ref[x].astype(F32) * correction
+            w_ref[x] = coef_ref[x].astype(F32) * correction
+
+        for n in range(2):
+
+            @pl.when(where_ref[1] % 2 == n)
+            def _():
+                for j in range(3):
+                    edges[n][j] = w_ref[:, ny - 3 + j, :]
+                    edges[1 - n][j] = w_ref[:, j, :]
+
+            @pl.when((i == 0) & (me % 2 == n))
+            def _():
+                slabs[1 - n][...] = w_ref[:3]
+
+            @pl.when((i == steps - 1) & (me % 2 == n))
+            def _():
+                slabs[n][...] = w_ref[xb - 3 :]
 
     field = pl.BlockSpec((xb, ny, nz), lambda i, w: (i, 0, 0))
+    slab = pl.BlockSpec((3, ny, nz), lambda i, w: (0, 0, 0))
+    edge = pl.BlockSpec((3, xb, nz), lambda i, w: (0, i, 0))
+    shapes = [(nx, ny, nz)] * 2 + [(3, ny, nz)] * 2 + [(3, nx, nz)] * 2
     return pl.pallas_call(
         kernel,
         grid_spec=pltpu.PrefetchScalarGridSpec(
             num_scalar_prefetch=1,
-            grid=(nx // xb,),
+            grid=(steps,),
             in_specs=[pl.BlockSpec(basis_zt.shape, lambda i, w: (0, 0)), field, field]
             + [pl.BlockSpec((xb, part, ny), lambda i, w: (i, 0, 0))] * len(flat),
-            out_specs=[field, field],
+            out_specs=[field] * 2 + [slab] * 2 + [edge] * 2,
         ),
-        out_shape=[jax.ShapeDtypeStruct((nx, ny, nz), F32)] * 2,
+        out_shape=[jax.ShapeDtypeStruct(shape, F32) for shape in shapes],
         compiler_params=params(1),
         cost_estimate=cost(6 * nx * ny * nz * nz, 22 * nx * ny * nz),
         name="backward_z",
@@ -248,45 +286,51 @@
     return out
 
 
-def stencil(weighted, residual, x_low, x_high, y_low, y_high, bands):
+def stencil(weighted, residual, bands, halos=None, after=None):
     nx, ny, nz = weighted.shape
     xb = 8
     steps = nx // xb
     halves = nz // 128
-
-    def kernel(bh, bl, xl, xh, yl, yh, prev, cur, nxt, r_ref, out, ps, qs, ph, qh):
+    outer = halos is not None
+    rows = lax.axis_size("row")
+
+    def kernel(_, bh, bl, *refs):
         i = pl.program_id(0)
+        if outer:
+            where_ref, xa, xc, prev, cur, nxt, r_ref, out, win, ps, qs = refs
+        else:
+            prev, cur, nxt, r_ref, out, win, ps, qs = refs
 
         @pl.when(i == 0)
         def _():
-            for side, ref in ((0, yl), (1, yh)):
-                for j in range(3):
-                    p, q = taps(lambda o: ref[j, 3 + o : 3 + o + nx, :])
-                    ph[side, :, j, :] = p
-                    qh[side, :, j, :] = q
-
-        first, last = i == 0, i == steps - 1
-        before = [
-            jnp.where(first, xl[j], prev[xb - 3 + j]) for j in range(3)
-        ]
-        after = [jnp.where(last, xh[j], nxt[j]) for j in range(3)]
-
-        for x in range(xb):
-
-            def plane(o):
-                n = x + o
-                if n < 0:
-                    return before[n + 3]
-                return cur[n] if n < xb else after[n - xb]
-
-            p, q = taps(plane)
+            zero = jnp.zeros((halves, 8, 128), F32)
+            for ref in (ps, qs):
+                ref[:, :8, :] = zero
+                ref[:, 8 + ny :, :] = zero
+
+        win[:3] = prev[xb - 3 :]
+        win[3 : 3 + xb] = cur[...]
+        win[3 + xb :] = nxt[:3]
+        if outer:
+            me = where_ref[0]
+
+            @pl.when(i == 0)
+            def _():
+                low = jnp.where(me % 2 == 0, xc[...], xa[...])
+                win[:3] = jnp.where(me == 0, 0.0, low)
+
+            @pl.when(i == 1)
+            def _():
+                high = jnp.where(me % 2 == 0, xa[...], xc[...])
+                win[3 + xb :] = jnp.where(me == rows - 1, 0.0, high)
+
+        @pl.loop(0, xb)
+        def _(x):
+            p, q = taps(lambda o: win[x + 3 + o])
             for h in range(halves):
                 cols = slice(h * 128, (h + 1) * 128)
                 ps[h, 8 : 8 + ny, :] = p[:, cols]
                 qs[h, 8 : 8 + ny, :] = q[:, cols]
-                for side, base in ((0, 5), (1, 8 + ny)):
-                    ps[h, base : base + 3, :] = ph[side, i * xb + x, :3, cols]
-                    qs[h, base : base + 3, :] = qh[side, i * xb + x, :3, cols]
             first_terms, second_terms = [], []
             for h in range(halves):
                 mp, kp = taps(lambda o: ps[h, 8 + o : 8 + o + ny, :])
@@ -296,27 +340,92 @@
             both = split(join(first_terms + second_terms, 1))
             out[x] = r_ref[x] - dot3(both, (bh[...], bl[...]), NN)
 
-    field = pl.BlockSpec((xb, ny, nz), lambda i: (i, 0, 0))
+    if outer:
+        at = lambda i: i * (steps - 1)
+        count = 2
+    else:
+        at = lambda i: i + 1
+        count = steps - 2
+
+    def block(shift):
+        return pl.BlockSpec(
+            (xb, ny, nz),
+            lambda i: (jnp.clip(at(i) + shift, 0, steps - 1), 0, 0),
+        )
+
+    extra = list(halos) if outer else []
     return pl.pallas_call(
         kernel,
-        grid=(steps,),
-        in_specs=[whole(b.shape) for b in bands]
-        + [whole(x_low.shape)] * 2
-        + [whole(y_low.shape)] * 2
-        + [
-            pl.BlockSpec((xb, ny, nz), lambda i: (jnp.maximum(i - 1, 0), 0, 0)),
-            field,
-            pl.BlockSpec((xb, ny, nz), lambda i: (jnp.minimum(i + 1, steps - 1), 0, 0)),
-            field,
-        ],
+        grid=(count,),
+        in_specs=[pl.BlockSpec(memory_space=pl.ANY)]
+        + [whole(b.shape) for b in bands]
+        + ([pl.BlockSpec(memory_space=pltpu.SMEM)] if outer else [])
+        + [whole(e.shape) for e in extra[1:]]
+        + [block(-1), block(0), block(1), block(0)],
+        out_specs=block(0),
+        out_shape=jax.ShapeDtypeStruct((nx, ny, nz), F32),
+        scratch_shapes=[pltpu.VMEM((xb + 6, ny, nz), F32)]
+        + [pltpu.VMEM((halves, ny + 16, 128), F32)] * 2,
+        input_output_aliases={0: 0} if outer else {},
+        compiler_params=params(1),
+        cost_estimate=cost(12 * count * xb * ny * nz * nz, 12 * count * xb * ny * nz),
+        name="stencil_outer" if outer else "stencil_inner",
+    )(weighted if after is None else after, *bands, *extra, weighted, weighted, weighted, residual)
+
+
+def stencil_sides(partial, where, bands, edges, corners):
+    nx, ny, nz = partial.shape
+
+    rows, cols = lax.axis_size("row"), lax.axis_size("col")
+
+    def kernel(where_ref, bh, bl, ea, ec, ca, cc, r_ref, out, ext, ph, qh):
+        me, mine = where_ref[0], where_ref[1]
+        for side in range(2):
+
+            @pl.when(pl.program_id(0) == side)
+            def _():
+                ph[...] = jnp.zeros_like(ph)
+                qh[...] = jnp.zeros_like(qh)
+                base = 5 if side == 0 else 16
+                near = mine % 2 == 1 - side
+                pick = jnp.where(near, 0, 1)
+                border = mine == (0 if side == 0 else cols - 1)
+                for j in range(3):
+                    edge = jnp.where(near, ea[j], ec[j])
+                    even = me % 2 == 0
+                    low = jnp.where(even, cc[pick, j], ca[pick, j])
+                    high = jnp.where(even, ca[pick, j], cc[pick, j])
+                    ext[:8] = jnp.where(border | (me == 0), 0.0, low)
+                    ext[8 : 8 + nx] = jnp.where(border, 0.0, edge)
+                    ext[8 + nx :] = jnp.where(border | (me == rows - 1), 0.0, high)
+                    p, q = taps(lambda o: ext[8 + o : 8 + o + nx, :])
+                    ph[:, base + j, :] = p
+                    qh[:, base + j, :] = q
+
+        mp, kp = taps(lambda o: ph[:, 8 + o : 16 + o, :])
+        (mq,) = taps(lambda o: qh[:, 8 + o : 16 + o, :], stiff=False)
+        both = split(jnp.concatenate([kp + mq, mp], 2).reshape(nx * 8, 2 * nz))
+        image = dot3(both, (bh[...], bl[...]), NN)
+        out[...] = r_ref[...] - image.reshape(nx, 8, nz)
+
+    field = pl.BlockSpec((nx, 8, nz), lambda i: (0, i * (ny // 8 - 1), 0))
+    return pl.pallas_call(
+        kernel,
+        grid=(2,),
+        in_specs=[pl.BlockSpec(memory_space=pltpu.SMEM)]
+        + [whole(b.shape) for b in bands]
+        + [whole(e.shape) for e in edges]
+        + [whole(c.shape) for c in corners]
+        + [field],
         out_specs=field,
         out_shape=jax.ShapeDtypeStruct((nx, ny, nz), F32),
-        scratch_shapes=[pltpu.VMEM((halves, ny + 16, 128), F32)] * 2
-        + [pltpu.VMEM((2, nx, 8, nz), F32)] * 2,
+        scratch_shapes=[pltpu.VMEM((nx + 16, nz), F32)]
+        + [pltpu.VMEM((nx, 24, nz), F32)] * 2,
+        input_output_aliases={7: 0},
         compiler_params=params(1),
-        cost_estimate=cost(12 * nx * ny * nz * nz, 12 * nx * ny * nz),
-        name="stencil",
-    )(*bands, x_low, x_high, y_low, y_high, weighted, weighted, weighted, residual)
+        cost_estimate=cost(12 * nx * 16 * nz * nz, 128 * nx * nz),
+        name="stencil_sides",
+    )(where, *bands, *edges, *corners, partial)
 
 
 def exchange(pieces, axis):
@@ -327,11 +436,12 @@
     return out
 
 
-def neighbours(low, high, axis):
+def swap(array, axis, near):
     n = lax.axis_size(axis)
-    up = [(i, i + 1) for i in range(n - 1)]
-    down = [(i + 1, i) for i in range(n - 1)]
-    return lax.ppermute(high, axis, up), lax.ppermute(low, axis, down)
+    other = [i ^ 1 if near else (i + 1 if i % 2 else i - 1) for i in range(n)]
+    return lax.ppermute(
+        array, axis, [(i, j if 0 <= j < n else i) for i, j in enumerate(other)]
+    )
 
 
 def schedule(chunks):
@@ -402,14 +512,19 @@
             back[k] = exchange(out, "row")
         if stage != "z":
             last = out[0]
-    adjoint_next, weighted = backward_z(back, basis_zt, where, adjoint, coefficient)
-    x_low, x_high = neighbours(weighted[:3], weighted[-3:], "row")
-    edge_low = jnp.concatenate([x_low[:, :3], weighted[:, :3], x_high[:, :3]], 0)
-    edge_high = jnp.concatenate([x_low[:, -3:], weighted[:, -3:], x_high[:, -3:]], 0)
-    y_low, y_high = neighbours(
-        edge_low.transpose(1, 0, 2), edge_high.transpose(1, 0, 2), "col"
-    )
-    residual_next = stencil(weighted, residual, x_low, x_high, y_low, y_high, bands)
+    adjoint_next, weighted, xa, xc, ea, ec = backward_z(
+        back, basis_zt, where, adjoint, coefficient
+    )
+    ea, ec = swap(ea, "col", True), swap(ec, "col", False)
+    xa, xc = swap(xa, "row", True), swap(xc, "row", False)
+    inner = stencil(weighted, residual, bands)
+    sides, _ = lax.optimization_barrier((jnp.stack([ea, ec]), inner))
+    low, high = sides[:, :, :8], sides[:, :, -8:]
+    even = ri % 2 == 0
+    ca = swap(jnp.where(even, high, low), "row", True)
+    cc = swap(jnp.where(even, low, high), "row", False)
+    outer = stencil(weighted, residual, bands, (where, xa, xc), inner)
+    residual_next = stencil_sides(outer, where, bands, (ea, ec), (ca, cc))
     return adjoint_next, residual_next
 
 

time: 561 us -> 546 us (0.973)
  Pallas kernels: 153 us -> 169 us
  local copies, waits for them, and re-layouts: 24.9 us -> 15.8 us
  waiting for transfers between devices: 236 us -> 227 us
  starting transfers between devices: 137 us -> 129 us
    ppermute x4 -> x6, waiting for transfers between devices: 23.7 us -> 0.02 us  [swap(): lax.ppermute(array, axis, [(i, j if 0 <= j < n else i) for i, j in enumer...]
    pallas_call x1 -> x3, Pallas kernels: 28.6 us -> 48.8 us  [the longest x2 41.4 us: stencil(): pl.pallas_call(kernel, grid=(count,), in_specs=[pl.BlockSpec(memory_space...]
    ppermute x80, waiting for transfers between devices: 212 us -> 227 us  [exchange(): out[d] = lax.ppermute(pieces[d], axis, [(i, i ^ d) for i in range(n)])]
    ppermute x80, starting transfers between devices: 127 us -> 117 us  [exchange(): out[d] = lax.ppermute(pieces[d], axis, [(i, i ^ d) for i in range(n)])]
    pallas_call x1 -> x0, local copies, waits for them, and re-layouts: 8.31 us -> none  [backward_z(): pl.pallas_call(kernel, grid_spec=pltpu.PrefetchScalarGridSpec(num_scalar_...]
    ppermute x4 -> x6, starting transfers between devices: 10.3 us -> 12.2 us  [swap(): lax.ppermute(array, axis, [(i, j if 0 <= j < n else i) for i, j in enumer...]
  transfers between devices with their start and end apart: 84 -> 86, of which waited for: 38 -> 35; matrix products, arithmetic and copies ran while one was open for 2% -> 2% of each run, Pallas kernels for 18% -> 25%
where the time goes in v2:
time: 546 us; the launch traced here: 543 us
  waiting for transfers between devices  227 us (42%)
  Pallas kernels  169 us (31%)
  starting transfers between devices  129 us (24%)
  local copies, waits for them, and re-layouts  15.8 us (3%)
    ppermute x80, waiting for transfers between devices, exchange(): out[d] = lax.ppermute(pieces[d], axis, [(i, i ^ d) for i in range(n)])  227 us
    ppermute x80, starting transfers between devices, exchange(): out[d] = lax.ppermute(pieces[d], axis, [(i, i ^ d) for i in range(n)])  117 us
    pallas_call x2, Pallas kernels, stencil(): pl.pallas_call(kernel, grid=(count,), in_specs=[pl.BlockSpec(memory_space...  41.4 us
    pallas_call x4, Pallas kernels, middle_y(): pl.pallas_call(kernel, grid=(part // cb,), out_shape=[jax.ShapeDtypeStruc...  29.7 us
    pallas_call x4, Pallas kernels, backward_x(): pl.pallas_call(kernel, out_shape=[jax.ShapeDtypeStruct((nx, part, ny), F3...  26 us
    pallas_call x4, Pallas kernels, forward_x(): pl.pallas_call(kernel, out_shape=[jax.ShapeDtypeStruct((part, wide, ny),...  25.9 us
    pallas_call x2, Pallas kernels, forward_z(): pl.pallas_call(kernel, grid_spec=pltpu.PrefetchScalarGridSpec(num_scalar_...  21.5 us
    pallas_call x1, Pallas kernels, backward_z(): pl.pallas_call(kernel, grid_spec=pltpu.PrefetchScalarGridSpec(num_scalar_...  17.4 us
  transfers between devices with their start and end apart: 86, of which 35 were waited for; matrix products, arithmetic and copies ran while one was open for 2% of the time, Pallas kernels for 25%

profile of v2, /device:TPU:9, one launch (start us, length us, event | category | flops | bytes accessed | tf_op | source)
XLA Modules:
  0.0 543.3 jit_solution(8011627760038196118)
XLA Ops:
  3.2 10.1 %forward_z.3 = (f32[64,8,128]{2,1,0:T(8,128)}, f32[64,8,128]{2,1,0:T(8,128)}, f32[64,8,128]{2,1,0:T(8,128)}, f32[64,8,128]{2,1,0:T(8,128)}, f32[64,8,128]{2,1,0:...) custom-call(s32[2]{0:T(128)} %pad_add_fusion.where_ref.refs_0_, ...), custom_call_target="tpu_custom_call" | custom-call | flops 805306368 | bytes 8388608 | tf_op jit(solution)/shard_map/forward_z/pallas_call | solution.py:93
  19.8 11.4 %forward_z.2 = (f32[64,8,128]{2,1,0:T(8,128)}, f32[64,8,128]{2,1,0:T(8,128)}, f32[64,8,128]{2,1,0:T(8,128)}, f32[64,8,128]{2,1,0:T(8,128)}, f32[64,8,128]{2,1,0:...) custom-call(s32[2]{0:T(128)} %pad_add_fusion.where_ref.refs_0_, ...), custom_call_target="tpu_custom_call" | custom-call | flops 2415919104 | bytes 8388608 | tf_op jit(solution)/shard_map/forward_z/pallas_call | solution.py:93
  49.7 8.4 %collective-permute-done.5.refs_6_ = f32[64,8,128]{2,1,0:T(8,128)} collective-permute-done((f32[64,8,128]{2,1,0:T(8,128)}, f32[64,8,128]{2,1,0:T(8,128)}, u32[]{:S(2)}, u32[]{:S(2)}) %collective-permute-start.5) | collective-permute-done | bytes 262176 | tf_op jit(solution)/shard_map/ppermute | solution.py:435
  58.1 11.7 %collective-permute-done.6.refs_7_ = f32[64,8,128]{2,1,0:T(8,128)} collective-permute-done((f32[64,8,128]{2,1,0:T(8,128)}, f32[64,8,128]{2,1,0:T(8,128)}, u32[]{:S(2)}, u32[]{:S(2)}) %collective-permute-start.6) | collective-permute-done | bytes 262176 | tf_op jit(solution)/shard_map/ppermute | solution.py:435
  79.5 11.1 %collective-permute-start.7 = (f32[8,128,128]{2,1,0:T(8,128)}, f32[8,128,128]{2,1,0:T(8,128)}, u32[]{:S(2)}, u32[]{:S(2)}) collective-permute-start(f32[8,128,128]{2,1,0:T(8,128)} %get-tuple-element.115), channel_id=1, source_target_pairs={{0,1},{1,0},{2,3},{3,2},{4,5},{5,4},{6,7},{7,6},{8,9},{9,8},{10,11... | collective-permute-start | bytes 1572872 | tf_op jit(solution)/shard_map/ppermute | solution.py:435
  120.9 7.4 %middle_y.4 = (f32[8,128,128]{2,1,0:T(8,128)}, f32[8,128,128]{2,1,0:T(8,128)}, f32[8,128,128]{2,1,0:T(8,128)}, f32[8,128,128]{2,1,0:T(8,128)}) custom-call(f32[8,128,128]{2,1,0:T(8,128)} %get-tuple-element.114._.refs_0_, bf16[512,512]{1,0:T(8,128)(2,1)} %copy.117.bh, bf16[512,512]{1,0:T(8,128)(2,1)} %copy.118.bl, bf16[512,512]{1,0:T(8,128)(2,1)} %bitcast.28, ...), custom_call_target="tpu_custom_call" | custom-call | flops 3221225472 | bytes 4194304 | tf_op jit(solution)/shard_map/middle_y/pallas_call | solution.py:162
  132.8 18.3 %collective-permute-done.31.refs_5_ = f32[64,8,128]{2,1,0:T(8,128)S(1)} collective-permute-done((f32[64,8,128]{2,1,0:T(8,128)}, f32[64,8,128]{2,1,0:T(8,128)S(1)}, u32[]{:S(2)}, u32[]{:S(2)}) %collective-permute-start.31) | collective-permute-done | bytes 262176 | tf_op jit(solution)/shard_map/ppermute | solution.py:435
  164.7 6.5 %collective-permute-done.37.refs_1_ = f32[64,8,128]{2,1,0:T(8,128)S(1)} collective-permute-done((f32[64,8,128]{2,1,0:T(8,128)}, f32[64,8,128]{2,1,0:T(8,128)S(1)}, u32[]{:S(2)}, u32[]{:S(2)}) %collective-permute-start.37) | collective-permute-done | bytes 262176 | tf_op jit(solution)/shard_map/ppermute | solution.py:435
  183.8 20.3 %collective-permute-start.14 = (f32[64,8,128]{2,1,0:T(8,128)}, f32[64,8,128]{2,1,0:T(8,128)S(1)}, u32[]{:S(2)}, u32[]{:S(2)}) collective-permute-start(f32[64,8,128]{2,1,0:T(8,128)} %get-tuple-element.124), channel_id=1, source_target_pairs={{0,8},{4,12},{8,0},{12,4},{16,24},{20,28},{24,16},{28,20},{1,9},{5... | collective-permute-start | bytes 786440 | tf_op jit(solution)/shard_map/ppermute | solution.py:435
  243.3 7.4 %middle_y.5 = (f32[8,128,128]{2,1,0:T(8,128)}, f32[8,128,128]{2,1,0:T(8,128)}, f32[8,128,128]{2,1,0:T(8,128)}, f32[8,128,128]{2,1,0:T(8,128)}) custom-call(f32[8,128,128]{2,1,0:T(8,128)} %get-tuple-element.147._.refs_0_, bf16[512,512]{1,0:T(8,128)(2,1)} %copy.117.bh, bf16[512,512]{1,0:T(8,128)(2,1)} %copy.118.bl, bf16[512,512]{1,0:T(8,128)(2,1)} %bitcast.29, ...), custom_call_target="tpu_custom_call" | custom-call | flops 3221225472 | bytes 4194304 | tf_op jit(solution)/shard_map/middle_y/pallas_call | solution.py:162
  273.3 7.3 %middle_y.6 = (f32[8,128,128]{2,1,0:T(8,128)}, f32[8,128,128]{2,1,0:T(8,128)}, f32[8,128,128]{2,1,0:T(8,128)}, f32[8,128,128]{2,1,0:T(8,128)}) custom-call(f32[8,128,128]{2,1,0:T(8,128)} %get-tuple-element.159._.refs_0_, bf16[512,512]{1,0:T(8,128)(2,1)} %copy.117.bh, bf16[512,512]{1,0:T(8,128)(2,1)} %copy.118.bl, bf16[512,512]{1,0:T(8,128)(2,1)} %bitcast.30, ...), custom_call_target="tpu_custom_call" | custom-call | flops 3221225472 | bytes 4194304 | tf_op jit(solution)/shard_map/middle_y/pallas_call | solution.py:162
  299.1 12.3 %collective-permute-done.59.refs_3_ = f32[8,128,128]{2,1,0:T(8,128)} collective-permute-done((f32[8,128,128]{2,1,0:T(8,128)}, f32[8,128,128]{2,1,0:T(8,128)}, u32[]{:S(2)}, u32[]{:S(2)}) %collective-permute-start.59) | collective-permute-done | bytes 524320 | tf_op jit(solution)/shard_map/ppermute | solution.py:435
  313.3 7.9 %collective-permute-done.61.refs_2_ = f32[8,128,128]{2,1,0:T(8,128)S(1)} collective-permute-done((f32[8,128,128]{2,1,0:T(8,128)}, f32[8,128,128]{2,1,0:T(8,128)S(1)}, u32[]{:S(2)}, u32[]{:S(2)}) %collective-permute-start.61) | collective-permute-done | bytes 524320 | tf_op jit(solution)/shard_map/ppermute | solution.py:435
  321.2 7.6 %middle_y.7 = (f32[8,128,128]{2,1,0:T(8,128)}, f32[8,128,128]{2,1,0:T(8,128)}, f32[8,128,128]{2,1,0:T(8,128)}, f32[8,128,128]{2,1,0:T(8,128)}) custom-call(f32[64,8,128]{2,1,0:T(8,128)} %get-tuple-element.167._.refs_8_, bf16[512,512]{1,0:T(8,128)(2,1)} %copy.117.bh, bf16[512,512]{1,0:T(8,128)(2,1)} %copy.118.bl, bf16[512,512]{1,0:T(8,128)(2,1)} %bitcast.31, ...), custom_call_target="tpu_custom_call" | custom-call | flops 3221225472 | bytes 4194304 | tf_op jit(solution)/shard_map/middle_y/pallas_call | solution.py:162
  336.4 6.6 %backward_x.6 = (f32[64,8,128]{2,1,0:T(8,128)}, f32[64,8,128]{2,1,0:T(8,128)}, f32[64,8,128]{2,1,0:T(8,128)}, f32[64,8,128]{2,1,0:T(8,128)}, f32[64,8,128]{2,1,0...) custom-call(f32[8,128,128]{2,1,0:T(8,128)} %get-tuple-element.178._.refs_0_, ...), custom_call_target="tpu_custom_call" | custom-call | flops 1610612736 | bytes 4194304 | tf_op jit(solution)/shard_map/backward_x/pallas_call | solution.py:196
  343.1 9.2 %collective-permute-done.54.refs_13_ = f32[64,8,128]{2,1,0:T(8,128)S(1)} collective-permute-done((f32[64,8,128]{2,1,0:T(8,128)S(1)}, f32[64,8,128]{2,1,0:T(8,128)S(1)}, u32[]{:S(2)}, u32[]{:S(2)}) %collective-permute-start.54) | collective-permute-done | bytes 262176 | tf_op jit(solution)/shard_map/ppermute | solution.py:435
  353.9 11.2 %collective-permute-done.55.refs_14_ = f32[64,8,128]{2,1,0:T(8,128)S(1)} collective-permute-done((f32[64,8,128]{2,1,0:T(8,128)S(1)}, f32[64,8,128]{2,1,0:T(8,128)S(1)}, u32[]{:S(2)}, u32[]{:S(2)}) %collective-permute-start.55) | collective-permute-done | bytes 262176 | tf_op jit(solution)/shard_map/ppermute | solution.py:435
  387.6 17.3 %collective-permute-done.67.refs_21_ = f32[64,8,128]{2,1,0:T(8,128)S(1)} collective-permute-done((f32[64,8,128]{2,1,0:T(8,128)}, f32[64,8,128]{2,1,0:T(8,128)S(1)}, u32[]{:S(2)}, u32[]{:S(2)}) %collective-permute-start.67) | collective-permute-done | bytes 262176 | tf_op jit(solution)/shard_map/ppermute | solution.py:435
  410.8 11.8 %collective-permute-done.69.refs_23_ = f32[64,8,128]{2,1,0:T(8,128)} collective-permute-done((f32[64,8,128]{2,1,0:T(8,128)}, f32[64,8,128]{2,1,0:T(8,128)}, u32[]{:S(2)}, u32[]{:S(2)}) %collective-permute-start.69) | collective-permute-done | bytes 262176 | tf_op jit(solution)/shard_map/ppermute | solution.py:435
  425.5 19.1 %collective-permute-done.76.refs_28_ = f32[64,8,128]{2,1,0:T(8,128)} collective-permute-done((f32[64,8,128]{2,1,0:T(8,128)}, f32[64,8,128]{2,1,0:T(8,128)}, u32[]{:S(2)}, u32[]{:S(2)}) %collective-permute-start.76) | collective-permute-done | bytes 262176 | tf_op jit(solution)/shard_map/ppermute | solution.py:435
  462.1 17.4 %backward_z.1 = (f32[64,128,256]{2,1,0:T(8,128)}, f32[64,128,256]{2,1,0:T(8,128)}, f32[3,128,256]{2,1,0:T(8,128)}, f32[3,128,256]{2,1,0:T(8,128)}, f32[3,64,256]{2,1,0:T(8,128)}, /*index=5*/f32[3,64,256]{2,1,0:T(8,128)}) custom-call(s32[2]{0:T(128)} %pad_add_fusion.where_ref.refs_0_, f32[256,256]{1,0:T(8,128)} %bitcast.21, f32[64,128,256]{2,1,0:T(8,128)} %adj_ref.1, ...), custom_call_target="tpu_custom_call" | custom-call | flops 3221225472 | bytes 46137344 | tf_op jit(solution)/shard_map/backward_z/pallas_call | solution.py:255
  487.0 29.0 %stencil_inner.1._ = f32[64,128,256]{2,1,0:T(8,128)} custom-call(f32[64,128,256]{2,1,0:T(8,128)} %get-tuple-element.204._.refs_0_.refs_1_.refs_2_.refs_3_.refs_4_.refs_5_, bf16[512,256]{1,0:T(8,128)(2,1)} %constant.46.bh, bf16[512,256]{1,0:T(8,128)(2,1)} %constant.48.bl, f32[64,128,256]{2,1,0:T(8,128)} %get-tuple-element.204._.refs_0_.refs_1_.refs_2_.refs_3_.refs_4_.refs_5_, ...), custom_call_target="tpu_custom_call" | custom-call | flops 4831838208 | bytes 18874368 | tf_op jit(solution)/shard_map/stencil_inner/pallas_call | solution.py:357
  522.2 12.4 %stencil_outer.1.r_ref = f32[64,128,256]{2,1,0:T(8,128)} custom-call(f32[64,128,256]{2,1,0:T(8,128)} %stencil_inner.1._, bf16[512,256]{1,0:T(8,128)(2,1)} %constant.46.bh, bf16[512,256]{1,0:T(8,128)(2,1)} %constant.48.bl, s32[2]{0:T(128)} %pad_add_fusion.where_ref.refs_0_, f32[3,128,256]{2,1,0:T(8,128)} %copy-done.8, ...), custom_call_target="tpu_custom_call", output_to_operand_aliasing={{}: (0, {})} | custom-call | flops 1610612736 | bytes 6291456 | tf_op jit(solution)/shard_map/stencil_outer/pallas_call | solution.py:357
  535.9 7.4 %stencil_sides.1 = f32[64,128,256]{2,1,0:T(8,128)} custom-call(s32[2]{0:T(128)} %pad_add_fusion.where_ref.refs_0_, bf16[512,256]{1,0:T(8,128)(2,1)} %constant.46.bh, bf16[512,256]{1,0:T(8,128)(2,1)} %constant.48.bl, f32[3,64,256]{2,1,0:T(8,128)} %copy-done.6, f32[3,64,256]{2,1,0:T(8,128)} %copy-done.7, ...), custom_call_target="tpu_custom_call", output_to_operand_aliasing={{}: (7, {})} | custom-call | flops 805306368 | bytes 2097152 | tf_op jit(solution)/shard_map/stencil_sides/pallas_call | solution.py:412
  (341 shorter events, 252.6 us)
Async XLA Ops:
  32.5 37.3 %collective-permute-start.6 = (f32[64,8,128]{2,1,0:T(8,128)}, f32[64,8,128]{2,1,0:T(8,128)}, u32[]{:S(2)}, u32[]{:S(2)}) collective-permute-start(f32[64,8,128]{2,1,0:T(8,128)} %get-tuple-element.113), channel_id=1, source_target_pairs={{0,28},{4,24},{8,20},{12,16},{16,12},{20,8},{24,4},{28,0},{1,29},{... | collective-permute-start | bytes 786440 | tf_op jit(solution)/shard_map/ppermute | solution.py:435
  69.9 34.4 %collective-permute-start.25 = (f32[64,8,128]{2,1,0:T(8,128)}, f32[64,8,128]{2,1,0:T(8,128)S(1)}, u32[]{:S(2)}, u32[]{:S(2)}) collective-permute-start(f32[64,8,128]{2,1,0:T(8,128)} %get-tuple-element.136), channel_id=1, source_target_pairs={{0,24},{4,28},{8,16},{12,20},{16,8},{20,12},{24,0},{28,4},{1,25},{... | collective-permute-start | bytes 786440 | tf_op jit(solution)/shard_map/ppermute | solution.py:435
  70.0 39.1 %collective-permute-start.26 = (f32[64,8,128]{2,1,0:T(8,128)}, f32[64,8,128]{2,1,0:T(8,128)S(1)}, u32[]{:S(2)}, u32[]{:S(2)}) collective-permute-start(f32[64,8,128]{2,1,0:T(8,128)} %get-tuple-element.137), channel_id=1, source_target_pairs={{0,28},{4,24},{8,20},{12,16},{16,12},{20,8},{24,4},{28,0},{1,29},{... | collective-permute-start | bytes 786440 | tf_op jit(solution)/shard_map/ppermute | solution.py:435
  79.5 38.6 %collective-permute-start.7 = (f32[8,128,128]{2,1,0:T(8,128)}, f32[8,128,128]{2,1,0:T(8,128)}, u32[]{:S(2)}, u32[]{:S(2)}) collective-permute-start(f32[8,128,128]{2,1,0:T(8,128)} %get-tuple-element.115), channel_id=1, source_target_pairs={{0,1},{1,0},{2,3},{3,2},{4,5},{5,4},{6,7},{7,6},{8,9},{9,8},{10,11... | collective-permute-start | bytes 1572872 | tf_op jit(solution)/shard_map/ppermute | solution.py:435
  120.8 38.0 %collective-permute-start.32 = (f32[64,8,128]{2,1,0:T(8,128)}, f32[64,8,128]{2,1,0:T(8,128)S(1)}, u32[]{:S(2)}, u32[]{:S(2)}) collective-permute-start(f32[64,8,128]{2,1,0:T(8,128)} %get-tuple-element.145), channel_id=1, source_target_pairs={{0,24},{4,28},{8,16},{12,20},{16,8},{20,12},{24,0},{28,4},{1,25},{... | collective-permute-start | bytes 786440 | tf_op jit(solution)/shard_map/ppermute | solution.py:435
  120.8 43.9 %collective-permute-start.33 = (f32[64,8,128]{2,1,0:T(8,128)}, f32[64,8,128]{2,1,0:T(8,128)S(1)}, u32[]{:S(2)}, u32[]{:S(2)}) collective-permute-start(f32[64,8,128]{2,1,0:T(8,128)} %get-tuple-element.146), channel_id=1, source_target_pairs={{0,28},{4,24},{8,20},{12,16},{16,12},{20,8},{24,4},{28,0},{1,29},{... | collective-permute-start | bytes 786440 | tf_op jit(solution)/shard_map/ppermute | solution.py:435
  128.3 44.2 %collective-permute-start.10 = (f32[8,128,128]{2,1,0:T(8,128)}, f32[8,128,128]{2,1,0:T(8,128)S(1)}, u32[]{:S(2)}, u32[]{:S(2)}) collective-permute-start(f32[8,128,128]{2,1,0:T(8,128)} %get-tuple-element.119), channel_id=1, source_target_pairs={{0,1},{1,0},{2,3},{3,2},{4,5},{5,4},{6,7},{7,6},{8,9},{9,8},{10,11... | collective-permute-start | bytes 1572872 | tf_op jit(solution)/shard_map/ppermute | solution.py:435
  131.6 42.8 %collective-permute-start.11 = (f32[8,128,128]{2,1,0:T(8,128)}, f32[8,128,128]{2,1,0:T(8,128)S(1)}, u32[]{:S(2)}, u32[]{:S(2)}) collective-permute-start(f32[8,128,128]{2,1,0:T(8,128)} %get-tuple-element.120), channel_id=1, source_target_pairs={{0,2},{1,3},{2,0},{3,1},{4,6},{5,7},{6,4},{7,5},{8,10},{9,11},{10,... | collective-permute-start | bytes 1572872 | tf_op jit(solution)/shard_map/ppermute | solution.py:435
  172.6 38.1 %collective-permute-start.41 = (f32[64,8,128]{2,1,0:T(8,128)}, f32[64,8,128]{2,1,0:T(8,128)S(1)}, u32[]{:S(2)}, u32[]{:S(2)}) collective-permute-start(f32[64,8,128]{2,1,0:T(8,128)} %get-tuple-element.156), channel_id=1, source_target_pairs={{0,20},{4,16},{8,28},{12,24},{16,4},{20,0},{24,12},{28,8},{1,21},{... | collective-permute-start | bytes 786440 | tf_op jit(solution)/shard_map/ppermute | solution.py:435
  174.4 39.8 %collective-permute-start.42 = (f32[64,8,128]{2,1,0:T(8,128)}, f32[64,8,128]{2,1,0:T(8,128)S(1)}, u32[]{:S(2)}, u32[]{:S(2)}) collective-permute-start(f32[64,8,128]{2,1,0:T(8,128)} %get-tuple-element.157), channel_id=1, source_target_pairs={{0,24},{4,28},{8,16},{12,20},{16,8},{20,12},{24,0},{28,4},{1,25},{... | collective-permute-start | bytes 786440 | tf_op jit(solution)/shard_map/ppermute | solution.py:435
  174.9 44.9 %collective-permute-start.43 = (f32[64,8,128]{2,1,0:T(8,128)S(1)}, f32[64,8,128]{2,1,0:T(8,128)S(1)}, u32[]{:S(2)}, u32[]{:S(2)}) collective-permute-start(f32[64,8,128]{2,1,0:T(8,128)S(1)} %copy-done.47), channel_id=1, source_target_pairs={{0,28},{4,24},{8,20},{12,16},{16,12},{20,8},{24,4},{28,0},{1,29},{... | collective-permute-start | bytes 786440 | tf_op jit(solution)/shard_map/ppermute | solution.py:435
  182.6 40.2 %collective-permute-start.13 = (f32[64,8,128]{2,1,0:T(8,128)}, f32[64,8,128]{2,1,0:T(8,128)S(1)}, u32[]{:S(2)}, u32[]{:S(2)}) collective-permute-start(f32[64,8,128]{2,1,0:T(8,128)} %get-tuple-element.123), channel_id=1, source_target_pairs={{0,4},{4,0},{8,12},{12,8},{16,20},{20,16},{24,28},{28,24},{1,5},{5... | collective-permute-start | bytes 786440 | tf_op jit(solution)/shard_map/ppermute | solution.py:435
  183.8 39.1 %collective-permute-start.14 = (f32[64,8,128]{2,1,0:T(8,128)}, f32[64,8,128]{2,1,0:T(8,128)S(1)}, u32[]{:S(2)}, u32[]{:S(2)}) collective-permute-start(f32[64,8,128]{2,1,0:T(8,128)} %get-tuple-element.124), channel_id=1, source_target_pairs={{0,8},{4,12},{8,0},{12,4},{16,24},{20,28},{24,16},{28,20},{1,9},{5... | collective-permute-start | bytes 786440 | tf_op jit(solution)/shard_map/ppermute | solution.py:435
  289.8 43.3 %collective-permute-start.62 = (f32[8,128,128]{2,1,0:T(8,128)}, f32[8,128,128]{2,1,0:T(8,128)}, u32[]{:S(2)}, u32[]{:S(2)}) collective-permute-start(f32[8,128,128]{2,1,0:T(8,128)} %get-tuple-element.181), channel_id=1, source_target_pairs={{0,3},{1,2},{2,1},{3,0},{4,7},{5,6},{6,5},{7,4},{8,11},{9,10},{10,... | collective-permute-start | bytes 1572872 | tf_op jit(solution)/shard_map/ppermute | solution.py:435
  298.7 34.4 %collective-permute-start.50 = (f32[64,8,128]{2,1,0:T(8,128)}, f32[64,8,128]{2,1,0:T(8,128)S(1)}, u32[]{:S(2)}, u32[]{:S(2)}) collective-permute-start(f32[64,8,128]{2,1,0:T(8,128)} %get-tuple-element.168), channel_id=1, source_target_pairs={{0,4},{4,0},{8,12},{12,8},{16,20},{20,16},{24,28},{28,24},{1,5},{5... | collective-permute-start | bytes 786440 | tf_op jit(solution)/shard_map/ppermute | solution.py:435
  383.6 39.0 %collective-permute-start.69 = (f32[64,8,128]{2,1,0:T(8,128)}, f32[64,8,128]{2,1,0:T(8,128)}, u32[]{:S(2)}, u32[]{:S(2)}) collective-permute-start(f32[64,8,128]{2,1,0:T(8,128)} %get-tuple-element.189), channel_id=1, source_target_pairs={{0,28},{4,24},{8,20},{12,16},{16,12},{20,8},{24,4},{28,0},{1,29},{... | collective-permute-start | bytes 786440 | tf_op jit(solution)/shard_map/ppermute | solution.py:435
  384.8 37.9 %collective-permute-start.73 = (f32[64,8,128]{2,1,0:T(8,128)}, f32[64,8,128]{2,1,0:T(8,128)}, u32[]{:S(2)}, u32[]{:S(2)}) collective-permute-start(f32[64,8,128]{2,1,0:T(8,128)} %get-tuple-element.194), channel_id=1, source_target_pairs={{0,4},{4,0},{8,12},{12,8},{16,20},{20,16},{24,28},{28,24},{1,5},{5... | collective-permute-start | bytes 786440 | tf_op jit(solution)/shard_map/ppermute | solution.py:435
  385.6 38.1 %collective-permute-start.74 = (f32[64,8,128]{2,1,0:T(8,128)}, f32[64,8,128]{2,1,0:T(8,128)}, u32[]{:S(2)}, u32[]{:S(2)}) collective-permute-start(f32[64,8,128]{2,1,0:T(8,128)} %get-tuple-element.195), channel_id=1, source_target_pairs={{0,8},{4,12},{8,0},{12,4},{16,24},{20,28},{24,16},{28,20},{1,9},{5... | collective-permute-start | bytes 786440 | tf_op jit(solution)/shard_map/ppermute | solution.py:435
  410.8 33.8 %collective-permute-start.76 = (f32[64,8,128]{2,1,0:T(8,128)}, f32[64,8,128]{2,1,0:T(8,128)}, u32[]{:S(2)}, u32[]{:S(2)}) collective-permute-start(f32[64,8,128]{2,1,0:T(8,128)} %get-tuple-element.197), channel_id=1, source_target_pairs={{0,16},{4,20},{8,24},{12,28},{16,0},{20,4},{24,8},{28,12},{1,17},{... | collective-permute-start | bytes 786440 | tf_op jit(solution)/shard_map/ppermute | solution.py:435
  423.7 38.3 %collective-permute-start.79 = (f32[64,8,128]{2,1,0:T(8,128)}, f32[64,8,128]{2,1,0:T(8,128)}, u32[]{:S(2)}, u32[]{:S(2)}) collective-permute-start(f32[64,8,128]{2,1,0:T(8,128)} %get-tuple-element.200), channel_id=1, source_target_pairs={{0,28},{4,24},{8,20},{12,16},{16,12},{20,8},{24,4},{28,0},{1,29},{... | collective-permute-start | bytes 786440 | tf_op jit(solution)/shard_map/ppermute | solution.py:435
  479.5 36.5 %collective-permute-start.80 = (f32[3,64,256]{2,1,0:T(8,128)}, f32[3,64,256]{2,1,0:T(8,128)S(1)}, u32[]{:S(2)}, u32[]{:S(2)}) collective-permute-start(f32[3,64,256]{2,1,0:T(8,128)} %get-tuple-element.202), channel_id=1, source_target_pairs={{0,1},{1,0},{2,3},{3,2},{4,5},{5,4},{6,7},{7,6},{8,9},{9,8},{10,11... | collective-permute-start | bytes 589832 | tf_op jit(solution)/shard_map/ppermute | solution.py:442
  481.5 34.5 %collective-permute-start.81 = (f32[3,64,256]{2,1,0:T(8,128)}, f32[3,64,256]{2,1,0:T(8,128)S(1)}, u32[]{:S(2)}, u32[]{:S(2)}) collective-permute-start(f32[3,64,256]{2,1,0:T(8,128)} %get-tuple-element.203), channel_id=1, source_target_pairs={{0,0},{1,2},{2,1},{3,3},{4,4},{5,6},{6,5},{7,7},{8,8},{9,10},{10,9... | collective-permute-start | bytes 589832 | tf_op jit(solution)/shard_map/ppermute | solution.py:442
  484.2 36.5 %collective-permute-start.84 = (f32[3,128,256]{2,1,0:T(8,128)}, f32[3,128,256]{2,1,0:T(8,128)S(1)}, u32[]{:S(2)}, u32[]{:S(2)}) collective-permute-start(f32[3,128,256]{2,1,0:T(8,128)} %get-tuple-element.206), channel_id=1, source_target_pairs={{0,4},{4,0},{8,12},{12,8},{16,20},{20,16},{24,28},{28,24},{1,5},{5... | collective-permute-start | bytes 1179656 | tf_op jit(solution)/shard_map/ppermute | solution.py:442
  485.1 35.7 %collective-permute-start.85 = (f32[3,128,256]{2,1,0:T(8,128)}, f32[3,128,256]{2,1,0:T(8,128)S(1)}, u32[]{:S(2)}, u32[]{:S(2)}) collective-permute-start(f32[3,128,256]{2,1,0:T(8,128)} %get-tuple-element.207), channel_id=1, source_target_pairs={{0,0},{4,8},{8,4},{12,16},{16,12},{20,24},{24,20},{28,28},{1,1},{5... | collective-permute-start | bytes 1179656 | tf_op jit(solution)/shard_map/ppermute | solution.py:442
  (133 other events, 4093.5 us)

commit v3 on v2

--- a/solution.py
+++ b/solution.py
@@ -84,10 +84,12 @@
         ]
         basis = split(join(rows, 0))
 
-        for x in range(xb):
-            t = dot3(basis, split(r_ref[x]), NT)
-            for n, out in enumerate(outs):
-                out[x] = t[n * part : (n + 1) * part, :]
+        @pl.loop(0, xb // 4)
+        def _(step):
+            for x in (4 * step + u for u in range(4)):
+                t = dot3(basis, split(r_ref[x]), NT)
+                for n, out in enumerate(outs):
+                    out[x] = t[n * part : (n + 1) * part, :]
 
     count = len(chunks) * peers
     outs = pl.pallas_call(
@@ -174,10 +176,10 @@
     )(after, *by, *byt, shift, eigen_y, *pieces)
 
 
-def backward_x(pieces, bx, peers, after):
+def backward_x(pieces, bx, peers, after, cuts=1):
     part, wide, ny = pieces[0].shape
     full = wide * len(pieces)
-    nx = full // peers
+    nx = full // peers // cuts
 
     def kernel(_, bh, bl, *refs):
         ins, outs, v, w = refs[: len(pieces)], refs[len(pieces) : -2], refs[-2], refs[-1]
@@ -190,15 +192,16 @@
                 w[c] = t
 
         for c in range(part):
-            for d, out in enumerate(outs):
-                out[:, c, :] = w[c, d * nx : (d + 1) * nx, :]
+            for n, out in enumerate(outs):
+                at = (n % peers) * cuts + n // peers
+                out[:, c, :] = w[c, at * nx : (at + 1) * nx, :]
 
     return pl.pallas_call(
         kernel,
-        out_shape=[jax.ShapeDtypeStruct((nx, part, ny), F32)] * peers,
+        out_shape=[jax.ShapeDtypeStruct((nx, part, ny), F32)] * (peers * cuts),
         in_specs=[pl.BlockSpec(memory_space=pl.ANY)]
         + [pl.BlockSpec(memory_space=pltpu.VMEM)] * (2 + len(pieces)),
-        out_specs=[pl.BlockSpec(memory_space=pltpu.VMEM)] * peers,
+        out_specs=[pl.BlockSpec(memory_space=pltpu.VMEM)] * (peers * cuts),
         compiler_params=params(0),
         cost_estimate=cost(6 * full * full * part * ny, 8 * full * part * ny),
         scratch_shapes=[pltpu.VMEM((part, full, ny), F32)] * 2,
@@ -206,18 +209,22 @@
     )(after, *bx, *pieces)
 
 
-def backward_z(pieces, basis_zt, where, adjoint, coefficient):
+def backward_z(pieces, basis_zt, where, adjoint, coefficient, cut=0, cuts=1, before=()):
     nx, ny, nz = adjoint.shape
     peers, part = len(pieces[0]), pieces[0][0].shape[1]
     group = peers * part
     chunks = len(pieces)
     xb = 8
-    steps = nx // xb
+    steps = nx // xb // cuts
     flat = [p for chunk in pieces for p in chunk]
+    last = cut == cuts - 1
 
     def kernel(where_ref, b_ref, adj_ref, coef_ref, *refs):
-        ins, (next_ref, w_ref, *slabs_edges) = refs[: len(flat)], refs[len(flat) :]
-        slabs, edges = slabs_edges[:2], slabs_edges[2:]
+        if before:
+            low_ref, refs = refs[4], refs[6:]
+        ins, outs = refs[: len(flat)], refs[len(flat) :]
+        next_ref, w_ref = outs[:2]
+        edges, slabs = outs[2:4], outs[4:]
         me, i = where_ref[0], pl.program_id(0)
         rows = [
             b_ref[pl.ds(pl.multiple_of(k * group + (me ^ d) * part, part), part), :]
@@ -226,11 +233,13 @@
         ]
         basis = split(join(rows, 0))
 
-        for x in range(xb):
-            v = split(join([r[x] for r in ins], 0))
-            correction = dot3(v, basis, TN)
-            next_ref[x] = adj_ref[x] + correction
-            w_ref[x] = coef_ref[x].astype(F32) * correction
+        @pl.loop(0, xb // 4)
+        def _(step):
+            for x in (4 * step + u for u in range(4)):
+                v = split(join([r[x] for r in ins], 0))
+                correction = dot3(v, basis, TN)
+                next_ref[x] = adj_ref[x] + correction
+                w_ref[x] = coef_ref[x].astype(F32) * correction
 
         for n in range(2):
 
@@ -240,32 +249,47 @@
                     edges[n][j] = w_ref[:, ny - 3 + j, :]
                     edges[1 - n][j] = w_ref[:, j, :]
 
-            @pl.when((i == 0) & (me % 2 == n))
+            if last:
+
+                @pl.when((i == 0) & (me % 2 == n))
+                def _():
+                    slabs[1 - n][...] = low_ref[...] if before else w_ref[:3]
+
+                @pl.when((i == steps - 1) & (me % 2 == n))
+                def _():
+                    slabs[n][...] = w_ref[xb - 3 :]
+
+        if not last:
+
+            @pl.when(i == 0)
             def _():
-                slabs[1 - n][...] = w_ref[:3]
-
-            @pl.when((i == steps - 1) & (me % 2 == n))
-            def _():
-                slabs[n][...] = w_ref[xb - 3 :]
-
-    field = pl.BlockSpec((xb, ny, nz), lambda i, w: (i, 0, 0))
+                slabs[0][...] = w_ref[:3]
+
+    skip = cut * steps
+    field = pl.BlockSpec((xb, ny, nz), lambda i, w: (i + skip, 0, 0))
     slab = pl.BlockSpec((3, ny, nz), lambda i, w: (0, 0, 0))
-    edge = pl.BlockSpec((3, xb, nz), lambda i, w: (0, i, 0))
-    shapes = [(nx, ny, nz)] * 2 + [(3, ny, nz)] * 2 + [(3, nx, nz)] * 2
+    edge = pl.BlockSpec((3, xb, nz), lambda i, w: (0, i + skip, 0))
+    whole_piece = pl.BlockSpec((xb, part, ny), lambda i, w: (i + skip, 0, 0))
+    cut_piece = pl.BlockSpec((xb, part, ny), lambda i, w: (i, 0, 0))
+    anywhere = pl.BlockSpec(memory_space=pl.ANY)
+    count = 2 if last else 1
+    shapes = [(nx, ny, nz)] * 2 + [(3, nx, nz)] * 2 + [(3, ny, nz)] * count
     return pl.pallas_call(
         kernel,
         grid_spec=pltpu.PrefetchScalarGridSpec(
             num_scalar_prefetch=1,
             grid=(steps,),
             in_specs=[pl.BlockSpec(basis_zt.shape, lambda i, w: (0, 0)), field, field]
-            + [pl.BlockSpec((xb, part, ny), lambda i, w: (i, 0, 0))] * len(flat),
-            out_specs=[field] * 2 + [slab] * 2 + [edge] * 2,
+            + ([anywhere] * 4 + [slab, anywhere] if before else [])
+            + [whole_piece if p.shape[0] == nx else cut_piece for p in flat],
+            out_specs=[field] * 2 + [edge] * 2 + [slab] * count,
         ),
         out_shape=[jax.ShapeDtypeStruct(shape, F32) for shape in shapes],
+        input_output_aliases={4 + n: n for n in range(4)} if before else {},
         compiler_params=params(1),
-        cost_estimate=cost(6 * nx * ny * nz * nz, 22 * nx * ny * nz),
+        cost_estimate=cost(6 * nx * ny * nz * nz // cuts, 22 * nx * ny * nz // cuts),
         name="backward_z",
-    )(where, basis_zt, adjoint, coefficient, *flat)
+    )(where, basis_zt, adjoint, coefficient, *before, *flat)
 
 
 def band(n):
@@ -286,9 +310,9 @@
     return out
 
 
-def stencil(weighted, residual, bands, halos=None, after=None):
+def stencil(weighted, residual, bands, first=1, count=0, halos=None, after=None):
     nx, ny, nz = weighted.shape
-    xb = 8
+    xb, unroll = 8, 4
     steps = nx // xb
     halves = nz // 128
     outer = halos is not None
@@ -303,10 +327,10 @@
 
         @pl.when(i == 0)
         def _():
-            zero = jnp.zeros((halves, 8, 128), F32)
+            zero = jnp.zeros((unroll, halves, 8, 128), F32)
             for ref in (ps, qs):
-                ref[:, :8, :] = zero
-                ref[:, 8 + ny :, :] = zero
+                ref[:, :, :8, :] = zero
+                ref[:, :, 8 + ny :, :] = zero
 
         win[:3] = prev[xb - 3 :]
         win[3 : 3 + xb] = cur[...]
@@ -324,28 +348,29 @@
                 high = jnp.where(me % 2 == 0, xa[...], xc[...])
                 win[3 + xb :] = jnp.where(me == rows - 1, 0.0, high)
 
-        @pl.loop(0, xb)
-        def _(x):
-            p, q = taps(lambda o: win[x + 3 + o])
-            for h in range(halves):
-                cols = slice(h * 128, (h + 1) * 128)
-                ps[h, 8 : 8 + ny, :] = p[:, cols]
-                qs[h, 8 : 8 + ny, :] = q[:, cols]
-            first_terms, second_terms = [], []
-            for h in range(halves):
-                mp, kp = taps(lambda o: ps[h, 8 + o : 8 + o + ny, :])
-                (mq,) = taps(lambda o: qs[h, 8 + o : 8 + o + ny, :], stiff=False)
-                first_terms.append(kp + mq)
-                second_terms.append(mp)
-            both = split(join(first_terms + second_terms, 1))
-            out[x] = r_ref[x] - dot3(both, (bh[...], bl[...]), NN)
+        @pl.loop(0, xb // unroll)
+        def _(step):
+            for u in range(unroll):
+                x = step * unroll + u
+                p, q = taps(lambda o: win[x + 3 + o])
+                for h in range(halves):
+                    cols = slice(h * 128, (h + 1) * 128)
+                    ps[u, h, 8 : 8 + ny, :] = p[:, cols]
+                    qs[u, h, 8 : 8 + ny, :] = q[:, cols]
+                first_terms, second_terms = [], []
+                for h in range(halves):
+                    mp, kp = taps(lambda o: ps[u, h, 8 + o : 8 + o + ny, :])
+                    (mq,) = taps(lambda o: qs[u, h, 8 + o : 8 + o + ny, :], stiff=False)
+                    first_terms.append(kp + mq)
+                    second_terms.append(mp)
+                both = split(join(first_terms + second_terms, 1))
+                out[x] = r_ref[x] - dot3(both, (bh[...], bl[...]), NN)
 
     if outer:
         at = lambda i: i * (steps - 1)
         count = 2
     else:
-        at = lambda i: i + 1
-        count = steps - 2
+        at = lambda i: i + first
 
     def block(shift):
         return pl.BlockSpec(
@@ -365,8 +390,8 @@
         out_specs=block(0),
         out_shape=jax.ShapeDtypeStruct((nx, ny, nz), F32),
         scratch_shapes=[pltpu.VMEM((xb + 6, ny, nz), F32)]
-        + [pltpu.VMEM((halves, ny + 16, 128), F32)] * 2,
-        input_output_aliases={0: 0} if outer else {},
+        + [pltpu.VMEM((unroll, halves, ny + 16, 128), F32)] * 2,
+        input_output_aliases={} if after is None else {0: 0},
         compiler_params=params(1),
         cost_estimate=cost(12 * count * xb * ny * nz * nz, 12 * count * xb * ny * nz),
         name="stencil_outer" if outer else "stencil_inner",
@@ -447,11 +472,15 @@
 def schedule(chunks):
     order = [("z", 0), ("z", 1)][:chunks]
     if chunks == 4:
-        order += [("x", 0), ("y", 0), ("b", 0), ("x", 1), ("x", 2), ("y", 1)]
-        order += [("x", 3), ("y", 2), ("b", 1), ("y", 3), ("b", 2), ("b", 3)]
+        order += [("x", 0), ("y", 0), ("x", 1), ("b", 0), ("y", 1), ("x", 2)]
+        order += [("b", 1), ("y", 2), ("x", 3), ("b", 2), ("y", 3), ("b", 3)]
     else:
         order += [(s, k) for k in range(chunks) for s in ("x", "y", "b")]
     return order
+
+
+def cut_count(nx):
+    return 2 if nx % 16 == 0 and nx // 8 >= 6 else 1
 
 
 def chunk_count(nz, rows):
@@ -467,6 +496,8 @@
     chunks = chunk_count(nz, rows)
     part = nz // (rows * chunks)
     where = jnp.stack([ri, ci]).astype(jnp.int32)
+    steps = nx // 8
+    cuts = cut_count(nx)
 
     basis_zt = basis_z.T
     bx = jnp.concatenate(
@@ -500,30 +531,41 @@
         elif stage == "y":
             out = middle_y(mid[k], by2, byt2, shift[k], ey, last)
         else:
-            out = backward_x(ret[k], bx2, rows, last)
+            parts = cuts if k == chunks - 1 else 1
+            out = backward_x(ret[k], bx2, rows, last, parts)
         if stage == "z":
-            for n in these:
-                fw[n] = exchange(*fw[n])
+            fw[k] = exchange(*fw[k])
         elif stage == "x":
             mid[k] = exchange(out, "col")
         elif stage == "y":
             ret[k] = exchange(out, "col")
         else:
-            back[k] = exchange(out, "row")
+            back[k] = exchange(out[:rows], "row")
+        if stage == "x" and k + 2 < chunks:
+            fw[k + 2] = exchange(*fw[k + 2])
         if stage != "z":
             last = out[0]
-    adjoint_next, weighted, xa, xc, ea, ec = backward_z(
-        back, basis_zt, where, adjoint, coefficient
-    )
+    late = exchange(out[rows:], "row") if cuts > 1 else None
+    fields = (basis_zt, where, adjoint, coefficient)
+    if cuts > 1:
+        early = backward_z(back, *fields, 0, cuts)
+        begun = stencil(early[1], residual, bands, 1, steps // 2 - 2)
+        back = back[:-1] + [late]
+        done = backward_z(back, *fields, 1, cuts, (*early, begun))
+        rest = (steps // 2 - 1, steps // 2)
+    else:
+        done = backward_z(back, *fields)
+        begun, rest = None, (1, steps - 2)
+    adjoint_next, weighted, ea, ec, xa, xc = done
     ea, ec = swap(ea, "col", True), swap(ec, "col", False)
     xa, xc = swap(xa, "row", True), swap(xc, "row", False)
-    inner = stencil(weighted, residual, bands)
+    inner = stencil(weighted, residual, bands, *rest, after=begun)
     sides, _ = lax.optimization_barrier((jnp.stack([ea, ec]), inner))
     low, high = sides[:, :, :8], sides[:, :, -8:]
     even = ri % 2 == 0
     ca = swap(jnp.where(even, high, low), "row", True)
     cc = swap(jnp.where(even, low, high), "row", False)
-    outer = stencil(weighted, residual, bands, (where, xa, xc), inner)
+    outer = stencil(weighted, residual, bands, halos=(where, xa, xc), after=inner)
     residual_next = stencil_sides(outer, where, bands, (ea, ec), (ca, cc))
     return adjoint_next, residual_next
 

time: 546 us -> 539 us (0.987)
  the two profiles are of different devices: /device:TPU:9 before, /device:TPU:0 now
where the time goes in v3:
time: 539 us; the launch traced here: 529 us
  starting transfers between devices  201 us (37%)
  Pallas kernels  170 us (32%)
  waiting for transfers between devices  135 us (25%)
  local copies, waits for them, and re-layouts  20.2 us (4%)
    ppermute x87, starting transfers between devices, exchange(): out[d] = lax.ppermute(pieces[d], axis, [(i, i ^ d) for i in range(n)])  190 us
    ppermute x87, waiting for transfers between devices, exchange(): out[d] = lax.ppermute(pieces[d], axis, [(i, i ^ d) for i in range(n)])  135 us
    pallas_call x3, Pallas kernels, stencil(): pl.pallas_call(kernel, grid=(count,), in_specs=[pl.BlockSpec(memory_space...  36.7 us
    pallas_call x4, Pallas kernels, middle_y(): pl.pallas_call(kernel, grid=(part // cb,), out_shape=[jax.ShapeDtypeStruc...  30.2 us
    pallas_call x4, Pallas kernels, forward_x(): pl.pallas_call(kernel, out_shape=[jax.ShapeDtypeStruct((part, wide, ny),...  26 us
    pallas_call x4, Pallas kernels, backward_x(): pl.pallas_call(kernel, out_shape=[jax.ShapeDtypeStruct((nx, part, ny), F3...  25.9 us
    pallas_call x2, Pallas kernels, forward_z(): pl.pallas_call(kernel, grid_spec=pltpu.PrefetchScalarGridSpec(num_scalar_...  23.5 us
    pallas_call x2, Pallas kernels, backward_z(): pl.pallas_call(kernel, grid_spec=pltpu.PrefetchScalarGridSpec(num_scalar_...  20.8 us
  transfers between devices with their start and end apart: 93, of which 23 were waited for; matrix products, arithmetic and copies ran while one was open for 2% of the time, Pallas kernels for 27%

profile of v3, /device:TPU:0, one launch (start us, length us, event | category | flops | bytes accessed | tf_op | source)
XLA Modules:
  0.0 529.2 jit_solution(18324476379036192921)
XLA Ops:
  3.1 10.9 %forward_z.3 = (f32[64,8,128]{2,1,0:T(8,128)}, f32[64,8,128]{2,1,0:T(8,128)}, f32[64,8,128]{2,1,0:T(8,128)}, f32[64,8,128]{2,1,0:T(8,128)}, f32[64,8,128]{2,1,0:...) custom-call(s32[2]{0:T(128)} %pad_add_fusion.where_ref.refs_0_, ...), custom_call_target="tpu_custom_call" | custom-call | flops 805306368 | bytes 8388608 | tf_op jit(solution)/shard_map/forward_z/pallas_call | solution.py:95
  27.4 9.4 %collective-permute-done.1.refs_2_ = f32[64,8,128]{2,1,0:T(8,128)S(1)} collective-permute-done((f32[64,8,128]{2,1,0:T(8,128)}, f32[64,8,128]{2,1,0:T(8,128)S(1)}, u32[]{:S(2)}, u32[]{:S(2)}) %collective-permute-start.1) | collective-permute-done | bytes 262176 | tf_op jit(solution)/shard_map/ppermute | solution.py:460
  40.5 12.6 %forward_z.2 = (f32[64,8,128]{2,1,0:T(8,128)}, f32[64,8,128]{2,1,0:T(8,128)}, f32[64,8,128]{2,1,0:T(8,128)}, f32[64,8,128]{2,1,0:T(8,128)}, f32[64,8,128]{2,1,0:...) custom-call(s32[2]{0:T(128)} %pad_add_fusion.where_ref.refs_0_, ...), custom_call_target="tpu_custom_call" | custom-call | flops 2415919104 | bytes 8388608 | tf_op jit(solution)/shard_map/forward_z/pallas_call | solution.py:95
  68.6 9.5 %collective-permute-start.12 = (f32[64,8,128]{2,1,0:T(8,128)}, f32[64,8,128]{2,1,0:T(8,128)}, u32[]{:S(2)}, u32[]{:S(2)}) collective-permute-start(f32[64,8,128]{2,1,0:T(8,128)} %get-tuple-element.135), channel_id=1, source_target_pairs={{0,12},{4,8},{8,4},{12,0},{16,28},{20,24},{24,20},{28,16},{1,13},{... | collective-permute-start | bytes 786440 | tf_op jit(solution)/shard_map/ppermute | solution.py:460
  95.7 7.4 %middle_y.4 = (f32[8,128,128]{2,1,0:T(8,128)}, f32[8,128,128]{2,1,0:T(8,128)}, f32[8,128,128]{2,1,0:T(8,128)}, f32[8,128,128]{2,1,0:T(8,128)}) custom-call(f32[8,128,128]{2,1,0:T(8,128)} %get-tuple-element.127._.refs_0_, bf16[512,512]{1,0:T(8,128)(2,1)} %copy.122.bh, bf16[512,512]{1,0:T(8,128)(2,1)} %copy.123.bl, bf16[512,512]{1,0:T(8,128)(2,1)} %bitcast.29, ...), custom_call_target="tpu_custom_call" | custom-call | flops 3221225472 | bytes 4194304 | tf_op jit(solution)/shard_map/middle_y/pallas_call | solution.py:164
  103.1 10.8 %collective-permute-done.13.refs_4_ = f32[64,8,128]{2,1,0:T(8,128)S(1)} collective-permute-done((f32[64,8,128]{2,1,0:T(8,128)}, f32[64,8,128]{2,1,0:T(8,128)S(1)}, u32[]{:S(2)}, u32[]{:S(2)}) %collective-permute-start.13) | collective-permute-done | bytes 262176 | tf_op jit(solution)/shard_map/ppermute | solution.py:460
  121.7 9.4 %collective-permute-start.31 = (f32[64,8,128]{2,1,0:T(8,128)}, f32[64,8,128]{2,1,0:T(8,128)S(1)}, u32[]{:S(2)}, u32[]{:S(2)}) collective-permute-start(f32[64,8,128]{2,1,0:T(8,128)} %get-tuple-element.158), channel_id=1, source_target_pairs={{0,8},{4,12},{8,0},{12,4},{16,24},{20,28},{24,16},{28,20},{1,9},{5... | collective-permute-start | bytes 786440 | tf_op jit(solution)/shard_map/ppermute | solution.py:460
  157.0 10.2 %collective-permute-done.33.refs_4_ = f32[64,8,128]{2,1,0:T(8,128)} collective-permute-done((f32[64,8,128]{2,1,0:T(8,128)}, f32[64,8,128]{2,1,0:T(8,128)}, u32[]{:S(2)}, u32[]{:S(2)}) %collective-permute-start.33) | collective-permute-done | bytes 262176 | tf_op jit(solution)/shard_map/ppermute | solution.py:460
  169.8 9.0 %collective-permute-done.34.refs_5_ = f32[64,8,128]{2,1,0:T(8,128)} collective-permute-done((f32[64,8,128]{2,1,0:T(8,128)}, f32[64,8,128]{2,1,0:T(8,128)}, u32[]{:S(2)}, u32[]{:S(2)}) %collective-permute-start.34) | collective-permute-done | bytes 262176 | tf_op jit(solution)/shard_map/ppermute | solution.py:460
  185.5 7.9 %middle_y.5 = (f32[8,128,128]{2,1,0:T(8,128)}, f32[8,128,128]{2,1,0:T(8,128)}, f32[8,128,128]{2,1,0:T(8,128)}, f32[8,128,128]{2,1,0:T(8,128)}) custom-call(f32[64,8,128]{2,1,0:T(8,128)} %get-tuple-element.144._.refs_0_.refs_6_, bf16[512,512]{1,0:T(8,128)(2,1)} %copy.122.bh, bf16[512,512]{1,0:T(8,128)(2,1)} %copy.123.bl, bf16[512,512]{1,0:T(8,128)(2,1)} %bitcast.30, ...), custom_call_target="tpu_custom_call" | custom-call | flops 3221225472 | bytes 4194304 | tf_op jit(solution)/shard_map/middle_y/pallas_call | solution.py:164
  241.6 9.2 %collective-permute-start.21 = (f32[64,8,128]{2,1,0:T(8,128)S(1)}, f32[64,8,128]{2,1,0:T(8,128)S(1)}, u32[]{:S(2)}, u32[]{:S(2)}) collective-permute-start(f32[64,8,128]{2,1,0:T(8,128)S(1)} %copy-done.76), channel_id=1, source_target_pairs={{0,8},{4,12},{8,0},{12,4},{16,24},{20,28},{24,16},{28,20},{1,9},{5... | collective-permute-start | bytes 786440 | tf_op jit(solution)/shard_map/ppermute | solution.py:460
  255.2 7.4 %middle_y.6 = (f32[8,128,128]{2,1,0:T(8,128)}, f32[8,128,128]{2,1,0:T(8,128)}, f32[8,128,128]{2,1,0:T(8,128)}, f32[8,128,128]{2,1,0:T(8,128)}) custom-call(f32[64,8,128]{2,1,0:T(8,128)} %get-tuple-element.168._.refs_8_.refs_14_, bf16[512,512]{1,0:T(8,128)(2,1)} %copy.122.bh, bf16[512,512]{1,0:T(8,128)(2,1)} %copy.123.bl, bf16[512,512]{1,0:T(8,128)(2,1)} %bitcast.31, ...), custom_call_target="tpu_custom_call" | custom-call | flops 3221225472 | bytes 4194304 | tf_op jit(solution)/shard_map/middle_y/pallas_call | solution.py:164
  279.3 8.1 %collective-permute-start.26 = (f32[64,8,128]{2,1,0:T(8,128)S(1)}, f32[64,8,128]{2,1,0:T(8,128)S(1)}, u32[]{:S(2)}, u32[]{:S(2)}) collective-permute-start(f32[64,8,128]{2,1,0:T(8,128)S(1)} %copy-done.68), channel_id=1, source_target_pairs={{0,28},{4,24},{8,20},{12,16},{16,12},{20,8},{24,4},{28,0},{1,29},{... | collective-permute-start | bytes 786440 | tf_op jit(solution)/shard_map/ppermute | solution.py:460
  321.1 7.5 %middle_y.7 = (f32[8,128,128]{2,1,0:T(8,128)}, f32[8,128,128]{2,1,0:T(8,128)}, f32[8,128,128]{2,1,0:T(8,128)}, f32[8,128,128]{2,1,0:T(8,128)}) custom-call(f32[64,8,128]{2,1,0:T(8,128)} %get-tuple-element.191._.refs_16_.refs_22_, bf16[512,512]{1,0:T(8,128)(2,1)} %copy.122.bh, bf16[512,512]{1,0:T(8,128)(2,1)} %copy.123.bl, bf16[512,512]{1,0:T(8,128)(2,1)} %bitcast.32, ...), custom_call_target="tpu_custom_call" | custom-call | flops 3221225472 | bytes 4194304 | tf_op jit(solution)/shard_map/middle_y/pallas_call | solution.py:164
  328.8 16.6 %collective-permute-done.43.refs_12_.refs_18_ = f32[64,8,128]{2,1,0:T(8,128)S(1)} collective-permute-done((f32[64,8,128]{2,1,0:T(8,128)}, f32[64,8,128]{2,1,0:T(8,128)S(1)}, u32[]{:S(2)}, u32[]{:S(2)}) %collective-permute-start.43) | collective-permute-done | bytes 262176 | tf_op jit(solution)/shard_map/ppermute | solution.py:460
  352.6 10.2 %collective-permute-start.61 = (f32[64,8,128]{2,1,0:T(8,128)S(1)}, f32[64,8,128]{2,1,0:T(8,128)S(1)}, u32[]{:S(2)}, u32[]{:S(2)}) collective-permute-start(f32[64,8,128]{2,1,0:T(8,128)S(1)} %copy-done.89), channel_id=1, source_target_pairs={{0,8},{4,12},{8,0},{12,4},{16,24},{20,28},{24,16},{28,20},{1,9},{5... | collective-permute-start | bytes 786440 | tf_op jit(solution)/shard_map/ppermute | solution.py:460
  385.1 16.8 %collective-permute-done.63.refs_20_.refs_26_ = f32[64,8,128]{2,1,0:T(8,128)S(1)} collective-permute-done((f32[64,8,128]{2,1,0:T(8,128)S(1)}, f32[64,8,128]{2,1,0:T(8,128)S(1)}, u32[]{:S(2)}, u32[]{:S(2)}) %collective-permute-start.63) | collective-permute-done | bytes 262176 | tf_op jit(solution)/shard_map/ppermute | solution.py:460
  414.6 9.8 %collective-permute-start.77 = (f32[32,8,128]{2,1,0:T(8,128)}, f32[32,8,128]{2,1,0:T(8,128)}, u32[]{:S(2)}, u32[]{:S(2)}) collective-permute-start(f32[32,8,128]{2,1,0:T(8,128)} %get-tuple-element.211), channel_id=1, source_target_pairs={{0,20},{4,16},{8,28},{12,24},{16,4},{20,0},{24,12},{28,8},{1,21},{... | collective-permute-start | bytes 393224 | tf_op jit(solution)/shard_map/ppermute | solution.py:460
  445.7 10.3 %backward_z.2 = (f32[64,128,256]{2,1,0:T(8,128)}, f32[64,128,256]{2,1,0:T(8,128)}, f32[3,64,256]{2,1,0:T(8,128)}, f32[3,64,256]{2,1,0:T(8,128)}, f32[3,128,256]{2,1,0:T(8,128)}) custom-call(s32[2]{0:T(128)} %pad_add_fusion.where_ref.refs_0_, f32[256,256]{1,0:T(8,128)} %bitcast.21, f32[64,128,256]{2,1,0:T(8,128)} %adj_ref.3, bf16[64,128,256]{2,1,0:T(8,128)(2,1)} %coef_ref.3, ...), custom_call_target="tpu_custom_call" | custom-call | flops 1610612736 | bytes 23068672 | tf_op jit(solution)/shard_map/backward_z/pallas_call | solution.py:277
  460.2 9.9 %stencil_inner.2.refs_5_._ = f32[64,128,256]{2,1,0:T(8,128)} custom-call(f32[64,128,256]{2,1,0:T(8,128)} %get-tuple-element.215._.refs_0_.refs_1_.refs_2_, bf16[512,256]{1,0:T(8,128)(2,1)} %constant.46.bh, bf16[512,256]{1,0:T(8,128)(2,1)} %constant.48.bl, f32[64,128,256]{2,1,0:T(8,128)} %get-tuple-element.215._.refs_0_.refs_1_.refs_2_, ...), custom_call_target="tpu_custom_call" | custom-call | flops 1610612736 | bytes 6291456 | tf_op jit(solution)/shard_map/stencil_inner/pallas_call | solution.py:382
  470.9 10.5 %backward_z.3 = (f32[64,128,256]{2,1,0:T(8,128)}, f32[64,128,256]{2,1,0:T(8,128)}, f32[3,64,256]{2,1,0:T(8,128)}, f32[3,64,256]{2,1,0:T(8,128)}, f32[3,128,256]{2,1,0:T(8,128)}, /*index=5*/f32[3,128,256]{2,1,0:T(8,128)}) custom-call(s32[2]{0:T(128)} %pad_add_fusion.where_ref.refs_0_, ...), custom_call_target="tpu_custom_call", output_to_operand_aliasing={{0}: (4, {}), {1}: (5, {}), {2}: (6, {}), {3}: (7, {})} | custom-call | flops 1610612736 | bytes 23068672 | tf_op jit(solution)/shard_map/backward_z/pallas_call | solution.py:277
  486.0 16.3 %stencil_inner.3._ = f32[64,128,256]{2,1,0:T(8,128)} custom-call(f32[64,128,256]{2,1,0:T(8,128)} %stencil_inner.2.refs_5_._, bf16[512,256]{1,0:T(8,128)(2,1)} %constant.46.bh, bf16[512,256]{1,0:T(8,128)(2,1)} %constant.48.bl, f32[64,128,256]{2,1,0:T(8,128)} %get-tuple-element.230.refs_0_.refs_1_.refs_2_.refs_3_.refs_4_.refs_5_, ...), custom_call_target="tpu_custom_call", output_to_operand_aliasing={{}: (0, {})} | custom-call | flops 3221225472 | bytes 12582912 | tf_op jit(solution)/shard_map/stencil_inner/pallas_call | solution.py:382
  509.9 10.5 %stencil_outer.1.r_ref = f32[64,128,256]{2,1,0:T(8,128)} custom-call(f32[64,128,256]{2,1,0:T(8,128)} %stencil_inner.3._, bf16[512,256]{1,0:T(8,128)(2,1)} %constant.46.bh, bf16[512,256]{1,0:T(8,128)(2,1)} %constant.48.bl, s32[2]{0:T(128)} %pad_add_fusion.where_ref.refs_0_, f32[3,128,256]{2,1,0:T(8,128)} %copy-done.29, ...), custom_call_target="tpu_custom_call", output_to_operand_aliasing={{}: (0, {})} | custom-call | flops 1610612736 | bytes 6291456 | tf_op jit(solution)/shard_map/stencil_outer/pallas_call | solution.py:382
  521.6 7.4 %stencil_sides.1 = f32[64,128,256]{2,1,0:T(8,128)} custom-call(s32[2]{0:T(128)} %pad_add_fusion.where_ref.refs_0_, bf16[512,256]{1,0:T(8,128)(2,1)} %constant.46.bh, bf16[512,256]{1,0:T(8,128)(2,1)} %constant.48.bl, f32[3,64,256]{2,1,0:T(8,128)} %copy-done.27, f32[3,64,256]{2,1,0:T(8,128)} %copy-done.28, ...), custom_call_target="tpu_custom_call", output_to_operand_aliasing={{}: (7, {})} | custom-call | flops 805306368 | bytes 2097152 | tf_op jit(solution)/shard_map/stencil_sides/pallas_call | solution.py:437
  (413 shorter events, 279.8 us)
Async XLA Ops:
  18.6 34.5 %collective-permute-start.2 = (f32[64,8,128]{2,1,0:T(8,128)}, f32[64,8,128]{2,1,0:T(8,128)S(1)}, u32[]{:S(2)}, u32[]{:S(2)}) collective-permute-start(f32[64,8,128]{2,1,0:T(8,128)} %get-tuple-element.122), channel_id=1, source_target_pairs={{0,12},{4,8},{8,4},{12,0},{16,28},{20,24},{24,20},{28,16},{1,13},{... | collective-permute-start | bytes 786440 | tf_op jit(solution)/shard_map/ppermute | solution.py:460
  18.6 37.1 %collective-permute-start.3 = (f32[64,8,128]{2,1,0:T(8,128)}, f32[64,8,128]{2,1,0:T(8,128)S(1)}, u32[]{:S(2)}, u32[]{:S(2)}) collective-permute-start(f32[64,8,128]{2,1,0:T(8,128)} %get-tuple-element.123), channel_id=1, source_target_pairs={{0,16},{4,20},{8,24},{12,28},{16,0},{20,4},{24,8},{28,12},{1,17},{... | collective-permute-start | bytes 786440 | tf_op jit(solution)/shard_map/ppermute | solution.py:460
  21.6 36.7 %collective-permute-start.4 = (f32[64,8,128]{2,1,0:T(8,128)}, f32[64,8,128]{2,1,0:T(8,128)S(1)}, u32[]{:S(2)}, u32[]{:S(2)}) collective-permute-start(f32[64,8,128]{2,1,0:T(8,128)} %get-tuple-element.124), channel_id=1, source_target_pairs={{0,20},{4,16},{8,28},{12,24},{16,4},{20,0},{24,12},{28,8},{1,21},{... | collective-permute-start | bytes 786440 | tf_op jit(solution)/shard_map/ppermute | solution.py:460
  23.5 34.8 %collective-permute-start.5 = (f32[64,8,128]{2,1,0:T(8,128)}, f32[64,8,128]{2,1,0:T(8,128)}, u32[]{:S(2)}, u32[]{:S(2)}) collective-permute-start(f32[64,8,128]{2,1,0:T(8,128)} %get-tuple-element.125), channel_id=1, source_target_pairs={{0,24},{4,28},{8,16},{12,20},{16,8},{20,12},{24,0},{28,4},{1,25},{... | collective-permute-start | bytes 786440 | tf_op jit(solution)/shard_map/ppermute | solution.py:460
  81.1 32.8 %collective-permute-start.13 = (f32[64,8,128]{2,1,0:T(8,128)}, f32[64,8,128]{2,1,0:T(8,128)S(1)}, u32[]{:S(2)}, u32[]{:S(2)}) collective-permute-start(f32[64,8,128]{2,1,0:T(8,128)} %get-tuple-element.136), channel_id=1, source_target_pairs={{0,16},{4,20},{8,24},{12,28},{16,0},{20,4},{24,8},{28,12},{1,17},{... | collective-permute-start | bytes 786440 | tf_op jit(solution)/shard_map/ppermute | solution.py:460
  85.3 34.9 %collective-permute-start.14 = (f32[64,8,128]{2,1,0:T(8,128)}, f32[64,8,128]{2,1,0:T(8,128)S(1)}, u32[]{:S(2)}, u32[]{:S(2)}) collective-permute-start(f32[64,8,128]{2,1,0:T(8,128)} %get-tuple-element.137), channel_id=1, source_target_pairs={{0,20},{4,16},{8,28},{12,24},{16,4},{20,0},{24,12},{28,8},{1,21},{... | collective-permute-start | bytes 786440 | tf_op jit(solution)/shard_map/ppermute | solution.py:460
  95.2 35.9 %collective-permute-start.30 = (f32[64,8,128]{2,1,0:T(8,128)}, f32[64,8,128]{2,1,0:T(8,128)S(1)}, u32[]{:S(2)}, u32[]{:S(2)}) collective-permute-start(f32[64,8,128]{2,1,0:T(8,128)} %get-tuple-element.157), channel_id=1, source_target_pairs={{0,4},{4,0},{8,12},{12,8},{16,20},{20,16},{24,28},{28,24},{1,5},{5... | collective-permute-start | bytes 786440 | tf_op jit(solution)/shard_map/ppermute | solution.py:460
  138.4 43.5 %collective-permute-start.27 = (f32[8,128,128]{2,1,0:T(8,128)}, f32[8,128,128]{2,1,0:T(8,128)S(1)}, u32[]{:S(2)}, u32[]{:S(2)}) collective-permute-start(f32[8,128,128]{2,1,0:T(8,128)} %get-tuple-element.152), channel_id=1, source_target_pairs={{0,1},{1,0},{2,3},{3,2},{4,5},{5,4},{6,7},{7,6},{8,9},{9,8},{10,11... | collective-permute-start | bytes 1572872 | tf_op jit(solution)/shard_map/ppermute | solution.py:460
  143.2 40.2 %collective-permute-start.28 = (f32[8,128,128]{2,1,0:T(8,128)}, f32[8,128,128]{2,1,0:T(8,128)S(1)}, u32[]{:S(2)}, u32[]{:S(2)}) collective-permute-start(f32[8,128,128]{2,1,0:T(8,128)} %get-tuple-element.153), channel_id=1, source_target_pairs={{0,2},{1,3},{2,0},{3,1},{4,6},{5,7},{6,4},{7,5},{8,10},{9,11},{10,... | collective-permute-start | bytes 1572872 | tf_op jit(solution)/shard_map/ppermute | solution.py:460
  144.7 38.6 %collective-permute-start.29 = (f32[8,128,128]{2,1,0:T(8,128)}, f32[8,128,128]{2,1,0:T(8,128)S(1)}, u32[]{:S(2)}, u32[]{:S(2)}) collective-permute-start(f32[8,128,128]{2,1,0:T(8,128)} %get-tuple-element.154), channel_id=1, source_target_pairs={{0,3},{1,2},{2,1},{3,0},{4,7},{5,6},{6,5},{7,4},{8,11},{9,10},{10,... | collective-permute-start | bytes 1572872 | tf_op jit(solution)/shard_map/ppermute | solution.py:460
  193.5 32.9 %collective-permute-start.38 = (f32[8,128,128]{2,1,0:T(8,128)}, f32[8,128,128]{2,1,0:T(8,128)S(1)}, u32[]{:S(2)}, u32[]{:S(2)}) collective-permute-start(f32[8,128,128]{2,1,0:T(8,128)} %get-tuple-element.166), channel_id=1, source_target_pairs={{0,2},{1,3},{2,0},{3,1},{4,6},{5,7},{6,4},{7,5},{8,10},{9,11},{10,... | collective-permute-start | bytes 1572872 | tf_op jit(solution)/shard_map/ppermute | solution.py:460
  217.5 33.3 %collective-permute-start.47 = (f32[8,128,128]{2,1,0:T(8,128)}, f32[8,128,128]{2,1,0:T(8,128)S(1)}, u32[]{:S(2)}, u32[]{:S(2)}) collective-permute-start(f32[8,128,128]{2,1,0:T(8,128)} %get-tuple-element.176), channel_id=1, source_target_pairs={{0,1},{1,0},{2,3},{3,2},{4,5},{5,4},{6,7},{7,6},{8,9},{9,8},{10,11... | collective-permute-start | bytes 1572872 | tf_op jit(solution)/shard_map/ppermute | solution.py:460
  312.5 32.9 %collective-permute-start.43 = (f32[64,8,128]{2,1,0:T(8,128)}, f32[64,8,128]{2,1,0:T(8,128)S(1)}, u32[]{:S(2)}, u32[]{:S(2)}) collective-permute-start(f32[64,8,128]{2,1,0:T(8,128)} %get-tuple-element.172), channel_id=1, source_target_pairs={{0,16},{4,20},{8,24},{12,28},{16,0},{20,4},{24,8},{28,12},{1,17},{... | collective-permute-start | bytes 786440 | tf_op jit(solution)/shard_map/ppermute | solution.py:460
  316.3 34.9 %collective-permute-start.44 = (f32[64,8,128]{2,1,0:T(8,128)}, f32[64,8,128]{2,1,0:T(8,128)S(1)}, u32[]{:S(2)}, u32[]{:S(2)}) collective-permute-start(f32[64,8,128]{2,1,0:T(8,128)} %get-tuple-element.173), channel_id=1, source_target_pairs={{0,20},{4,16},{8,28},{12,24},{16,4},{20,0},{24,12},{28,8},{1,21},{... | collective-permute-start | bytes 786440 | tf_op jit(solution)/shard_map/ppermute | solution.py:460
  316.5 34.7 %collective-permute-start.45 = (f32[64,8,128]{2,1,0:T(8,128)}, f32[64,8,128]{2,1,0:T(8,128)S(1)}, u32[]{:S(2)}, u32[]{:S(2)}) collective-permute-start(f32[64,8,128]{2,1,0:T(8,128)} %get-tuple-element.174), channel_id=1, source_target_pairs={{0,24},{4,28},{8,16},{12,20},{16,8},{20,12},{24,0},{28,4},{1,25},{... | collective-permute-start | bytes 786440 | tf_op jit(solution)/shard_map/ppermute | solution.py:460
  319.2 33.3 %collective-permute-start.46 = (f32[64,8,128]{2,1,0:T(8,128)}, f32[64,8,128]{2,1,0:T(8,128)S(1)}, u32[]{:S(2)}, u32[]{:S(2)}) collective-permute-start(f32[64,8,128]{2,1,0:T(8,128)} %get-tuple-element.175), channel_id=1, source_target_pairs={{0,28},{4,24},{8,20},{12,16},{16,12},{20,8},{24,4},{28,0},{1,29},{... | collective-permute-start | bytes 786440 | tf_op jit(solution)/shard_map/ppermute | solution.py:460
  328.7 43.2 %collective-permute-start.70 = (f32[8,128,128]{2,1,0:T(8,128)}, f32[8,128,128]{2,1,0:T(8,128)S(1)}, u32[]{:S(2)}, u32[]{:S(2)}) collective-permute-start(f32[8,128,128]{2,1,0:T(8,128)} %get-tuple-element.203), channel_id=1, source_target_pairs={{0,1},{1,0},{2,3},{3,2},{4,5},{5,4},{6,7},{7,6},{8,9},{9,8},{10,11... | collective-permute-start | bytes 1572872 | tf_op jit(solution)/shard_map/ppermute | solution.py:460
  369.2 32.6 %collective-permute-start.63 = (f32[64,8,128]{2,1,0:T(8,128)S(1)}, f32[64,8,128]{2,1,0:T(8,128)S(1)}, u32[]{:S(2)}, u32[]{:S(2)}) collective-permute-start(f32[64,8,128]{2,1,0:T(8,128)S(1)} %copy-done.85), channel_id=1, source_target_pairs={{0,16},{4,20},{8,24},{12,28},{16,0},{20,4},{24,8},{28,12},{1,17},{... | collective-permute-start | bytes 786440 | tf_op jit(solution)/shard_map/ppermute | solution.py:460
  371.9 36.3 %collective-permute-start.64 = (f32[64,8,128]{2,1,0:T(8,128)S(1)}, f32[64,8,128]{2,1,0:T(8,128)S(1)}, u32[]{:S(2)}, u32[]{:S(2)}) collective-permute-start(f32[64,8,128]{2,1,0:T(8,128)S(1)} %copy-done.82), channel_id=1, source_target_pairs={{0,20},{4,16},{8,28},{12,24},{16,4},{20,0},{24,12},{28,8},{1,21},{... | collective-permute-start | bytes 786440 | tf_op jit(solution)/shard_map/ppermute | solution.py:460
  373.1 35.2 %collective-permute-start.65 = (f32[64,8,128]{2,1,0:T(8,128)S(1)}, f32[64,8,128]{2,1,0:T(8,128)S(1)}, u32[]{:S(2)}, u32[]{:S(2)}) collective-permute-start(f32[64,8,128]{2,1,0:T(8,128)S(1)} %copy-done.81), channel_id=1, source_target_pairs={{0,24},{4,28},{8,16},{12,20},{16,8},{20,12},{24,0},{28,4},{1,25},{... | collective-permute-start | bytes 786440 | tf_op jit(solution)/shard_map/ppermute | solution.py:460
  375.5 39.1 %collective-permute-start.66 = (f32[64,8,128]{2,1,0:T(8,128)S(1)}, f32[64,8,128]{2,1,0:T(8,128)S(1)}, u32[]{:S(2)}, u32[]{:S(2)}) collective-permute-start(f32[64,8,128]{2,1,0:T(8,128)S(1)} %copy-done.80), channel_id=1, source_target_pairs={{0,28},{4,24},{8,20},{12,16},{16,12},{20,8},{24,4},{28,0},{1,29},{... | collective-permute-start | bytes 786440 | tf_op jit(solution)/shard_map/ppermute | solution.py:460
  383.6 40.8 %collective-permute-start.73 = (f32[32,8,128]{2,1,0:T(8,128)}, f32[32,8,128]{2,1,0:T(8,128)S(1)}, u32[]{:S(2)}, u32[]{:S(2)}) collective-permute-start(f32[32,8,128]{2,1,0:T(8,128)} %get-tuple-element.207), channel_id=1, source_target_pairs={{0,4},{4,0},{8,12},{12,8},{16,20},{20,16},{24,28},{28,24},{1,5},{5... | collective-permute-start | bytes 393224 | tf_op jit(solution)/shard_map/ppermute | solution.py:460
  435.4 34.6 %collective-permute-start.82 = (f32[32,8,128]{2,1,0:T(8,128)}, f32[32,8,128]{2,1,0:T(8,128)S(1)}, u32[]{:S(2)}, u32[]{:S(2)}) collective-permute-start(f32[32,8,128]{2,1,0:T(8,128)} %get-tuple-element.222), channel_id=1, source_target_pairs={{0,12},{4,8},{8,4},{12,0},{16,28},{20,24},{24,20},{28,16},{1,13},{... | collective-permute-start | bytes 393224 | tf_op jit(solution)/shard_map/ppermute | solution.py:460
  435.9 34.2 %collective-permute-start.83 = (f32[32,8,128]{2,1,0:T(8,128)}, f32[32,8,128]{2,1,0:T(8,128)S(1)}, u32[]{:S(2)}, u32[]{:S(2)}) collective-permute-start(f32[32,8,128]{2,1,0:T(8,128)} %get-tuple-element.223), channel_id=1, source_target_pairs={{0,16},{4,20},{8,24},{12,28},{16,0},{20,4},{24,8},{28,12},{1,17},{... | collective-permute-start | bytes 393224 | tf_op jit(solution)/shard_map/ppermute | solution.py:460
  (168 other events, 4119.0 us)

commit v4 on v3

--- a/solution.py
+++ b/solution.py
@@ -1,6 +1,5 @@
 import jax
 import jax.numpy as jnp
-import numpy as np
 from jax import lax
 from jax.experimental import pallas as pl
 from jax.experimental.pallas import tpu as pltpu
@@ -12,7 +11,6 @@
 F32, BF16 = jnp.float32, jnp.bfloat16
 NN = (((1,), (0,)), ((), ()))
 NT = (((1,), (1,)), ((), ()))
-TN = (((0,), (0,)), ((), ()))
 
 
 def params(n, limit=56 << 20):
@@ -58,12 +56,22 @@
     return total
 
 
-def pairwise(a, v, i):
-    ny = v.shape[2]
-    if ny % 128:
-        return [(c, dot3(a, split(v[c]), NN)) for c in (2 * i, 2 * i + 1)]
-    t = dot3(a, split(join([v[2 * i], v[2 * i + 1]], 1)), NN)
-    return [(2 * i, t[:, :ny]), (2 * i + 1, t[:, ny:])]
+def products(mat, v, w):
+    full, ny = v.shape[1:]
+    rows = full // 2
+
+    @pl.loop(0, v.shape[0])
+    def _(i):
+        at = pl.ds(pl.multiple_of((i % 2) * rows, rows), rows)
+        a = (mat[0][at, :], mat[1][at, :])
+        c = 2 * (i // 2)
+        if ny % 128:
+            w[c, at, :] = dot3(a, split(v[c]), NN)
+            w[c + 1, at, :] = dot3(a, split(v[c + 1]), NN)
+        else:
+            t = dot3(a, split(join([v[c], v[c + 1]], 1)), NN)
+            w[c, at, :] = t[:, :ny]
+            w[c + 1, at, :] = t[:, ny:]
 
 
 def whole(shape):
@@ -72,7 +80,7 @@
 
 def forward_z(residual, basis_zt, where, chunks, peers, part):
     nx, ny, nz = residual.shape
-    xb = 8
+    xb = 32 if nx % 32 == 0 else 8
     group = peers * part
 
     def kernel(where_ref, r_ref, b_ref, *outs):
@@ -82,14 +90,19 @@
             for k in chunks
             for d in range(peers)
         ]
-        basis = split(join(rows, 0))
+        width = len(rows) * part
+        both = jnp.concatenate(split(join(rows, 0)), 0)
 
         @pl.loop(0, xb // 4)
         def _(step):
-            for x in (4 * step + u for u in range(4)):
-                t = dot3(basis, split(r_ref[x]), NT)
+            high, low = split(r_ref[pl.ds(4 * step, 4)].reshape(4 * ny, nz))
+            product = lax.dot_general(high, both, NT, preferred_element_type=F32)
+            product += lax.dot_general(low, both, NT, preferred_element_type=F32)
+            for u in range(4):
+                t = product[u * ny : (u + 1) * ny, :].T
+                t = t[:width] + t[width:]
                 for n, out in enumerate(outs):
-                    out[x] = t[n * part : (n + 1) * part, :]
+                    out[4 * step + u] = t[n * part : (n + 1) * part, :]
 
     count = len(chunks) * peers
     outs = pl.pallas_call(
@@ -117,16 +130,14 @@
     wide = full // peers
 
     def kernel(_, bh, bl, *refs):
-        ins, outs, v = refs[: len(pieces)], refs[len(pieces) : -1], refs[-1]
+        ins, outs, v, w = refs[: len(pieces)], refs[len(pieces) : -2], refs[-2], refs[-1]
         for c in range(part):
             for d, r in enumerate(ins):
                 v[c, d * nx : (d + 1) * nx, :] = r[:, c, :]
 
-        @pl.loop(0, part // 2)
-        def _(i):
-            for c, t in pairwise((bh[...], bl[...]), v, i):
-                for e, out in enumerate(outs):
-                    out[c] = t[e * wide : (e + 1) * wide, :]
+        products((bh, bl), v, w)
+        for e, out in enumerate(outs):
+            out[...] = w[:, e * wide : (e + 1) * wide, :]
 
     return pl.pallas_call(
         kernel,
@@ -136,7 +147,7 @@
         out_specs=[pl.BlockSpec(memory_space=pltpu.VMEM)] * peers,
         compiler_params=params(0),
         cost_estimate=cost(6 * full * full * part * ny, 8 * full * part * ny),
-        scratch_shapes=[pltpu.VMEM((part, full, ny), F32)],
+        scratch_shapes=[pltpu.VMEM((part, full, ny), F32)] * 2,
         name="forward_x",
     )(after, *bxt, *pieces)
 
@@ -186,11 +197,7 @@
         for n, r in enumerate(ins):
             v[:, n * wide : (n + 1) * wide, :] = r[...]
 
-        @pl.loop(0, part // 2)
-        def _(i):
-            for c, t in pairwise((bh[...], bl[...]), v, i):
-                w[c] = t
-
+        products((bh, bl), v, w)
         for c in range(part):
             for n, out in enumerate(outs):
                 at = (n % peers) * cuts + n // peers
@@ -214,7 +221,7 @@
     peers, part = len(pieces[0]), pieces[0][0].shape[1]
     group = peers * part
     chunks = len(pieces)
-    xb = 8
+    xb = 16 if nx // cuts % 16 == 0 else 8
     steps = nx // xb // cuts
     flat = [p for chunk in pieces for p in chunk]
     last = cut == cuts - 1
@@ -235,11 +242,11 @@
 
         @pl.loop(0, xb // 4)
         def _(step):
-            for x in (4 * step + u for u in range(4)):
-                v = split(join([r[x] for r in ins], 0))
-                correction = dot3(v, basis, TN)
-                next_ref[x] = adj_ref[x] + correction
-                w_ref[x] = coef_ref[x].astype(F32) * correction
+            planes = pl.ds(4 * step, 4)
+            v = [join([r[4 * step + u] for r in ins], 0).T for u in range(4)]
+            correction = dot3(split(join(v, 0)), basis, NN).reshape(4, ny, nz)
+            next_ref[planes] = adj_ref[planes] + correction
+            w_ref[planes] = coef_ref[planes].astype(F32) * correction
 
         for n in range(2):
 
@@ -293,10 +300,11 @@
 
 
 def band(n):
-    out = np.zeros((2 * n, n), np.float32)
+    row = lax.broadcasted_iota(jnp.int32, (2 * n, n), 0)
+    offset = lax.broadcasted_iota(jnp.int32, (2 * n, n), 1) - row % n
+    out = jnp.zeros((2 * n, n), F32)
     for j in range(-3, 4):
-        out[:n] += MASS[j + 3] * np.eye(n, k=j, dtype=np.float32)
-        out[n:] += STIFF[j + 3] * np.eye(n, k=j, dtype=np.float32)
+        out = jnp.where(offset == j, jnp.where(row < n, MASS[j + 3], STIFF[j + 3]), out)
     return out
 
 
@@ -312,7 +320,7 @@
 
 def stencil(weighted, residual, bands, first=1, count=0, halos=None, after=None):
     nx, ny, nz = weighted.shape
-    xb, unroll = 8, 4
+    xb, unroll = 8, 4 if halos is None else 2
     steps = nx // xb
     halves = nz // 128
     outer = halos is not None
@@ -321,9 +329,9 @@
     def kernel(_, bh, bl, *refs):
         i = pl.program_id(0)
         if outer:
-            where_ref, xa, xc, prev, cur, nxt, r_ref, out, win, ps, qs = refs
+            where_ref, xa, xc, prev, cur, nxt, r_ref, out, win, ps, qs, high, low = refs
         else:
-            prev, cur, nxt, r_ref, out, win, ps, qs = refs
+            prev, cur, nxt, r_ref, out, win, ps, qs, high, low = refs
 
         @pl.when(i == 0)
         def _():
@@ -363,8 +371,12 @@
                     (mq,) = taps(lambda o: qs[u, h, 8 + o : 8 + o + ny, :], stiff=False)
                     first_terms.append(kp + mq)
                     second_terms.append(mp)
+                rows_u = slice(u * ny, (u + 1) * ny)
                 both = split(join(first_terms + second_terms, 1))
-                out[x] = r_ref[x] - dot3(both, (bh[...], bl[...]), NN)
+                high[rows_u], low[rows_u] = both
+            planes = pl.ds(step * unroll, unroll)
+            image = dot3((high[...], low[...]), (bh[...], bl[...]), NN)
+            out[planes] = r_ref[planes] - image.reshape(unroll, ny, nz)
 
     if outer:
         at = lambda i: i * (steps - 1)
@@ -390,7 +402,8 @@
         out_specs=block(0),
         out_shape=jax.ShapeDtypeStruct((nx, ny, nz), F32),
         scratch_shapes=[pltpu.VMEM((xb + 6, ny, nz), F32)]
-        + [pltpu.VMEM((unroll, halves, ny + 16, 128), F32)] * 2,
+        + [pltpu.VMEM((unroll, halves, ny + 16, 128), F32)] * 2
+        + [pltpu.VMEM((unroll * ny, 2 * nz), BF16)] * 2,
         input_output_aliases={} if after is None else {0: 0},
         compiler_params=params(1),
         cost_estimate=cost(12 * count * xb * ny * nz * nz, 12 * count * xb * ny * nz),
@@ -427,11 +440,14 @@
                     ph[:, base + j, :] = p
                     qh[:, base + j, :] = q
 
-        mp, kp = taps(lambda o: ph[:, 8 + o : 16 + o, :])
-        (mq,) = taps(lambda o: qh[:, 8 + o : 16 + o, :], stiff=False)
-        both = split(jnp.concatenate([kp + mq, mp], 2).reshape(nx * 8, 2 * nz))
-        image = dot3(both, (bh[...], bl[...]), NN)
-        out[...] = r_ref[...] - image.reshape(nx, 8, nz)
+        @pl.loop(0, nx // 16)
+        def _(g):
+            at = pl.ds(16 * g, 16)
+            mp, kp = taps(lambda o: ph[at, 8 + o : 16 + o, :])
+            (mq,) = taps(lambda o: qh[at, 8 + o : 16 + o, :], stiff=False)
+            both = split(jnp.concatenate([kp + mq, mp], 2).reshape(128, 2 * nz))
+            image = dot3(both, (bh[...], bl[...]), NN)
+            out[at] = r_ref[at] - image.reshape(16, 8, nz)
 
     field = pl.BlockSpec((nx, 8, nz), lambda i: (0, i * (ny // 8 - 1), 0))
     return pl.pallas_call(
@@ -515,7 +531,7 @@
     ez = lax.dynamic_slice_in_dim(eigen_z.reshape(chunks, rows, part), ri, 1, 1)[:, 0]
     shift = (ez[:, :, None] + ex[None, None, :])[..., None]
     ey = eigen_y[None, :]
-    bands = split_outside(jnp.asarray(band(nz)))
+    bands = split_outside(band(nz))
 
     fw, mid, ret, back = ([None] * chunks for _ in range(4))
     last = where

time: 539 us -> 539 us (level)
  Pallas kernels: 170 us -> 178 us
  waiting for transfers between devices: 135 us -> 128 us
    ppermute x87, waiting for transfers between devices: 135 us -> 128 us  [exchange(): out[d] = lax.ppermute(pieces[d], axis, [(i, i ^ d) for i in range(n)])]
  transfers between devices with their start and end apart: 93 -> 93, of which waited for: 23 -> 22; matrix products, arithmetic and copies ran while one was open for 2% -> 2% of each run, Pallas kernels for 27% -> 28%
where the time goes in v4:
time: 539 us; the launch traced here: 530 us
  starting transfers between devices  200 us (37%)
  Pallas kernels  178 us (33%)
  waiting for transfers between devices  128 us (24%)
  local copies, waits for them, and re-layouts  19.6 us (4%)
    ppermute x87, starting transfers between devices, exchange(): out[d] = lax.ppermute(pieces[d], axis, [(i, i ^ d) for i in range(n)])  189 us
    ppermute x87, waiting for transfers between devices, exchange(): out[d] = lax.ppermute(pieces[d], axis, [(i, i ^ d) for i in range(n)])  128 us
    pallas_call x3, Pallas kernels, stencil(): pl.pallas_call(kernel, grid=(count,), in_specs=[pl.BlockSpec(memory_space...  37.7 us
    pallas_call x4, Pallas kernels, middle_y(): pl.pallas_call(kernel, grid=(part // cb,), out_shape=[jax.ShapeDtypeStruc...  30.2 us
    pallas_call x4, Pallas kernels, forward_x(): pl.pallas_call(kernel, out_shape=[jax.ShapeDtypeStruct((part, wide, ny),...  29.4 us
    pallas_call x4, Pallas kernels, backward_x(): pl.pallas_call(kernel, out_shape=[jax.ShapeDtypeStruct((nx, part, ny), F3...  28.7 us
    pallas_call x2, Pallas kernels, forward_z(): pl.pallas_call(kernel, grid_spec=pltpu.PrefetchScalarGridSpec(num_scalar_...  24.6 us
    pallas_call x2, Pallas kernels, backward_z(): pl.pallas_call(kernel, grid_spec=pltpu.PrefetchScalarGridSpec(num_scalar_...  18.7 us
  transfers between devices with their start and end apart: 93, of which 22 were waited for; matrix products, arithmetic and copies ran while one was open for 2% of the time, Pallas kernels for 28%

profile of v4, /device:TPU:0, one launch (start us, length us, event | category | flops | bytes accessed | tf_op | source)
XLA Modules:
  0.0 529.8 jit_solution(10662302929813330172)
XLA Ops:
  3.1 10.1 %forward_z.3 = (f32[64,8,128]{2,1,0:T(8,128)}, f32[64,8,128]{2,1,0:T(8,128)}, f32[64,8,128]{2,1,0:T(8,128)}, f32[64,8,128]{2,1,0:T(8,128)}, f32[64,8,128]{2,1,0:...) custom-call(s32[2]{0:T(128)} %pad_add_fusion.where_ref.refs_0_, ...), custom_call_target="tpu_custom_call" | custom-call | flops 805306368 | bytes 8388608 | tf_op jit(solution)/shard_map/forward_z/pallas_call | solution.py:108
  26.6 9.4 %collective-permute-done.1.refs_2_ = f32[64,8,128]{2,1,0:T(8,128)S(1)} collective-permute-done((f32[64,8,128]{2,1,0:T(8,128)}, f32[64,8,128]{2,1,0:T(8,128)S(1)}, u32[]{:S(2)}, u32[]{:S(2)}) %collective-permute-start.1) | collective-permute-done | bytes 262176 | tf_op jit(solution)/shard_map/ppermute | solution.py:476
  39.7 14.5 %forward_z.2 = (f32[64,8,128]{2,1,0:T(8,128)}, f32[64,8,128]{2,1,0:T(8,128)}, f32[64,8,128]{2,1,0:T(8,128)}, f32[64,8,128]{2,1,0:T(8,128)}, f32[64,8,128]{2,1,0:...) custom-call(s32[2]{0:T(128)} %pad_add_fusion.where_ref.refs_0_, ...), custom_call_target="tpu_custom_call" | custom-call | flops 2415919104 | bytes 8388608 | tf_op jit(solution)/shard_map/forward_z/pallas_call | solution.py:108
  68.7 9.5 %collective-permute-start.12 = (f32[64,8,128]{2,1,0:T(8,128)}, f32[64,8,128]{2,1,0:T(8,128)}, u32[]{:S(2)}, u32[]{:S(2)}) collective-permute-start(f32[64,8,128]{2,1,0:T(8,128)} %get-tuple-element.135), channel_id=1, source_target_pairs={{0,12},{4,8},{8,4},{12,0},{16,28},{20,24},{24,20},{28,16},{1,13},{... | collective-permute-start | bytes 786440 | tf_op jit(solution)/shard_map/ppermute | solution.py:476
  95.8 7.4 %middle_y.4 = (f32[8,128,128]{2,1,0:T(8,128)}, f32[8,128,128]{2,1,0:T(8,128)}, f32[8,128,128]{2,1,0:T(8,128)}, f32[8,128,128]{2,1,0:T(8,128)}) custom-call(f32[8,128,128]{2,1,0:T(8,128)} %get-tuple-element.127._.refs_0_, bf16[512,512]{1,0:T(8,128)(2,1)} %copy.121.bh, bf16[512,512]{1,0:T(8,128)(2,1)} %copy.122.bl, bf16[512,512]{1,0:T(8,128)(2,1)} %bitcast.29, ...), custom_call_target="tpu_custom_call" | custom-call | flops 3221225472 | bytes 4194304 | tf_op jit(solution)/shard_map/middle_y/pallas_call | solution.py:175
  103.2 10.7 %collective-permute-done.13.refs_4_ = f32[64,8,128]{2,1,0:T(8,128)S(1)} collective-permute-done((f32[64,8,128]{2,1,0:T(8,128)}, f32[64,8,128]{2,1,0:T(8,128)S(1)}, u32[]{:S(2)}, u32[]{:S(2)}) %collective-permute-start.13) | collective-permute-done | bytes 262176 | tf_op jit(solution)/shard_map/ppermute | solution.py:476
  121.7 9.4 %collective-permute-start.31 = (f32[64,8,128]{2,1,0:T(8,128)}, f32[64,8,128]{2,1,0:T(8,128)S(1)}, u32[]{:S(2)}, u32[]{:S(2)}) collective-permute-start(f32[64,8,128]{2,1,0:T(8,128)} %get-tuple-element.158), channel_id=1, source_target_pairs={{0,8},{4,12},{8,0},{12,4},{16,24},{20,28},{24,16},{28,20},{1,9},{5... | collective-permute-start | bytes 786440 | tf_op jit(solution)/shard_map/ppermute | solution.py:476
  157.8 9.5 %collective-permute-done.33.refs_4_ = f32[64,8,128]{2,1,0:T(8,128)} collective-permute-done((f32[64,8,128]{2,1,0:T(8,128)}, f32[64,8,128]{2,1,0:T(8,128)}, u32[]{:S(2)}, u32[]{:S(2)}) %collective-permute-start.33) | collective-permute-done | bytes 262176 | tf_op jit(solution)/shard_map/ppermute | solution.py:476
  169.9 9.0 %collective-permute-done.34.refs_5_ = f32[64,8,128]{2,1,0:T(8,128)} collective-permute-done((f32[64,8,128]{2,1,0:T(8,128)}, f32[64,8,128]{2,1,0:T(8,128)}, u32[]{:S(2)}, u32[]{:S(2)}) %collective-permute-start.34) | collective-permute-done | bytes 262176 | tf_op jit(solution)/shard_map/ppermute | solution.py:476
  185.5 7.9 %middle_y.5 = (f32[8,128,128]{2,1,0:T(8,128)}, f32[8,128,128]{2,1,0:T(8,128)}, f32[8,128,128]{2,1,0:T(8,128)}, f32[8,128,128]{2,1,0:T(8,128)}) custom-call(f32[64,8,128]{2,1,0:T(8,128)} %get-tuple-element.144._.refs_0_.refs_6_, bf16[512,512]{1,0:T(8,128)(2,1)} %copy.121.bh, bf16[512,512]{1,0:T(8,128)(2,1)} %copy.122.bl, bf16[512,512]{1,0:T(8,128)(2,1)} %bitcast.30, ...), custom_call_target="tpu_custom_call" | custom-call | flops 3221225472 | bytes 4194304 | tf_op jit(solution)/shard_map/middle_y/pallas_call | solution.py:175
  241.7 9.3 %collective-permute-start.21 = (f32[64,8,128]{2,1,0:T(8,128)S(1)}, f32[64,8,128]{2,1,0:T(8,128)S(1)}, u32[]{:S(2)}, u32[]{:S(2)}) collective-permute-start(f32[64,8,128]{2,1,0:T(8,128)S(1)} %copy-done.79), channel_id=1, source_target_pairs={{0,8},{4,12},{8,0},{12,4},{16,24},{20,28},{24,16},{28,20},{1,9},{5... | collective-permute-start | bytes 786440 | tf_op jit(solution)/shard_map/ppermute | solution.py:476
  255.3 7.4 %middle_y.6 = (f32[8,128,128]{2,1,0:T(8,128)}, f32[8,128,128]{2,1,0:T(8,128)}, f32[8,128,128]{2,1,0:T(8,128)}, f32[8,128,128]{2,1,0:T(8,128)}) custom-call(f32[64,8,128]{2,1,0:T(8,128)} %get-tuple-element.168._.refs_8_.refs_14_, bf16[512,512]{1,0:T(8,128)(2,1)} %copy.121.bh, bf16[512,512]{1,0:T(8,128)(2,1)} %copy.122.bl, bf16[512,512]{1,0:T(8,128)(2,1)} %bitcast.31, ...), custom_call_target="tpu_custom_call" | custom-call | flops 3221225472 | bytes 4194304 | tf_op jit(solution)/shard_map/middle_y/pallas_call | solution.py:175
  279.4 8.1 %collective-permute-start.26 = (f32[64,8,128]{2,1,0:T(8,128)S(1)}, f32[64,8,128]{2,1,0:T(8,128)S(1)}, u32[]{:S(2)}, u32[]{:S(2)}) collective-permute-start(f32[64,8,128]{2,1,0:T(8,128)S(1)} %copy-done.71), channel_id=1, source_target_pairs={{0,28},{4,24},{8,20},{12,16},{16,12},{20,8},{24,4},{28,0},{1,29},{... | collective-permute-start | bytes 786440 | tf_op jit(solution)/shard_map/ppermute | solution.py:476
  321.9 7.5 %middle_y.7 = (f32[8,128,128]{2,1,0:T(8,128)}, f32[8,128,128]{2,1,0:T(8,128)}, f32[8,128,128]{2,1,0:T(8,128)}, f32[8,128,128]{2,1,0:T(8,128)}) custom-call(f32[64,8,128]{2,1,0:T(8,128)} %get-tuple-element.191._.refs_16_.refs_22_, bf16[512,512]{1,0:T(8,128)(2,1)} %copy.121.bh, bf16[512,512]{1,0:T(8,128)(2,1)} %copy.122.bl, bf16[512,512]{1,0:T(8,128)(2,1)} %bitcast.32, ...), custom_call_target="tpu_custom_call" | custom-call | flops 3221225472 | bytes 4194304 | tf_op jit(solution)/shard_map/middle_y/pallas_call | solution.py:175
  329.6 16.6 %collective-permute-done.43.refs_12_.refs_18_ = f32[64,8,128]{2,1,0:T(8,128)S(1)} collective-permute-done((f32[64,8,128]{2,1,0:T(8,128)}, f32[64,8,128]{2,1,0:T(8,128)S(1)}, u32[]{:S(2)}, u32[]{:S(2)}) %collective-permute-start.43) | collective-permute-done | bytes 262176 | tf_op jit(solution)/shard_map/ppermute | solution.py:476
  353.3 10.2 %collective-permute-start.61 = (f32[64,8,128]{2,1,0:T(8,128)S(1)}, f32[64,8,128]{2,1,0:T(8,128)S(1)}, u32[]{:S(2)}, u32[]{:S(2)}) collective-permute-start(f32[64,8,128]{2,1,0:T(8,128)S(1)} %copy-done.89), channel_id=1, source_target_pairs={{0,8},{4,12},{8,0},{12,4},{16,24},{20,28},{24,16},{28,20},{1,9},{5... | collective-permute-start | bytes 786440 | tf_op jit(solution)/shard_map/ppermute | solution.py:476
  386.4 16.2 %collective-permute-done.63.refs_20_.refs_26_ = f32[64,8,128]{2,1,0:T(8,128)S(1)} collective-permute-done((f32[64,8,128]{2,1,0:T(8,128)S(1)}, f32[64,8,128]{2,1,0:T(8,128)S(1)}, u32[]{:S(2)}, u32[]{:S(2)}) %collective-permute-start.63) | collective-permute-done | bytes 262176 | tf_op jit(solution)/shard_map/ppermute | solution.py:476
  415.3 9.8 %collective-permute-start.77 = (f32[32,8,128]{2,1,0:T(8,128)}, f32[32,8,128]{2,1,0:T(8,128)S(1)}, u32[]{:S(2)}, u32[]{:S(2)}) collective-permute-start(f32[32,8,128]{2,1,0:T(8,128)} %get-tuple-element.211), channel_id=1, source_target_pairs={{0,20},{4,16},{8,28},{12,24},{16,4},{20,0},{24,12},{28,8},{1,21},{... | collective-permute-start | bytes 393224 | tf_op jit(solution)/shard_map/ppermute | solution.py:476
  446.4 9.3 %backward_z.2 = (f32[64,128,256]{2,1,0:T(8,128)}, f32[64,128,256]{2,1,0:T(8,128)}, f32[3,64,256]{2,1,0:T(8,128)}, f32[3,64,256]{2,1,0:T(8,128)}, f32[3,128,256]{2,1,0:T(8,128)}) custom-call(s32[2]{0:T(128)} %pad_add_fusion.where_ref.refs_0_, f32[256,256]{1,0:T(8,128)} %bitcast.21, f32[64,128,256]{2,1,0:T(8,128)} %adj_ref.3, bf16[64,128,256]{2,1,0:T(8,128)(2,1)} %coef_ref.3, ...), custom_call_target="tpu_custom_call" | custom-call | flops 1610612736 | bytes 23068672 | tf_op jit(solution)/shard_map/backward_z/pallas_call | solution.py:284
  459.7 10.0 %stencil_inner.2.refs_5_._ = f32[64,128,256]{2,1,0:T(8,128)} custom-call(f32[64,128,256]{2,1,0:T(8,128)} %get-tuple-element.215._.refs_0_.refs_1_.refs_2_, bf16[512,256]{1,0:T(8,128)(2,1)} %get-tuple-element.253.bh, bf16[512,256]{1,0:T(8,128)(2,1)} %get-tuple-element.252.bl, f32[64,128,256]{2,1,0:T(8,128)} %get-tuple-element.215._.refs_0_.refs_1_.refs_2_, ...), custom_call_target="tpu_custom_call" | custom-call | flops 1610612736 | bytes 6291456 | tf_op jit(solution)/shard_map/stencil_inner/pallas_call | solution.py:394
  470.6 9.4 %backward_z.3 = (f32[64,128,256]{2,1,0:T(8,128)}, f32[64,128,256]{2,1,0:T(8,128)}, f32[3,64,256]{2,1,0:T(8,128)}, f32[3,64,256]{2,1,0:T(8,128)}, f32[3,128,256]{2,1,0:T(8,128)}, /*index=5*/f32[3,128,256]{2,1,0:T(8,128)}) custom-call(s32[2]{0:T(128)} %pad_add_fusion.where_ref.refs_0_, ...), custom_call_target="tpu_custom_call", output_to_operand_aliasing={{0}: (4, {}), {1}: (5, {}), {2}: (6, {}), {3}: (7, {})} | custom-call | flops 1610612736 | bytes 23068672 | tf_op jit(solution)/shard_map/backward_z/pallas_call | solution.py:284
  484.8 16.5 %stencil_inner.3._ = f32[64,128,256]{2,1,0:T(8,128)} custom-call(f32[64,128,256]{2,1,0:T(8,128)} %stencil_inner.2.refs_5_._, bf16[512,256]{1,0:T(8,128)(2,1)} %get-tuple-element.253.bh, bf16[512,256]{1,0:T(8,128)(2,1)} %get-tuple-element.252.bl, ...), custom_call_target="tpu_custom_call", output_to_operand_aliasing={{}: (0, {})} | custom-call | flops 3221225472 | bytes 12582912 | tf_op jit(solution)/shard_map/stencil_inner/pallas_call | solution.py:394
  508.6 11.2 %stencil_outer.1.r_ref = f32[64,128,256]{2,1,0:T(8,128)} custom-call(f32[64,128,256]{2,1,0:T(8,128)} %stencil_inner.3._, bf16[512,256]{1,0:T(8,128)(2,1)} %get-tuple-element.253.bh, bf16[512,256]{1,0:T(8,128)(2,1)} %get-tuple-element.252.bl, s32[2]{0:T(128)} %pad_add_fusion.where_ref.refs_0_, ...), custom_call_target="tpu_custom_call", output_to_operand_aliasing={{}: (0, {})} | custom-call | flops 1610612736 | bytes 6291456 | tf_op jit(solution)/shard_map/stencil_outer/pallas_call | solution.py:394
  521.1 8.5 %stencil_sides.1 = f32[64,128,256]{2,1,0:T(8,128)} custom-call(s32[2]{0:T(128)} %pad_add_fusion.where_ref.refs_0_, bf16[512,256]{1,0:T(8,128)(2,1)} %get-tuple-element.253.bh, bf16[512,256]{1,0:T(8,128)(2,1)} %get-tuple-element.252.bl, f32[3,64,256]{2,1,0:T(8,128)} %copy-done.27, f32[3,64,256]{2,1,0:T(8,128)} %copy-done.28, ...), custom_call_target="tpu_custom_call", output_to_operand_aliasing={{}: (7, {})} | custom-call | flops 805306368 | bytes 2097152 | tf_op jit(solution)/shard_map/stencil_sides/pallas_call | solution.py:453
  (418 shorter events, 280.3 us)
Async XLA Ops:
  17.8 36.3 %collective-permute-start.2 = (f32[64,8,128]{2,1,0:T(8,128)}, f32[64,8,128]{2,1,0:T(8,128)S(1)}, u32[]{:S(2)}, u32[]{:S(2)}) collective-permute-start(f32[64,8,128]{2,1,0:T(8,128)} %get-tuple-element.122), channel_id=1, source_target_pairs={{0,12},{4,8},{8,4},{12,0},{16,28},{20,24},{24,20},{28,16},{1,13},{... | collective-permute-start | bytes 786440 | tf_op jit(solution)/shard_map/ppermute | solution.py:476
  17.8 39.0 %collective-permute-start.3 = (f32[64,8,128]{2,1,0:T(8,128)}, f32[64,8,128]{2,1,0:T(8,128)S(1)}, u32[]{:S(2)}, u32[]{:S(2)}) collective-permute-start(f32[64,8,128]{2,1,0:T(8,128)} %get-tuple-element.123), channel_id=1, source_target_pairs={{0,16},{4,20},{8,24},{12,28},{16,0},{20,4},{24,8},{28,12},{1,17},{... | collective-permute-start | bytes 786440 | tf_op jit(solution)/shard_map/ppermute | solution.py:476
  20.8 36.8 %collective-permute-start.4 = (f32[64,8,128]{2,1,0:T(8,128)}, f32[64,8,128]{2,1,0:T(8,128)S(1)}, u32[]{:S(2)}, u32[]{:S(2)}) collective-permute-start(f32[64,8,128]{2,1,0:T(8,128)} %get-tuple-element.124), channel_id=1, source_target_pairs={{0,20},{4,16},{8,28},{12,24},{16,4},{20,0},{24,12},{28,8},{1,21},{... | collective-permute-start | bytes 786440 | tf_op jit(solution)/shard_map/ppermute | solution.py:476
  22.8 34.8 %collective-permute-start.5 = (f32[64,8,128]{2,1,0:T(8,128)}, f32[64,8,128]{2,1,0:T(8,128)}, u32[]{:S(2)}, u32[]{:S(2)}) collective-permute-start(f32[64,8,128]{2,1,0:T(8,128)} %get-tuple-element.125), channel_id=1, source_target_pairs={{0,24},{4,28},{8,16},{12,20},{16,8},{20,12},{24,0},{28,4},{1,25},{... | collective-permute-start | bytes 786440 | tf_op jit(solution)/shard_map/ppermute | solution.py:476
  81.2 32.8 %collective-permute-start.13 = (f32[64,8,128]{2,1,0:T(8,128)}, f32[64,8,128]{2,1,0:T(8,128)S(1)}, u32[]{:S(2)}, u32[]{:S(2)}) collective-permute-start(f32[64,8,128]{2,1,0:T(8,128)} %get-tuple-element.136), channel_id=1, source_target_pairs={{0,16},{4,20},{8,24},{12,28},{16,0},{20,4},{24,8},{28,12},{1,17},{... | collective-permute-start | bytes 786440 | tf_op jit(solution)/shard_map/ppermute | solution.py:476
  85.4 34.8 %collective-permute-start.14 = (f32[64,8,128]{2,1,0:T(8,128)}, f32[64,8,128]{2,1,0:T(8,128)S(1)}, u32[]{:S(2)}, u32[]{:S(2)}) collective-permute-start(f32[64,8,128]{2,1,0:T(8,128)} %get-tuple-element.137), channel_id=1, source_target_pairs={{0,20},{4,16},{8,28},{12,24},{16,4},{20,0},{24,12},{28,8},{1,21},{... | collective-permute-start | bytes 786440 | tf_op jit(solution)/shard_map/ppermute | solution.py:476
  95.3 35.8 %collective-permute-start.30 = (f32[64,8,128]{2,1,0:T(8,128)}, f32[64,8,128]{2,1,0:T(8,128)S(1)}, u32[]{:S(2)}, u32[]{:S(2)}) collective-permute-start(f32[64,8,128]{2,1,0:T(8,128)} %get-tuple-element.157), channel_id=1, source_target_pairs={{0,4},{4,0},{8,12},{12,8},{16,20},{20,16},{24,28},{28,24},{1,5},{5... | collective-permute-start | bytes 786440 | tf_op jit(solution)/shard_map/ppermute | solution.py:476
  138.9 43.1 %collective-permute-start.27 = (f32[8,128,128]{2,1,0:T(8,128)}, f32[8,128,128]{2,1,0:T(8,128)S(1)}, u32[]{:S(2)}, u32[]{:S(2)}) collective-permute-start(f32[8,128,128]{2,1,0:T(8,128)} %get-tuple-element.152), channel_id=1, source_target_pairs={{0,1},{1,0},{2,3},{3,2},{4,5},{5,4},{6,7},{7,6},{8,9},{9,8},{10,11... | collective-permute-start | bytes 1572872 | tf_op jit(solution)/shard_map/ppermute | solution.py:476
  143.3 40.2 %collective-permute-start.28 = (f32[8,128,128]{2,1,0:T(8,128)}, f32[8,128,128]{2,1,0:T(8,128)S(1)}, u32[]{:S(2)}, u32[]{:S(2)}) collective-permute-start(f32[8,128,128]{2,1,0:T(8,128)} %get-tuple-element.153), channel_id=1, source_target_pairs={{0,2},{1,3},{2,0},{3,1},{4,6},{5,7},{6,4},{7,5},{8,10},{9,11},{10,... | collective-permute-start | bytes 1572872 | tf_op jit(solution)/shard_map/ppermute | solution.py:476
  144.8 38.6 %collective-permute-start.29 = (f32[8,128,128]{2,1,0:T(8,128)}, f32[8,128,128]{2,1,0:T(8,128)S(1)}, u32[]{:S(2)}, u32[]{:S(2)}) collective-permute-start(f32[8,128,128]{2,1,0:T(8,128)} %get-tuple-element.154), channel_id=1, source_target_pairs={{0,3},{1,2},{2,1},{3,0},{4,7},{5,6},{6,5},{7,4},{8,11},{9,10},{10,... | collective-permute-start | bytes 1572872 | tf_op jit(solution)/shard_map/ppermute | solution.py:476
  193.6 33.0 %collective-permute-start.38 = (f32[8,128,128]{2,1,0:T(8,128)}, f32[8,128,128]{2,1,0:T(8,128)S(1)}, u32[]{:S(2)}, u32[]{:S(2)}) collective-permute-start(f32[8,128,128]{2,1,0:T(8,128)} %get-tuple-element.166), channel_id=1, source_target_pairs={{0,2},{1,3},{2,0},{3,1},{4,6},{5,7},{6,4},{7,5},{8,10},{9,11},{10,... | collective-permute-start | bytes 1572872 | tf_op jit(solution)/shard_map/ppermute | solution.py:476
  217.6 33.4 %collective-permute-start.47 = (f32[8,128,128]{2,1,0:T(8,128)}, f32[8,128,128]{2,1,0:T(8,128)S(1)}, u32[]{:S(2)}, u32[]{:S(2)}) collective-permute-start(f32[8,128,128]{2,1,0:T(8,128)} %get-tuple-element.176), channel_id=1, source_target_pairs={{0,1},{1,0},{2,3},{3,2},{4,5},{5,4},{6,7},{7,6},{8,9},{9,8},{10,11... | collective-permute-start | bytes 1572872 | tf_op jit(solution)/shard_map/ppermute | solution.py:476
  262.7 33.1 %collective-permute-start.57 = (f32[8,128,128]{2,1,0:T(8,128)}, f32[8,128,128]{2,1,0:T(8,128)S(1)}, u32[]{:S(2)}, u32[]{:S(2)}) collective-permute-start(f32[8,128,128]{2,1,0:T(8,128)} %get-tuple-element.188), channel_id=1, source_target_pairs={{0,1},{1,0},{2,3},{3,2},{4,5},{5,4},{6,7},{7,6},{8,9},{9,8},{10,11... | collective-permute-start | bytes 1572872 | tf_op jit(solution)/shard_map/ppermute | solution.py:476
  313.3 32.9 %collective-permute-start.43 = (f32[64,8,128]{2,1,0:T(8,128)}, f32[64,8,128]{2,1,0:T(8,128)S(1)}, u32[]{:S(2)}, u32[]{:S(2)}) collective-permute-start(f32[64,8,128]{2,1,0:T(8,128)} %get-tuple-element.172), channel_id=1, source_target_pairs={{0,16},{4,20},{8,24},{12,28},{16,0},{20,4},{24,8},{28,12},{1,17},{... | collective-permute-start | bytes 786440 | tf_op jit(solution)/shard_map/ppermute | solution.py:476
  317.1 35.3 %collective-permute-start.44 = (f32[64,8,128]{2,1,0:T(8,128)}, f32[64,8,128]{2,1,0:T(8,128)S(1)}, u32[]{:S(2)}, u32[]{:S(2)}) collective-permute-start(f32[64,8,128]{2,1,0:T(8,128)} %get-tuple-element.173), channel_id=1, source_target_pairs={{0,20},{4,16},{8,28},{12,24},{16,4},{20,0},{24,12},{28,8},{1,21},{... | collective-permute-start | bytes 786440 | tf_op jit(solution)/shard_map/ppermute | solution.py:476
  317.6 34.7 %collective-permute-start.45 = (f32[64,8,128]{2,1,0:T(8,128)}, f32[64,8,128]{2,1,0:T(8,128)S(1)}, u32[]{:S(2)}, u32[]{:S(2)}) collective-permute-start(f32[64,8,128]{2,1,0:T(8,128)} %get-tuple-element.174), channel_id=1, source_target_pairs={{0,24},{4,28},{8,16},{12,20},{16,8},{20,12},{24,0},{28,4},{1,25},{... | collective-permute-start | bytes 786440 | tf_op jit(solution)/shard_map/ppermute | solution.py:476
  320.3 33.1 %collective-permute-start.46 = (f32[64,8,128]{2,1,0:T(8,128)}, f32[64,8,128]{2,1,0:T(8,128)S(1)}, u32[]{:S(2)}, u32[]{:S(2)}) collective-permute-start(f32[64,8,128]{2,1,0:T(8,128)} %get-tuple-element.175), channel_id=1, source_target_pairs={{0,28},{4,24},{8,20},{12,16},{16,12},{20,8},{24,4},{28,0},{1,29},{... | collective-permute-start | bytes 786440 | tf_op jit(solution)/shard_map/ppermute | solution.py:476
  329.5 43.2 %collective-permute-start.70 = (f32[8,128,128]{2,1,0:T(8,128)}, f32[8,128,128]{2,1,0:T(8,128)S(1)}, u32[]{:S(2)}, u32[]{:S(2)}) collective-permute-start(f32[8,128,128]{2,1,0:T(8,128)} %get-tuple-element.203), channel_id=1, source_target_pairs={{0,1},{1,0},{2,3},{3,2},{4,5},{5,4},{6,7},{7,6},{8,9},{9,8},{10,11... | collective-permute-start | bytes 1572872 | tf_op jit(solution)/shard_map/ppermute | solution.py:476
  372.6 36.3 %collective-permute-start.64 = (f32[64,8,128]{2,1,0:T(8,128)}, f32[64,8,128]{2,1,0:T(8,128)S(1)}, u32[]{:S(2)}, u32[]{:S(2)}) collective-permute-start(f32[64,8,128]{2,1,0:T(8,128)} %get-tuple-element.196), channel_id=1, source_target_pairs={{0,20},{4,16},{8,28},{12,24},{16,4},{20,0},{24,12},{28,8},{1,21},{... | collective-permute-start | bytes 786440 | tf_op jit(solution)/shard_map/ppermute | solution.py:476
  373.8 35.2 %collective-permute-start.65 = (f32[64,8,128]{2,1,0:T(8,128)}, f32[64,8,128]{2,1,0:T(8,128)S(1)}, u32[]{:S(2)}, u32[]{:S(2)}) collective-permute-start(f32[64,8,128]{2,1,0:T(8,128)} %get-tuple-element.197), channel_id=1, source_target_pairs={{0,24},{4,28},{8,16},{12,20},{16,8},{20,12},{24,0},{28,4},{1,25},{... | collective-permute-start | bytes 786440 | tf_op jit(solution)/shard_map/ppermute | solution.py:476
  376.2 39.1 %collective-permute-start.66 = (f32[64,8,128]{2,1,0:T(8,128)}, f32[64,8,128]{2,1,0:T(8,128)S(1)}, u32[]{:S(2)}, u32[]{:S(2)}) collective-permute-start(f32[64,8,128]{2,1,0:T(8,128)} %get-tuple-element.198), channel_id=1, source_target_pairs={{0,28},{4,24},{8,20},{12,16},{16,12},{20,8},{24,4},{28,0},{1,29},{... | collective-permute-start | bytes 786440 | tf_op jit(solution)/shard_map/ppermute | solution.py:476
  384.9 40.2 %collective-permute-start.73 = (f32[32,8,128]{2,1,0:T(8,128)}, f32[32,8,128]{2,1,0:T(8,128)S(1)}, u32[]{:S(2)}, u32[]{:S(2)}) collective-permute-start(f32[32,8,128]{2,1,0:T(8,128)} %get-tuple-element.207), channel_id=1, source_target_pairs={{0,4},{4,0},{8,12},{12,8},{16,20},{20,16},{24,28},{28,24},{1,5},{5... | collective-permute-start | bytes 393224 | tf_op jit(solution)/shard_map/ppermute | solution.py:476
  436.0 33.7 %collective-permute-start.82 = (f32[32,8,128]{2,1,0:T(8,128)}, f32[32,8,128]{2,1,0:T(8,128)S(1)}, u32[]{:S(2)}, u32[]{:S(2)}) collective-permute-start(f32[32,8,128]{2,1,0:T(8,128)} %get-tuple-element.222), channel_id=1, source_target_pairs={{0,12},{4,8},{8,4},{12,0},{16,28},{20,24},{24,20},{28,16},{1,13},{... | collective-permute-start | bytes 393224 | tf_op jit(solution)/shard_map/ppermute | solution.py:476
  436.6 33.2 %collective-permute-start.83 = (f32[32,8,128]{2,1,0:T(8,128)}, f32[32,8,128]{2,1,0:T(8,128)S(1)}, u32[]{:S(2)}, u32[]{:S(2)}) collective-permute-start(f32[32,8,128]{2,1,0:T(8,128)} %get-tuple-element.223), channel_id=1, source_target_pairs={{0,16},{4,20},{8,24},{12,28},{16,0},{20,4},{24,8},{28,12},{1,17},{... | collective-permute-start | bytes 393224 | tf_op jit(solution)/shard_map/ppermute | solution.py:476
  (168 other events, 3969.5 us)
